TPU v7x, 32 devices: a whole 2x2x4 slice. The times are simulated.
32 devices in a mesh: path: 8 (over z, x), shard: 4 (over y, core).
Axes of the slice: x: 2, y: 2, z: 4, core: 2. Of those that a mesh axis runs over, the one named last changes fastest.
Arguments:
- master: float32 [2, 4096, 2048], P(None, ('path', 'shard')), may hold values from -6 to 6
- momentum: float32 [2, 4096, 2048], P(None, ('path', 'shard')), may hold values from -2 to 2
- routes: int32 [8, 1], replicated, may hold values from 0 to 1
- counts: int32 [8], replicated, may hold values from 1 to 8
- tokens: bfloat16 [12288, 4096], P(('path', 'shard')), may hold values from -6 to 6
- cotangent: bfloat16 [12288, 2048], P(('path', 'shard')), may hold values from -6 to 6
Outputs:
- master_new: float32 [2, 4096, 2048], P(None, ('path', 'shard'))
- momentum_new: float32 [2, 4096, 2048], P(None, ('path', 'shard'))
Inputs may be any that keep to these rules, and one draw needn't show every extreme that they name: `routes`: every module is read by at least one path.
All inputs are finite; a program needn't handle non-finite values.
Results may differ from a plain program's by a relative error of at most 0.0032.
Values may be sent and summed in bfloat16 or wider, within the bound.
No kernel may reach another device: no remote copies, remote signals or barrier semaphores. Data moves between devices by JAX's collectives and lax.ppermute only.
A program may use at most 128 MiB of HBM per device.

v0:
```python
import jax
import jax.numpy as jnp
from jax import lax
from jax.sharding import PartitionSpec as P


def local(master, momentum, routes, counts, tokens, cotangent):
    path_count = routes.shape[0]
    shards = lax.axis_size("shard")
    modules = master.shape[0]
    rows_block = master.shape[1]
    feat_width = master.shape[2]
    tok_rows = tokens.shape[0]
    model_width = tokens.shape[1]
    inv_root = model_width ** (-0.5)
    chosen = routes[:, 0]
    onehot = (chosen[None, :] == jnp.arange(modules, dtype=jnp.int32)[:, None]).astype(jnp.float32)
    outgoing = jnp.take(master.astype(jnp.bfloat16), chosen, axis=0)
    local_rows = lax.all_to_all(outgoing, "path", split_axis=0, concat_axis=0, tiled=True)
    local_weight = local_rows.reshape(path_count * rows_block, feat_width)
    permuted = tokens.reshape(tok_rows, path_count, shards, rows_block)
    permuted = permuted.transpose(0, 2, 1, 3).reshape(tok_rows, model_width)
    columns = lax.all_to_all(permuted, "shard", split_axis=1, concat_axis=0, tiled=True)
    columns_part = permuted
    pre_sum = jnp.dot(
        columns_part,
        lax.all_gather(local_weight, "shard", axis=0, tiled=True),
        preferred_element_type=jnp.float32,
    )
    pre_act = pre_sum * inv_root
    gate_value = jax.nn.sigmoid(pre_act)
    signal = (
        cotangent.astype(jnp.float32) * gate_value * (1.0 + pre_act * (1.0 - gate_value))
    ).astype(jnp.bfloat16)
    columns_part = columns
    product = lax.dot_general(
        columns_part,
        lax.all_gather(signal, "shard", axis=0, tiled=True),
        (((0,), (0,)), ((), ())),
        preferred_element_type=jnp.float32,
    )
    path_grad = (
        (product * inv_root).astype(jnp.bfloat16).reshape(path_count, rows_block, feat_width)
    )
    received = lax.all_to_all(path_grad, "path", split_axis=0, concat_axis=0, tiled=True)
    mixing = onehot * counts.astype(jnp.float32)[None, :]
    mixing = mixing / jnp.sum(mixing, axis=1, keepdims=True)
    flat_recv = received.reshape(path_count, rows_block * feat_width).astype(jnp.float32)
    outer_grad = jnp.dot(mixing, flat_recv, precision=lax.Precision.HIGHEST).reshape(
        modules, rows_block, feat_width
    )
    momentum_new = 0.9 * momentum + outer_grad
    master_new = master - 0.7 * (outer_grad + 0.9 * momentum_new)
    return (master_new, momentum_new)


def solution(mesh):
    placed = (
        P(None, ("path", "shard"), None),
        P(None, ("path", "shard"), None),
        P(),
        P(),
        P(("path", "shard"), None),
        P(("path", "shard"), None),
    )
    return jax.shard_map(
        local,
        mesh=mesh,
        in_specs=placed,
        out_specs=(P(None, ("path", "shard"), None), P(None, ("path", "shard"), None)),
        check_vma=False,
    )
```

profile of v0, /device:TPU:0, one launch (start us, length us, event | category | flops | bytes accessed | tf_op | source)
XLA Modules:
  0.0 444.9 jit_solution(9973681836863088704)
XLA Ops:
  7.2 0.0 all-gather.3.cloned.1.call-start
  7.2 0.7 fusion.16
  7.9 0.7 and_bitcast_fusion
  8.5 1.7 convert_element_type.22
  10.3 2.8 gather_fusion
  13.0 2.7 broadcast_select_fusion
  15.7 100.3 %all_to_all.29 = bf16[8,128,2048]{2,1,0:T(8,128)(2,1)} all-to-all(bf16[8,128,2048]{2,1,0:T(8,128)(2,1)S(1)} %broadcast_select_fusion), channel_id=1, replica_groups=mesh['path'=8,'shard'=4] {'path'}, dimensions={0} | all-to-all | bytes 8388608 | tf_op jit(solution)/shard_map/all_to_all | solution.py:19
  116.0 0.0 copy-start
  116.0 0.0 all-gather.3.cloned.1.call-update
  116.1 0.0 all-gather.5.cloned.1.call-start
  116.1 1.8 copy-done
  117.9 2.8 copy.27
  120.7 2.7 copy.28
  123.5 2.8 copy.26
  126.3 94.9 %all-gather.3.cloned.1.call-done = bf16[4096,2048]{1,0:T(8,128)(2,1)} async-done(((bf16[1024,2048]{1,0:T(8,128)(2,1)}), bf16[4096,2048]{1,0:T(8,128)(2,1)}) %all-gather.3.cloned.1.call-update) | async-done | bytes 16777232 | tf_op jit(solution)/shard_map/all_gather | solution.py:27
  221.2 14.3 %fusion.5 = bf16[384,2048]{0,1:T(8,128)(2,1)} fusion(bf16[384,2048]{0,1:T(8,128)(2,1)} %copy.26, bf16[4096,2048]{1,0:T(8,128)(2,1)} %all-gather.3.cloned.1.call-done, bf16[384,4096]{0,1:T(8,128)(2,1)S(1)} %bitcast.51), kind=kOutput, calls=%fused_computation.11 | convolution fusion | flops 6451101696 | bytes 23068672 | tf_op jit(solution)/shard_map/dot_general | solution.py:25
  235.5 0.0 all-gather.5.cloned.1.call-update
  235.5 69.7 %all_to_all.30 = bf16[384,4,1024]{0,2,1:T(8,128)(2,1)} all-to-all(bf16[384,4,1024]{0,2,1:T(8,128)(2,1)S(1)} %bitcast.52), channel_id=1, replica_groups=mesh['path'=8,'shard'=4] {'shard'}, dimensions={1} | all-to-all | bytes 6291456 | tf_op jit(solution)/shard_map/all_to_all | solution.py:23
  305.1 3.2 copy.30
  308.4 2.6 all-gather.5.cloned.1.call-done
  311.0 11.1 %multiply_convert_fusion = bf16[2048,1024]{0,1:T(8,128)(2,1)} fusion(bf16[1536,2048]{0,1:T(8,128)(2,1)} %all-gather.5.cloned.1.call-done, bf16[1536,1024]{1,0:T(8,128)(2,1)S(1)} %bitcast.56), kind=kOutput, calls=%fused_computation.1 | convolution fusion | flops 6446645248 | bytes 13631488 | tf_op jit(solution)/shard_map/dot_general | solution.py:36
  322.1 0.0 copy-start.2
  322.1 0.0 copy-start.3
  322.1 0.0 copy-start.1
  322.1 5.6 %all-to-all-start.2 = ((bf16[8,128,2048]{2,1,0:T(8,128)(2,1)}), bf16[8,128,2048]{2,1,0:T(8,128)(2,1)}, u32[]{:S(2)}, u32[]{:S(2)}) async-start(bf16[8,128,2048]{2,1,0:T(8,128)(2,1)} %bitcast.55), calls=%async_computation.2 | async-start | bytes 8388608 | tf_op jit(solution)/shard_map/all_to_all | solution.py:45
  327.8 0.0 copy-done.2
  327.8 0.0 copy-done.3
  327.8 0.1 fusion.10
  327.9 93.6 %all-to-all-done.2 = bf16[8,128,2048]{2,1,0:T(8,128)(2,1)} async-done(((bf16[8,128,2048]{2,1,0:T(8,128)(2,1)}), bf16[8,128,2048]{2,1,0:T(8,128)(2,1)}, u32[]{:S(2)}, u32[]{:S(2)}) %all-to-all-start.2) | async-done | bytes 4194336 | tf_op jit(solution)/shard_map/all_to_all | solution.py:45
  421.5 0.0 copy-done.1
  421.5 11.5 %fusion.6 = (f32[2,128,2048]{2,0,1:T(2,128)S(1)}, f32[2,128,2048]{2,0,1:T(2,128)S(1)}) fusion(f32[2,128,2048]{2,1,0:T(8,128)} %param.7, f32[2,128,2048]{2,1,0:T(8,128)S(1)} %copy-done.1, f32[2]{0:T(128)S(1)} %fusion.10, f32[8]{0:T(128)S(1)} %convert_element_type.20, s32[8]{0:T(128)S(1)} %bitcast.58, bf16[1,8,128,2048]{3,2,1,0:T(8,128)(2,1)} %bitcast.19), kind=kOutput, calls=%fused_computation.14 | convolution fusion | flops 53477424 | bytes 12582984 | tf_op jit(solution)/shard_map/dot_general | solution.py:49
  433.0 2.5 copy.33
  435.5 2.5 copy.34
  (2 shorter events, 0.0 us)
Async XLA Ops:
  7.2 214.0 %all-gather.3.cloned.1.call-start = ((), (), s32[]{:S(2)}) async-start(), calls=%async_computation.3 | async-start | bytes 20971520 | tf_op jit(solution)/shard_map/all_gather | solution.py:27
  116.0 1.9 copy-start
  116.1 194.9 %all-gather.5.cloned.1.call-start = ((), (), s32[]{:S(2)}) async-start(), calls=%async_computation.4 | async-start | bytes 7864320 | tf_op jit(solution)/shard_map/all_gather | solution.py:38
  322.1 5.7 %copy-start.2 = (s32[8]{0:T(128)S(1)}, s32[8]{0:T(128)}, u32[]{:S(2)}) copy-start(s32[8]{0:T(128)} %param.9) | copy-start | bytes 100
  322.1 5.7 %copy-start.3 = (s32[8,1]{0,1:T(1,128)S(1)}, s32[8,1]{0,1:T(1,128)}, u32[]{:S(2)}) copy-start(s32[8,1]{0,1:T(1,128)} %param.8) | copy-start | bytes 100
  322.1 99.3 %copy-start.1 = (f32[2,128,2048]{2,1,0:T(8,128)S(1)}, f32[2,128,2048]{2,1,0:T(8,128)}, u32[]{:S(2)}) copy-start(f32[2,128,2048]{2,1,0:T(8,128)} %param.6) | copy-start | bytes 6291460
  322.1 99.3 %all-to-all-start.2 = ((bf16[8,128,2048]{2,1,0:T(8,128)(2,1)}), bf16[8,128,2048]{2,1,0:T(8,128)(2,1)}, u32[]{:S(2)}, u32[]{:S(2)}) async-start(bf16[8,128,2048]{2,1,0:T(8,128)(2,1)} %bitcast.55), calls=%async_computation.2 | async-start | bytes 8388608 | tf_op jit(solution)/shard_map/all_to_all | solution.py:45
Sparse Core Ops, SparseCore 0:
  116.2 104.9 all-gather.2
  235.6 75.3 all-gather.4
where the time goes:
time: 445 us
  waiting for transfers between devices  191 us (43%)
  blocking collectives  170 us (38%)
  matrix products  36.9 us (8%)
  local copies, waits for them, and re-layouts  21.2 us (5%)
  between operations  14.1 us (3%)
  other arithmetic  5.83 us (1%)
  starting transfers between devices  5.72 us (1%)
    all_to_all x1, blocking collectives, local(): lax.all_to_all(outgoing, 'path', split_axis=0, concat_axis=0, tiled=True)  100 us
    all_gather x1, waiting for transfers between devices, local(): lax.all_gather(local_weight, 'shard', axis=0, tiled=True)  94.9 us
    all_to_all x1, waiting for transfers between devices, local(): lax.all_to_all(path_grad, 'path', split_axis=0, concat_axis=0, tiled=True)  93.6 us
    all_to_all x1, blocking collectives, local(): lax.all_to_all(permuted, 'shard', split_axis=1, concat_axis=0, tiled=True)  69.7 us
    dot_general x1, matrix products, local(): jnp.dot(columns_part, lax.all_gather(local_weight, 'shard', axis=0, tiled...  14.3 us
    unnamed x12, local copies, waits for them, and re-layouts  12.5 us
    dot_general x1, matrix products, local(): jnp.dot(mixing, flat_recv, precision=lax.Precision.HIGHEST)  11.5 us
    dot_general x1, matrix products, local(): lax.dot_general(columns_part, lax.all_gather(signal, 'shard', axis=0, til...  11.1 us
  transfers between devices with their start and end apart: 3, of which 3 were waited for; matrix products, arithmetic and copies ran while one was open for 3% of the time, Pallas kernels for 0%

commit v1 on v0

--- a/solution.py
+++ b/solution.py
@@ -1,10 +1,14 @@
 import jax
 import jax.numpy as jnp
 from jax import lax
+from jax.experimental import pallas as pl
+from jax.experimental.pallas import tpu as pltpu
 from jax.sharding import PartitionSpec as P
 
-
-def local(master, momentum, routes, counts, tokens, cotangent):
+CHUNKS = 2
+
+
+def plain(master, momentum, routes, counts, tokens, cotangent):
     path_count = routes.shape[0]
     shards = lax.axis_size("shard")
     modules = master.shape[0]
@@ -21,9 +25,8 @@
     permuted = tokens.reshape(tok_rows, path_count, shards, rows_block)
     permuted = permuted.transpose(0, 2, 1, 3).reshape(tok_rows, model_width)
     columns = lax.all_to_all(permuted, "shard", split_axis=1, concat_axis=0, tiled=True)
-    columns_part = permuted
     pre_sum = jnp.dot(
-        columns_part,
+        permuted,
         lax.all_gather(local_weight, "shard", axis=0, tiled=True),
         preferred_element_type=jnp.float32,
     )
@@ -32,9 +35,8 @@
     signal = (
         cotangent.astype(jnp.float32) * gate_value * (1.0 + pre_act * (1.0 - gate_value))
     ).astype(jnp.bfloat16)
-    columns_part = columns
     product = lax.dot_general(
-        columns_part,
+        columns,
         lax.all_gather(signal, "shard", axis=0, tiled=True),
         (((0,), (0,)), ((), ())),
         preferred_element_type=jnp.float32,
@@ -48,6 +50,133 @@
     flat_recv = received.reshape(path_count, rows_block * feat_width).astype(jnp.float32)
     outer_grad = jnp.dot(mixing, flat_recv, precision=lax.Precision.HIGHEST).reshape(
         modules, rows_block, feat_width
+    )
+    momentum_new = 0.9 * momentum + outer_grad
+    master_new = master - 0.7 * (outer_grad + 0.9 * momentum_new)
+    return (master_new, momentum_new)
+
+
+def column_blocks(tokens, order, width):
+    rows = tokens.shape[0]
+    sets, blocks = order.shape
+
+    def body(order_ref, src, dst):
+        dst[...] = src[...]
+
+    return pl.pallas_call(
+        body,
+        out_shape=jax.ShapeDtypeStruct((sets, rows, blocks * width), tokens.dtype),
+        grid_spec=pltpu.PrefetchScalarGridSpec(
+            num_scalar_prefetch=1,
+            grid=(sets, blocks),
+            in_specs=[pl.BlockSpec((rows, width), lambda a, q, o: (0, o[a, q]))],
+            out_specs=pl.BlockSpec((None, rows, width), lambda a, q, o: (a, 0, q)),
+        ),
+    )(order, tokens)
+
+
+def ringed(master, momentum, routes, counts, tokens, cotangent):
+    bf16, f32 = jnp.bfloat16, jnp.float32
+    paths = routes.shape[0]
+    modules, rows, feats = master.shape
+    tok_rows, model_width = tokens.shape
+    inv_root = model_width ** (-0.5)
+    ring = paths // 2
+    half = feats // 2
+    width = half // CHUNKS
+    pair = 2 * rows
+    p = lax.axis_index("path")
+    s = lax.axis_index("shard")
+    z, x = p // 2, p % 2
+    y, c = s // 2, s % 2
+    first = c == 0
+
+    def over(axis, pairs):
+        return lambda a: lax.ppermute(a, axis, pairs)
+
+    swap_core = over("shard", [(i, i ^ 1) for i in range(4)])
+    swap_y = over("shard", [(i, i ^ 2) for i in range(4)])
+    swap_x = over("path", [(i, i ^ 1) for i in range(paths)])
+    ahead = over("path", [(i, (i + 2) % paths) for i in range(paths)])
+    back = over("path", [(i, (i - 2) % paths) for i in range(paths)])
+
+    def mine_and_other(a):
+        low, high = a[..., :half], a[..., half:]
+        return jnp.where(first, low, high), jnp.where(first, high, low)
+
+    chosen = routes[:, 0]
+    m_own = lax.dynamic_index_in_dim(chosen, p, 0, keepdims=False)
+    m_near = lax.dynamic_index_in_dim(chosen, p ^ 1, 0, keepdims=False)
+    weight = counts.astype(f32)
+    mixing = (chosen[None, :] == jnp.arange(modules, dtype=jnp.int32)[:, None]).astype(f32) * weight[None, :]
+    mixing = mixing / jnp.sum(mixing, axis=1, keepdims=True)
+    mix_own = lax.dynamic_slice_in_dim(mixing, p, 1, 1).reshape(modules, 1, 1)
+    mix_near = lax.dynamic_slice_in_dim(mixing, p ^ 1, 1, 1).reshape(modules, 1, 1)
+
+    keep, give = mine_and_other(master)
+    keep, give = keep.astype(bf16), give.astype(bf16)
+    got = swap_core(give)
+    block = jnp.concatenate(
+        [jnp.where(first, keep, got), jnp.where(first, got, keep)], axis=1
+    )
+
+    steps = jnp.arange(ring, dtype=jnp.int32)
+    owner = ((z - steps) % ring)[:, None] * 2 + (x ^ jnp.arange(2, dtype=jnp.int32))[None, :]
+    owner = owner.reshape(-1)
+    order = jnp.stack([owner * 2 + (1 - y), owner * 2 + y]).astype(jnp.int32)
+    cut = column_blocks(tokens, order, pair)
+    tok_far = swap_y(cut[0])
+    tok_near = swap_core(cut[1])
+    tok_far_near = swap_core(tok_far)
+    tok = jnp.concatenate([cut[1], tok_near, tok_far, tok_far_near], axis=0)
+
+    cot_keep, cot_give = mine_and_other(cotangent)
+    cot = jnp.concatenate([cot_keep, swap_core(cot_give)], axis=0)
+
+    def gather(j):
+        cur = block[:, :, j * width : (j + 1) * width]
+        parts = []
+        for k in range(ring):
+            if k:
+                cur = ahead(cur)
+            parts.append(lax.dynamic_index_in_dim(cur, m_own, 0, keepdims=False))
+            parts.append(swap_x(lax.dynamic_index_in_dim(cur, m_near, 0, keepdims=False)))
+        return jnp.concatenate(parts, axis=0)
+
+    near_rows = 2 * tok_rows
+
+    def signals(j, w):
+        far = jnp.dot(tok[near_rows:], w, preferred_element_type=f32).astype(bf16)
+        far = swap_y(far)
+        pre = jnp.dot(tok[:near_rows], w, preferred_element_type=f32)
+        pre = (pre + far.astype(f32)) * inv_root
+        gate = jax.nn.sigmoid(pre)
+        sig = cot[:, j * width : (j + 1) * width].astype(f32) * gate * (1.0 + pre * (1.0 - gate))
+        sig = sig.astype(bf16)
+        return jnp.concatenate([sig, swap_y(sig)], axis=0)
+
+    def scatter(j, sig):
+        grad = lax.dot_general(tok, sig, (((0,), (0,)), ((), ())), preferred_element_type=f32)
+        grad = (grad * inv_root).astype(bf16).reshape(ring, 2, pair, width)
+        total = None
+        for k in reversed(range(ring)):
+            near = swap_x(grad[k, 1])
+            part = mix_own * grad[k, 0].astype(f32) + mix_near * near.astype(f32)
+            if total is not None:
+                part = part + total.astype(f32)
+            if k:
+                total = back(part.astype(bf16))
+        low, high = part[:, :rows], part[:, rows:]
+        return jnp.where(first, low, high), swap_core(jnp.where(first, high, low))
+
+    kept, came = [], []
+    for j in range(CHUNKS):
+        a, b = scatter(j, signals(j, gather(j)))
+        kept.append(a)
+        came.append(b)
+    kept, came = jnp.concatenate(kept, axis=2), jnp.concatenate(came, axis=2)
+    outer_grad = jnp.concatenate(
+        [jnp.where(first, kept, came), jnp.where(first, came, kept)], axis=2
     )
     momentum_new = 0.9 * momentum + outer_grad
     master_new = master - 0.7 * (outer_grad + 0.9 * momentum_new)
@@ -63,6 +192,11 @@
         P(("path", "shard"), None),
         P(("path", "shard"), None),
     )
+
+    def local(master, *rest):
+        few = mesh.shape["path"] == 8 and mesh.shape["shard"] == 4 and master.shape[0] <= 2
+        return (ringed if few else plain)(master, *rest)
+
     return jax.shard_map(
         local,
         mesh=mesh,

time: 445 us -> 261 us (0.59)
  blocking collectives: 170 us -> 0 us
  starting transfers between devices: 5.72 us -> 34.6 us
  matrix products: 36.9 us -> 16.8 us
  waiting for transfers between devices: 191 us -> 173 us
  local copies, waits for them, and re-layouts: 21.2 us -> 8.25 us
  Pallas kernels: 0 us -> 10.7 us
  between operations: 14.1 us -> 4.98 us
  other arithmetic: 5.83 us -> 11.9 us
    ppermute x0 -> x39, waiting for transfers between devices: none -> 173 us  [over(): return lambda a: lax.ppermute(a, axis, pairs)]
    all_to_all x2 -> x0, blocking collectives: 170 us -> none  [the longest x1 100 us: local(): lax.all_to_all(outgoing, 'path', split_axis=0, concat_axis=0, tiled=True)]
    all_gather x2 -> x0, waiting for transfers between devices: 97.5 us -> none  [the longest x1 94.9 us: local(): lax.all_gather(local_weight, 'shard', axis=0, tiled=True)]
    all_to_all x1 -> x0, waiting for transfers between devices: 93.6 us -> none  [local(): lax.all_to_all(path_grad, 'path', split_axis=0, concat_axis=0, tiled=True)]
    ppermute x0 -> x39, starting transfers between devices: none -> 34.6 us  [over(): return lambda a: lax.ppermute(a, axis, pairs)]
    dot_general x3 -> x6, matrix products: 36.9 us -> 16.8 us  [the longest x2 9.64 us: scatter(): lax.dot_general(tok, sig, (((0,), (0,)), ((), ())), preferred_element_typ...]
    pallas_call x0 -> x1, Pallas kernels: none -> 10.7 us  [column_blocks(): pl.pallas_call(body, out_shape=jax.ShapeDtypeStruct((sets, rows, blocks *...]
    unnamed x12 -> x25, local copies, waits for them, and re-layouts: 12.5 us -> 3.2 us
  transfers between devices with their start and end apart: 3 -> 39, of which waited for: 3 -> 30; matrix products, arithmetic and copies ran while one was open for 3% -> 11% of each run, Pallas kernels for 0% -> 4%
where the time goes in v1:
time: 261 us; the launch traced here: 260 us
  waiting for transfers between devices  173 us (66%)
  starting transfers between devices  34.6 us (13%)
  matrix products  16.8 us (6%)
  other arithmetic  11.9 us (5%)
  Pallas kernels  10.7 us (4%)
  local copies, waits for them, and re-layouts  8.25 us (3%)
  between operations  4.98 us (2%)
    ppermute x39, waiting for transfers between devices, over(): return lambda a: lax.ppermute(a, axis, pairs)  173 us
    ppermute x39, starting transfers between devices, over(): return lambda a: lax.ppermute(a, axis, pairs)  34.6 us
    pallas_call x1, Pallas kernels, column_blocks(): pl.pallas_call(body, out_shape=jax.ShapeDtypeStruct((sets, rows, blocks *...  10.7 us
    dot_general x2, matrix products, scatter(): lax.dot_general(tok, sig, (((0,), (0,)), ((), ())), preferred_element_typ...  9.64 us
  transfers between devices with their start and end apart: 39, of which 30 were waited for; matrix products, arithmetic and copies ran while one was open for 11% of the time, Pallas kernels for 4%

profile of v1, /device:TPU:0, one launch (start us, length us, event | category | flops | bytes accessed | tf_op | source)
XLA Modules:
  0.0 260.2 jit_solution(5040045234822098664)
XLA Ops:
  0.6 1.6 select_convert_fusion
  3.7 10.7 %shard_map.77 = bf16[2,384,2048]{2,1,0:T(8,128)(2,1)} custom-call(s32[2,8]{1,0:T(2,128)} %pad_add_fusion.order_ref, bf16[384,4096]{1,0:T(8,128)(2,1)} %src.1), custom_call_target="tpu_custom_call" | custom-call | tf_op jit(solution)/shard_map/pallas_call | solution.py:66
  14.3 4.0 %slice_bitcast_fusion = (bf16[384,2048]{1,0:T(8,128)(2,1)}, bf16[384,2048]{1,0:T(8,128)(2,1)}) fusion(bf16[2,384,2048]{2,1,0:T(8,128)(2,1)} %shard_map.77), kind=kLoop, calls=%fused_computation.9 | loop fusion | bytes 6291456 | tf_op jit(solution)/shard_map/squeeze | solution.py:128
  18.3 2.6 collective-permute-start.1
  27.1 1.6 collective-permute-start.6
  28.8 1.6 collective-permute-start.5
  30.9 1.6 collective-permute-start.22
  32.6 5.4 %collective-permute-done.5 = bf16[256,512]{1,0:T(8,128)(2,1)S(1)} collective-permute-done((bf16[256,512]{1,0:T(8,128)(2,1)S(1)}, bf16[256,512]{1,0:T(8,128)(2,1)S(1)}, u32[]{:S(2)}, u32[]{:S(2)}) %collective-permute-start.5) | collective-permute-done | bytes 262176 | tf_op jit(solution)/shard_map/ppermute | solution.py:95
  38.0 4.5 %collective-permute-done.21 = bf16[256,512]{1,0:T(8,128)(2,1)S(1)} collective-permute-done((bf16[256,512]{1,0:T(8,128)(2,1)S(1)}, bf16[256,512]{1,0:T(8,128)(2,1)S(1)}, u32[]{:S(2)}, u32[]{:S(2)}) %collective-permute-start.21) | collective-permute-done | bytes 262176 | tf_op jit(solution)/shard_map/ppermute | solution.py:95
  45.7 9.2 %collective-permute-done.22 = bf16[2,256,512]{2,1,0:T(8,128)(2,1)S(1)} collective-permute-done((bf16[2,256,512]{2,1,0:T(8,128)(2,1)S(1)}, bf16[2,256,512]{2,1,0:T(8,128)(2,1)S(1)}, u32[]{:S(2)}, u32[]{:S(2)}) %collective-permute-start.22) | collective-permute-done | bytes 524320 | tf_op jit(solution)/shard_map/ppermute | solution.py:95
  55.0 1.6 collective-permute-start.23
  56.6 5.3 %collective-permute-done.23 = bf16[256,512]{1,0:T(8,128)(2,1)S(1)} collective-permute-done((bf16[256,512]{1,0:T(8,128)(2,1)S(1)}, bf16[256,512]{1,0:T(8,128)(2,1)S(1)}, u32[]{:S(2)}, u32[]{:S(2)}) %collective-permute-start.23) | collective-permute-done | bytes 262176 | tf_op jit(solution)/shard_map/ppermute | solution.py:95
  62.1 4.1 %collective-permute-done.8 = bf16[2,256,512]{2,1,0:T(8,128)(2,1)S(1)} collective-permute-done((bf16[2,256,512]{2,1,0:T(8,128)(2,1)S(1)}, bf16[2,256,512]{2,1,0:T(8,128)(2,1)S(1)}, u32[]{:S(2)}, u32[]{:S(2)}) %collective-permute-start.8) | collective-permute-done | bytes 524320 | tf_op jit(solution)/shard_map/ppermute | solution.py:95
  66.2 1.6 collective-permute-start.9
  67.8 9.0 %collective-permute-done.24 = bf16[2,256,512]{2,1,0:T(8,128)(2,1)S(1)} collective-permute-done((bf16[2,256,512]{2,1,0:T(8,128)(2,1)S(1)}, bf16[2,256,512]{2,1,0:T(8,128)(2,1)S(1)}, u32[]{:S(2)}, u32[]{:S(2)}) %collective-permute-start.24) | collective-permute-done | bytes 524320 | tf_op jit(solution)/shard_map/ppermute | solution.py:95
  76.8 1.6 collective-permute-start.25
  81.3 3.1 %collective-permute-done.25 = bf16[256,512]{1,0:T(8,128)(2,1)S(1)} collective-permute-done((bf16[256,512]{1,0:T(8,128)(2,1)S(1)}, bf16[256,512]{1,0:T(8,128)(2,1)S(1)}, u32[]{:S(2)}, u32[]{:S(2)}) %collective-permute-start.25) | collective-permute-done | bytes 262176 | tf_op jit(solution)/shard_map/ppermute | solution.py:95
  84.5 10.5 %collective-permute-done.10 = bf16[2,256,512]{2,1,0:T(8,128)(2,1)S(1)} collective-permute-done((bf16[2,256,512]{2,1,0:T(8,128)(2,1)S(1)}, bf16[2,256,512]{2,1,0:T(8,128)(2,1)S(1)}, u32[]{:S(2)}, u32[]{:S(2)}) %collective-permute-start.10) | collective-permute-done | bytes 524320 | tf_op jit(solution)/shard_map/ppermute | solution.py:95
  95.6 8.7 %collective-permute-done.26 = bf16[2,256,512]{2,1,0:T(8,128)(2,1)S(1)} collective-permute-done((bf16[2,256,512]{2,1,0:T(8,128)(2,1)S(1)}, bf16[2,256,512]{2,1,0:T(8,128)(2,1)S(1)}, u32[]{:S(2)}, u32[]{:S(2)}) %collective-permute-start.26) | collective-permute-done | bytes 524320 | tf_op jit(solution)/shard_map/ppermute | solution.py:95
  105.0 5.8 %collective-permute-done.27 = bf16[256,512]{1,0:T(8,128)(2,1)S(1)} collective-permute-done((bf16[256,512]{1,0:T(8,128)(2,1)S(1)}, bf16[256,512]{1,0:T(8,128)(2,1)S(1)}, u32[]{:S(2)}, u32[]{:S(2)}) %collective-permute-start.27) | collective-permute-done | bytes 262176 | tf_op jit(solution)/shard_map/ppermute | solution.py:95
  111.0 1.8 convolution_convert_fusion.1
  113.3 1.8 convolution_convert_fusion
  115.1 1.6 collective-permute-start.28
  116.7 1.8 fusion.1
  118.5 1.8 fusion
  120.3 13.0 %collective-permute-done.12 = bf16[768,512]{1,0:T(8,128)(2,1)S(1)} collective-permute-done((bf16[768,512]{1,0:T(8,128)(2,1)S(1)}, bf16[768,512]{1,0:T(8,128)(2,1)S(1)}, u32[]{:S(2)}, u32[]{:S(2)}) %collective-permute-start.12) | collective-permute-done | bytes 786464 | tf_op jit(solution)/shard_map/ppermute | solution.py:95
  133.3 12.8 %collective-permute-done.28 = bf16[768,512]{1,0:T(8,128)(2,1)S(1)} collective-permute-done((bf16[768,512]{1,0:T(8,128)(2,1)S(1)}, bf16[768,512]{1,0:T(8,128)(2,1)S(1)}, u32[]{:S(2)}, u32[]{:S(2)}) %collective-permute-start.28) | collective-permute-done | bytes 786464 | tf_op jit(solution)/shard_map/ppermute | solution.py:95
  148.5 1.6 collective-permute-start.13
  150.0 18.2 %collective-permute-done.29 = bf16[768,512]{1,0:T(8,128)(2,1)S(1)} collective-permute-done((bf16[768,512]{1,0:T(8,128)(2,1)S(1)}, bf16[768,512]{1,0:T(8,128)(2,1)S(1)}, u32[]{:S(2)}, u32[]{:S(2)}) %collective-permute-start.29) | collective-permute-done | bytes 786464 | tf_op jit(solution)/shard_map/ppermute | solution.py:95
  168.2 4.8 %multiply_convert_fusion = bf16[2048,512]{1,0:T(8,128)(2,1)S(1)} fusion(bf16[768,512]{1,0:T(8,128)(2,1)S(1)} %collective-permute-done.29, bf16[768,512]{1,0:T(8,128)(2,1)S(1)} %get-tuple-element.26, bf16[384,2048]{1,0:T(8,128)(2,1)S(1)} %collective-permute-done.2, bf16[384,2048]{1,0:T(8,128)(2,1)} %collective-permute-done.1, ...), kind=kOutput, calls=%fused_computation.1 | convolution fusion | flops 3251634176 | bytes 9961472 | tf_op jit(solution)/shard_map/dot_general | solution.py:159
  174.0 6.1 %collective-permute-done.13 = bf16[768,512]{1,0:T(8,128)(2,1)S(1)} collective-permute-done((bf16[768,512]{1,0:T(8,128)(2,1)S(1)}, bf16[768,512]{1,0:T(8,128)(2,1)S(1)}, u32[]{:S(2)}, u32[]{:S(2)}) %collective-permute-start.13) | collective-permute-done | bytes 786464 | tf_op jit(solution)/shard_map/ppermute | solution.py:95
  180.2 4.8 %multiply_convert_fusion.1 = bf16[2048,512]{1,0:T(8,128)(2,1)S(1)} fusion(bf16[768,512]{1,0:T(8,128)(2,1)S(1)} %collective-permute-done.13, bf16[768,512]{1,0:T(8,128)(2,1)S(1)} %get-tuple-element.27, bf16[384,2048]{1,0:T(8,128)(2,1)S(1)} %collective-permute-done.2, bf16[384,2048]{1,0:T(8,128)(2,1)} %collective-permute-done.1, ...), kind=kOutput, calls=%fused_computation.2 | convolution fusion | flops 3251634176 | bytes 9961472 | tf_op jit(solution)/shard_map/dot_general | solution.py:159
  187.8 4.3 %collective-permute-done.17 = bf16[256,512]{1,0:T(8,128)(2,1)S(1)} collective-permute-done((bf16[256,512]{1,0:T(8,128)(2,1)S(1)}, bf16[256,512]{1,0:T(8,128)(2,1)S(1)}, u32[]{:S(2)}, u32[]{:S(2)}) %collective-permute-start.17) | collective-permute-done | bytes 262176 | tf_op jit(solution)/shard_map/ppermute | solution.py:95
  192.2 2.7 %collective-permute-done.32 = bf16[256,512]{1,0:T(8,128)(2,1)S(1)} collective-permute-done((bf16[256,512]{1,0:T(8,128)(2,1)S(1)}, bf16[256,512]{1,0:T(8,128)(2,1)S(1)}, u32[]{:S(2)}, u32[]{:S(2)}) %collective-permute-start.32) | collective-permute-done | bytes 262176 | tf_op jit(solution)/shard_map/ppermute | solution.py:95
  197.4 1.9 collective-permute-start.35
  199.3 2.0 collective-permute-start.31
  201.3 4.3 %collective-permute-done.16 = bf16[256,512]{1,0:T(8,128)(2,1)S(1)} collective-permute-done((bf16[256,512]{1,0:T(8,128)(2,1)S(1)}, bf16[256,512]{1,0:T(8,128)(2,1)S(1)}, u32[]{:S(2)}, u32[]{:S(2)}) %collective-permute-start.16) | collective-permute-done | bytes 262176 | tf_op jit(solution)/shard_map/ppermute | solution.py:95
  205.7 2.7 %collective-permute-done.31 = bf16[256,512]{1,0:T(8,128)(2,1)S(1)} collective-permute-done((bf16[256,512]{1,0:T(8,128)(2,1)S(1)}, bf16[256,512]{1,0:T(8,128)(2,1)S(1)}, u32[]{:S(2)}, u32[]{:S(2)}) %collective-permute-start.31) | collective-permute-done | bytes 262176 | tf_op jit(solution)/shard_map/ppermute | solution.py:95
  208.5 2.8 %collective-permute-done.18 = bf16[2,256,512]{2,1,0:T(8,128)(2,1)S(1)} collective-permute-done((bf16[2,256,512]{2,1,0:T(8,128)(2,1)S(1)}, bf16[2,256,512]{2,1,0:T(8,128)(2,1)S(1)}, u32[]{:S(2)}, u32[]{:S(2)}) %collective-permute-start.18) | collective-permute-done | bytes 524320 | tf_op jit(solution)/shard_map/ppermute | solution.py:95
  211.3 8.4 %collective-permute-done.35 = bf16[2,256,512]{2,1,0:T(8,128)(2,1)S(1)} collective-permute-done((bf16[2,256,512]{2,1,0:T(8,128)(2,1)S(1)}, bf16[2,256,512]{2,1,0:T(8,128)(2,1)S(1)}, u32[]{:S(2)}, u32[]{:S(2)}) %collective-permute-start.35) | collective-permute-done | bytes 524320 | tf_op jit(solution)/shard_map/ppermute | solution.py:95
  221.9 1.9 collective-permute-start.30
  223.8 4.3 %collective-permute-done.15 = bf16[256,512]{1,0:T(8,128)(2,1)S(1)} collective-permute-done((bf16[256,512]{1,0:T(8,128)(2,1)S(1)}, bf16[256,512]{1,0:T(8,128)(2,1)S(1)}, u32[]{:S(2)}, u32[]{:S(2)}) %collective-permute-start.15) | collective-permute-done | bytes 262176 | tf_op jit(solution)/shard_map/ppermute | solution.py:95
  228.2 2.7 %collective-permute-done.30 = bf16[256,512]{1,0:T(8,128)(2,1)S(1)} collective-permute-done((bf16[256,512]{1,0:T(8,128)(2,1)S(1)}, bf16[256,512]{1,0:T(8,128)(2,1)S(1)}, u32[]{:S(2)}, u32[]{:S(2)}) %collective-permute-start.30) | collective-permute-done | bytes 262176 | tf_op jit(solution)/shard_map/ppermute | solution.py:95
  231.0 2.8 %collective-permute-done.19 = bf16[2,256,512]{2,1,0:T(8,128)(2,1)S(1)} collective-permute-done((bf16[2,256,512]{2,1,0:T(8,128)(2,1)S(1)}, bf16[2,256,512]{2,1,0:T(8,128)(2,1)S(1)}, u32[]{:S(2)}, u32[]{:S(2)}) %collective-permute-start.19) | collective-permute-done | bytes 524320 | tf_op jit(solution)/shard_map/ppermute | solution.py:95
  233.8 9.3 %collective-permute-done.36 = bf16[2,256,512]{2,1,0:T(8,128)(2,1)S(1)} collective-permute-done((bf16[2,256,512]{2,1,0:T(8,128)(2,1)S(1)}, bf16[2,256,512]{2,1,0:T(8,128)(2,1)S(1)}, u32[]{:S(2)}, u32[]{:S(2)}) %collective-permute-start.36) | collective-permute-done | bytes 524320 | tf_op jit(solution)/shard_map/ppermute | solution.py:95
  244.9 5.5 %collective-permute-done.14 = bf16[256,512]{1,0:T(8,128)(2,1)S(1)} collective-permute-done((bf16[256,512]{1,0:T(8,128)(2,1)S(1)}, bf16[256,512]{1,0:T(8,128)(2,1)S(1)}, u32[]{:S(2)}, u32[]{:S(2)}) %collective-permute-start.14) | collective-permute-done | bytes 262176 | tf_op jit(solution)/shard_map/ppermute | solution.py:95
  250.5 2.4 collective-permute-done.20
  257.6 2.7 %multiply_subtract_fusion = (f32[2,128,2048]{2,1,0:T(8,128)}, f32[2,128,2048]{2,1,0:T(8,128)}) fusion(f32[2,128,2048]{2,1,0:T(8,128)S(1)} %copy-done, f32[2,128,1024]{2,1,0:T(8,128)S(1)} %get-tuple-element.9, f32[2,128,1024]{2,1,0:T(8,128)S(1)} %get-tuple-element.8, f32[2,128,2048]{2,1,0:T(8,128)S(1)} %copy-done.1), kind=kLoop, calls=%fused_computation.5 | loop fusion | flops 3670016 | bytes 10485760 | tf_op jit(solution)/shard_map/sub | solution.py:182
  (112 shorter events, 30.1 us)
Async XLA Ops:
  2.3 24.5 %collective-permute-start.4 = (bf16[2,128,1024]{2,1,0:T(8,128)(2,1)S(1)}, bf16[2,128,1024]{2,1,0:T(8,128)(2,1)S(1)}, u32[]{:S(2)}, u32[]{:S(2)}) collective-permute-start(bf16[2,128,1024]{2,1,0:T(8,128)(2,1)S(1)} %select_convert_fusion), channel_id=1, source_target_pairs={{0,1},{1,0},{2,3},{3,2},{4,5},{5,4},{6,7},{7,6},{8,9},{9,8},{10,11... | collective-permute-start | bytes 1572872 | tf_op jit(solution)/shard_map/ppermute | solution.py:95
  14.3 6.6 %copy-start.3 = (s32[8,1]{0,1:T(1,128)S(1)}, s32[8,1]{0,1:T(1,128)}, u32[]{:S(2)}) copy-start(s32[8,1]{0,1:T(1,128)} %param.8) | copy-start | bytes 100
  18.3 8.5 %copy-start = (f32[2,128,2048]{2,1,0:T(8,128)S(1)}, f32[2,128,2048]{2,1,0:T(8,128)}, u32[]{:S(2)}) copy-start(f32[2,128,2048]{2,1,0:T(8,128)} %param.6) | copy-start | bytes 6291460
  18.3 43.7 %collective-permute-start.1 = (bf16[384,2048]{1,0:T(8,128)(2,1)}, bf16[384,2048]{1,0:T(8,128)(2,1)}, u32[]{:S(2)}, u32[]{:S(2)}) collective-permute-start(bf16[384,2048]{1,0:T(8,128)(2,1)} %get-tuple-element.6), channel_id=1, source_target_pairs={{0,2},{1,3},{2,0},{3,1},{4,6},{5,7},{6,4},{7,5},{8,10},{9,11},{10,... | collective-permute-start | bytes 4718600 | tf_op jit(solution)/shard_map/ppermute | solution.py:95
  27.1 16.6 %collective-permute-start.6 = (bf16[2,256,512]{2,1,0:T(8,128)(2,1)S(1)}, bf16[2,256,512]{2,1,0:T(8,128)(2,1)S(1)}, u32[]{:S(2)}, u32[]{:S(2)}) collective-permute-start(bf16[2,256,512]{2,1,0:T(8,128)(2,1)S(1)} %get-tuple-element.35), channel_id=1, source_target_pairs={{0,8},{4,12},{8,16},{12,20},{16,24},{20,28},{24,0},{28,4},{1,9},{5... | collective-permute-start | bytes 1572872 | tf_op jit(solution)/shard_map/ppermute | solution.py:95
  28.8 9.3 %collective-permute-start.5 = (bf16[256,512]{1,0:T(8,128)(2,1)S(1)}, bf16[256,512]{1,0:T(8,128)(2,1)S(1)}, u32[]{:S(2)}, u32[]{:S(2)}) collective-permute-start(bf16[256,512]{1,0:T(8,128)(2,1)S(1)} %dynamic-slice_bitcast_fusion.6), channel_id=1, source_target_pairs={{0,4},{4,0},{8,12},{12,8},{16,20},{20,16},{24,28},{28,24},{1,5},{5... | collective-permute-start | bytes 786440 | tf_op jit(solution)/shard_map/ppermute | solution.py:95
  30.3 12.2 %collective-permute-start.21 = (bf16[256,512]{1,0:T(8,128)(2,1)S(1)}, bf16[256,512]{1,0:T(8,128)(2,1)S(1)}, u32[]{:S(2)}, u32[]{:S(2)}) collective-permute-start(bf16[256,512]{1,0:T(8,128)(2,1)S(1)} %fusion.16), channel_id=1, source_target_pairs={{0,4},{4,0},{8,12},{12,8},{16,20},{20,16},{24,28},{28,24},{1,5},{5... | collective-permute-start | bytes 786440 | tf_op jit(solution)/shard_map/ppermute | solution.py:95
  30.9 24.0 %collective-permute-start.22 = (bf16[2,256,512]{2,1,0:T(8,128)(2,1)S(1)}, bf16[2,256,512]{2,1,0:T(8,128)(2,1)S(1)}, u32[]{:S(2)}, u32[]{:S(2)}) collective-permute-start(bf16[2,256,512]{2,1,0:T(8,128)(2,1)S(1)} %get-tuple-element.34), channel_id=1, source_target_pairs={{0,8},{4,12},{8,16},{12,20},{16,24},{20,28},{24,0},{28,4},{1,9},{5... | collective-permute-start | bytes 1572872 | tf_op jit(solution)/shard_map/ppermute | solution.py:95
  43.7 12.9 %collective-permute-start.7 = (bf16[256,512]{1,0:T(8,128)(2,1)S(1)}, bf16[256,512]{1,0:T(8,128)(2,1)S(1)}, u32[]{:S(2)}, u32[]{:S(2)}) collective-permute-start(bf16[256,512]{1,0:T(8,128)(2,1)S(1)} %dynamic-slice_bitcast_fusion.5), channel_id=1, source_target_pairs={{0,4},{4,0},{8,12},{12,8},{16,20},{20,16},{24,28},{28,24},{1,5},{5... | collective-permute-start | bytes 786440 | tf_op jit(solution)/shard_map/ppermute | solution.py:95
  45.3 20.9 %collective-permute-start.8 = (bf16[2,256,512]{2,1,0:T(8,128)(2,1)S(1)}, bf16[2,256,512]{2,1,0:T(8,128)(2,1)S(1)}, u32[]{:S(2)}, u32[]{:S(2)}) collective-permute-start(bf16[2,256,512]{2,1,0:T(8,128)(2,1)S(1)} %collective-permute-done.6), channel_id=1, source_target_pairs={{0,8},{4,12},{8,16},{12,20},{16,24},{20,28},{24,0},{28,4},{1,9},{5... | collective-permute-start | bytes 1572872 | tf_op jit(solution)/shard_map/ppermute | solution.py:95
  55.0 7.0 %collective-permute-start.23 = (bf16[256,512]{1,0:T(8,128)(2,1)S(1)}, bf16[256,512]{1,0:T(8,128)(2,1)S(1)}, u32[]{:S(2)}, u32[]{:S(2)}) collective-permute-start(bf16[256,512]{1,0:T(8,128)(2,1)S(1)} %dynamic-slice_bitcast_fusion.2), channel_id=1, source_target_pairs={{0,4},{4,0},{8,12},{12,8},{16,20},{20,16},{24,28},{28,24},{1,5},{5... | collective-permute-start | bytes 786440 | tf_op jit(solution)/shard_map/ppermute | solution.py:95
  56.5 20.2 %collective-permute-start.24 = (bf16[2,256,512]{2,1,0:T(8,128)(2,1)S(1)}, bf16[2,256,512]{2,1,0:T(8,128)(2,1)S(1)}, u32[]{:S(2)}, u32[]{:S(2)}) collective-permute-start(bf16[2,256,512]{2,1,0:T(8,128)(2,1)S(1)} %collective-permute-done.22), channel_id=1, source_target_pairs={{0,8},{4,12},{8,16},{12,20},{16,24},{20,28},{24,0},{28,4},{1,9},{5... | collective-permute-start | bytes 1572872 | tf_op jit(solution)/shard_map/ppermute | solution.py:95
  62.0 48.8 %collective-permute-start.2 = (bf16[384,2048]{1,0:T(8,128)(2,1)}, bf16[384,2048]{1,0:T(8,128)(2,1)S(1)}, u32[]{:S(2)}, u32[]{:S(2)}) collective-permute-start(bf16[384,2048]{1,0:T(8,128)(2,1)} %collective-permute-done.1), channel_id=1, source_target_pairs={{0,1},{1,0},{2,3},{3,2},{4,5},{5,4},{6,7},{7,6},{8,9},{9,8},{10,11... | collective-permute-start | bytes 4718600 | tf_op jit(solution)/shard_map/ppermute | solution.py:95
  66.2 15.0 %collective-permute-start.9 = (bf16[256,512]{1,0:T(8,128)(2,1)S(1)}, bf16[256,512]{1,0:T(8,128)(2,1)S(1)}, u32[]{:S(2)}, u32[]{:S(2)}) collective-permute-start(bf16[256,512]{1,0:T(8,128)(2,1)S(1)} %dynamic-slice_bitcast_fusion.4), channel_id=1, source_target_pairs={{0,4},{4,0},{8,12},{12,8},{16,20},{20,16},{24,28},{28,24},{1,5},{5... | collective-permute-start | bytes 786440 | tf_op jit(solution)/shard_map/ppermute | solution.py:95
  76.7 4.4 %copy-start.2 = (bf16[384,2048]{1,0:T(8,128)(2,1)S(1)}, bf16[384,2048]{1,0:T(8,128)(2,1)}, u32[]{:S(2)}) copy-start(bf16[384,2048]{1,0:T(8,128)(2,1)} %get-tuple-element.7) | copy-start | bytes 4718596
  76.8 7.7 %collective-permute-start.25 = (bf16[256,512]{1,0:T(8,128)(2,1)S(1)}, bf16[256,512]{1,0:T(8,128)(2,1)S(1)}, u32[]{:S(2)}, u32[]{:S(2)}) collective-permute-start(bf16[256,512]{1,0:T(8,128)(2,1)S(1)} %dynamic-slice_bitcast_fusion.1), channel_id=1, source_target_pairs={{0,4},{4,0},{8,12},{12,8},{16,20},{20,16},{24,28},{28,24},{1,5},{5... | collective-permute-start | bytes 786440 | tf_op jit(solution)/shard_map/ppermute | solution.py:95
  78.3 16.7 %collective-permute-start.10 = (bf16[2,256,512]{2,1,0:T(8,128)(2,1)S(1)}, bf16[2,256,512]{2,1,0:T(8,128)(2,1)S(1)}, u32[]{:S(2)}, u32[]{:S(2)}) collective-permute-start(bf16[2,256,512]{2,1,0:T(8,128)(2,1)S(1)} %collective-permute-done.8), channel_id=1, source_target_pairs={{0,8},{4,12},{8,16},{12,20},{16,24},{20,28},{24,0},{28,4},{1,9},{5... | collective-permute-start | bytes 1572872 | tf_op jit(solution)/shard_map/ppermute | solution.py:95
  78.3 26.0 %collective-permute-start.26 = (bf16[2,256,512]{2,1,0:T(8,128)(2,1)S(1)}, bf16[2,256,512]{2,1,0:T(8,128)(2,1)S(1)}, u32[]{:S(2)}, u32[]{:S(2)}) collective-permute-start(bf16[2,256,512]{2,1,0:T(8,128)(2,1)S(1)} %collective-permute-done.24), channel_id=1, source_target_pairs={{0,8},{4,12},{8,16},{12,20},{16,24},{20,28},{24,0},{28,4},{1,9},{5... | collective-permute-start | bytes 1572872 | tf_op jit(solution)/shard_map/ppermute | solution.py:95
  81.2 35.5 %collective-permute-start = (bf16[384,2048]{1,0:T(8,128)(2,1)S(1)}, bf16[384,2048]{1,0:T(8,128)(2,1)S(1)}, u32[]{:S(2)}, u32[]{:S(2)}) collective-permute-start(bf16[384,2048]{1,0:T(8,128)(2,1)S(1)} %copy-done.2), channel_id=1, source_target_pairs={{0,1},{1,0},{2,3},{3,2},{4,5},{5,4},{6,7},{7,6},{8,9},{9,8},{10,11... | collective-permute-start | bytes 4718600 | tf_op jit(solution)/shard_map/ppermute | solution.py:95
  84.4 35.9 %collective-permute-start.3 = (bf16[384,1024]{1,0:T(8,128)(2,1)S(1)}, bf16[384,1024]{1,0:T(8,128)(2,1)S(1)}, u32[]{:S(2)}, u32[]{:S(2)}) collective-permute-start(bf16[384,1024]{1,0:T(8,128)(2,1)S(1)} %get-tuple-element.28), channel_id=1, source_target_pairs={{0,1},{1,0},{2,3},{3,2},{4,5},{5,4},{6,7},{7,6},{8,9},{9,8},{10,11... | collective-permute-start | bytes 2359304 | tf_op jit(solution)/shard_map/ppermute | solution.py:95
  95.0 10.0 %collective-permute-start.11 = (bf16[256,512]{1,0:T(8,128)(2,1)S(1)}, bf16[256,512]{1,0:T(8,128)(2,1)S(1)}, u32[]{:S(2)}, u32[]{:S(2)}) collective-permute-start(bf16[256,512]{1,0:T(8,128)(2,1)S(1)} %dynamic-slice_bitcast_fusion.3), channel_id=1, source_target_pairs={{0,4},{4,0},{8,12},{12,8},{16,20},{20,16},{24,28},{28,24},{1,5},{5... | collective-permute-start | bytes 786440 | tf_op jit(solution)/shard_map/ppermute | solution.py:95
  104.3 6.5 %collective-permute-start.27 = (bf16[256,512]{1,0:T(8,128)(2,1)S(1)}, bf16[256,512]{1,0:T(8,128)(2,1)S(1)}, u32[]{:S(2)}, u32[]{:S(2)}) collective-permute-start(bf16[256,512]{1,0:T(8,128)(2,1)S(1)} %dynamic-slice_bitcast_fusion), channel_id=1, source_target_pairs={{0,4},{4,0},{8,12},{12,8},{16,20},{20,16},{24,28},{28,24},{1,5},{5... | collective-permute-start | bytes 786440 | tf_op jit(solution)/shard_map/ppermute | solution.py:95
  112.8 20.5 %collective-permute-start.12 = (bf16[768,512]{1,0:T(8,128)(2,1)S(1)}, bf16[768,512]{1,0:T(8,128)(2,1)S(1)}, u32[]{:S(2)}, u32[]{:S(2)}) collective-permute-start(bf16[768,512]{1,0:T(8,128)(2,1)S(1)} %convolution_convert_fusion.1), channel_id=1, source_target_pairs={{0,2},{1,3},{2,0},{3,1},{4,6},{5,7},{6,4},{7,5},{8,10},{9,11},{10,... | collective-permute-start | bytes 2359304 | tf_op jit(solution)/shard_map/ppermute | solution.py:95
  115.1 31.0 %collective-permute-start.28 = (bf16[768,512]{1,0:T(8,128)(2,1)S(1)}, bf16[768,512]{1,0:T(8,128)(2,1)S(1)}, u32[]{:S(2)}, u32[]{:S(2)}) collective-permute-start(bf16[768,512]{1,0:T(8,128)(2,1)S(1)} %convolution_convert_fusion), channel_id=1, source_target_pairs={{0,2},{1,3},{2,0},{3,1},{4,6},{5,7},{6,4},{7,5},{8,10},{9,11},{10,... | collective-permute-start | bytes 2359304 | tf_op jit(solution)/shard_map/ppermute | solution.py:95
  146.1 2.1 copy-start.4
  147.7 20.5 %collective-permute-start.29 = (bf16[768,512]{1,0:T(8,128)(2,1)S(1)}, bf16[768,512]{1,0:T(8,128)(2,1)S(1)}, u32[]{:S(2)}, u32[]{:S(2)}) collective-permute-start(bf16[768,512]{1,0:T(8,128)(2,1)S(1)} %get-tuple-element.26), channel_id=1, source_target_pairs={{0,2},{1,3},{2,0},{3,1},{4,6},{5,7},{6,4},{7,5},{8,10},{9,11},{10,... | collective-permute-start | bytes 2359304 | tf_op jit(solution)/shard_map/ppermute | solution.py:95
  148.5 31.7 %collective-permute-start.13 = (bf16[768,512]{1,0:T(8,128)(2,1)S(1)}, bf16[768,512]{1,0:T(8,128)(2,1)S(1)}, u32[]{:S(2)}, u32[]{:S(2)}) collective-permute-start(bf16[768,512]{1,0:T(8,128)(2,1)S(1)} %get-tuple-element.27), channel_id=1, source_target_pairs={{0,2},{1,3},{2,0},{3,1},{4,6},{5,7},{6,4},{7,5},{8,10},{9,11},{10,... | collective-permute-start | bytes 2359304 | tf_op jit(solution)/shard_map/ppermute | solution.py:95
  173.4 11.6 %collective-permute-start.33 = (bf16[256,512]{1,0:T(8,128)(2,1)S(1)}, bf16[256,512]{1,0:T(8,128)(2,1)S(1)}, u32[]{:S(2)}, u32[]{:S(2)}) collective-permute-start(bf16[256,512]{1,0:T(8,128)(2,1)S(1)} %get-tuple-element.11), channel_id=1, source_target_pairs={{0,4},{4,0},{8,12},{12,8},{16,20},{20,16},{24,28},{28,24},{1,5},{5... | collective-permute-start | bytes 786440 | tf_op jit(solution)/shard_map/ppermute | solution.py:95
  185.3 11.3 %collective-permute-start.34 = (bf16[2,256,512]{2,1,0:T(8,128)(2,1)S(1)}, bf16[2,256,512]{2,1,0:T(8,128)(2,1)S(1)}, u32[]{:S(2)}, u32[]{:S(2)}) collective-permute-start(bf16[2,256,512]{2,1,0:T(8,128)(2,1)S(1)} %add_convert_fusion.2), channel_id=1, source_target_pairs={{0,24},{4,28},{8,0},{12,4},{16,8},{20,12},{24,16},{28,20},{1,25},{... | collective-permute-start | bytes 1572872 | tf_op jit(solution)/shard_map/ppermute | solution.py:95
  185.7 6.4 %collective-permute-start.17 = (bf16[256,512]{1,0:T(8,128)(2,1)S(1)}, bf16[256,512]{1,0:T(8,128)(2,1)S(1)}, u32[]{:S(2)}, u32[]{:S(2)}) collective-permute-start(bf16[256,512]{1,0:T(8,128)(2,1)S(1)} %get-tuple-element.19), channel_id=1, source_target_pairs={{0,4},{4,0},{8,12},{12,8},{16,20},{20,16},{24,28},{28,24},{1,5},{5... | collective-permute-start | bytes 786440 | tf_op jit(solution)/shard_map/ppermute | solution.py:95
  186.6 8.3 %collective-permute-start.32 = (bf16[256,512]{1,0:T(8,128)(2,1)S(1)}, bf16[256,512]{1,0:T(8,128)(2,1)S(1)}, u32[]{:S(2)}, u32[]{:S(2)}) collective-permute-start(bf16[256,512]{1,0:T(8,128)(2,1)S(1)} %get-tuple-element.13), channel_id=1, source_target_pairs={{0,4},{4,0},{8,12},{12,8},{16,20},{20,16},{24,28},{28,24},{1,5},{5... | collective-permute-start | bytes 786440 | tf_op jit(solution)/shard_map/ppermute | solution.py:95
  196.9 14.4 %collective-permute-start.18 = (bf16[2,256,512]{2,1,0:T(8,128)(2,1)S(1)}, bf16[2,256,512]{2,1,0:T(8,128)(2,1)S(1)}, u32[]{:S(2)}, u32[]{:S(2)}) collective-permute-start(bf16[2,256,512]{2,1,0:T(8,128)(2,1)S(1)} %get-tuple-element.43), channel_id=1, source_target_pairs={{0,24},{4,28},{8,0},{12,4},{16,8},{20,12},{24,16},{28,20},{1,25},{... | collective-permute-start | bytes 1572872 | tf_op jit(solution)/shard_map/ppermute | solution.py:95
  197.4 22.4 %collective-permute-start.35 = (bf16[2,256,512]{2,1,0:T(8,128)(2,1)S(1)}, bf16[2,256,512]{2,1,0:T(8,128)(2,1)S(1)}, u32[]{:S(2)}, u32[]{:S(2)}) collective-permute-start(bf16[2,256,512]{2,1,0:T(8,128)(2,1)S(1)} %get-tuple-element.42), channel_id=1, source_target_pairs={{0,24},{4,28},{8,0},{12,4},{16,8},{20,12},{24,16},{28,20},{1,25},{... | collective-permute-start | bytes 1572872 | tf_op jit(solution)/shard_map/ppermute | solution.py:95
  199.3 6.4 %collective-permute-start.16 = (bf16[256,512]{1,0:T(8,128)(2,1)S(1)}, bf16[256,512]{1,0:T(8,128)(2,1)S(1)}, u32[]{:S(2)}, u32[]{:S(2)}) collective-permute-start(bf16[256,512]{1,0:T(8,128)(2,1)S(1)} %get-tuple-element.21), channel_id=1, source_target_pairs={{0,4},{4,0},{8,12},{12,8},{16,20},{20,16},{24,28},{28,24},{1,5},{5... | collective-permute-start | bytes 786440 | tf_op jit(solution)/shard_map/ppermute | solution.py:95
  199.3 9.2 %collective-permute-start.31 = (bf16[256,512]{1,0:T(8,128)(2,1)S(1)}, bf16[256,512]{1,0:T(8,128)(2,1)S(1)}, u32[]{:S(2)}, u32[]{:S(2)}) collective-permute-start(bf16[256,512]{1,0:T(8,128)(2,1)S(1)} %get-tuple-element.15), channel_id=1, source_target_pairs={{0,4},{4,0},{8,12},{12,8},{16,20},{20,16},{24,28},{28,24},{1,5},{5... | collective-permute-start | bytes 786440 | tf_op jit(solution)/shard_map/ppermute | solution.py:95
  220.3 13.5 %collective-permute-start.19 = (bf16[2,256,512]{2,1,0:T(8,128)(2,1)S(1)}, bf16[2,256,512]{2,1,0:T(8,128)(2,1)S(1)}, u32[]{:S(2)}, u32[]{:S(2)}) collective-permute-start(bf16[2,256,512]{2,1,0:T(8,128)(2,1)S(1)} %get-tuple-element.41), channel_id=1, source_target_pairs={{0,24},{4,28},{8,0},{12,4},{16,8},{20,12},{24,16},{28,20},{1,25},{... | collective-permute-start | bytes 1572872 | tf_op jit(solution)/shard_map/ppermute | solution.py:95
  220.7 22.4 %collective-permute-start.36 = (bf16[2,256,512]{2,1,0:T(8,128)(2,1)S(1)}, bf16[2,256,512]{2,1,0:T(8,128)(2,1)S(1)}, u32[]{:S(2)}, u32[]{:S(2)}) collective-permute-start(bf16[2,256,512]{2,1,0:T(8,128)(2,1)S(1)} %get-tuple-element.40), channel_id=1, source_target_pairs={{0,24},{4,28},{8,0},{12,4},{16,8},{20,12},{24,16},{28,20},{1,25},{... | collective-permute-start | bytes 1572872 | tf_op jit(solution)/shard_map/ppermute | solution.py:95
  221.7 6.4 %collective-permute-start.15 = (bf16[256,512]{1,0:T(8,128)(2,1)S(1)}, bf16[256,512]{1,0:T(8,128)(2,1)S(1)}, u32[]{:S(2)}, u32[]{:S(2)}) collective-permute-start(bf16[256,512]{1,0:T(8,128)(2,1)S(1)} %get-tuple-element.23), channel_id=1, source_target_pairs={{0,4},{4,0},{8,12},{12,8},{16,20},{20,16},{24,28},{28,24},{1,5},{5... | collective-permute-start | bytes 786440 | tf_op jit(solution)/shard_map/ppermute | solution.py:95
  221.9 9.1 %collective-permute-start.30 = (bf16[256,512]{1,0:T(8,128)(2,1)S(1)}, bf16[256,512]{1,0:T(8,128)(2,1)S(1)}, u32[]{:S(2)}, u32[]{:S(2)}) collective-permute-start(bf16[256,512]{1,0:T(8,128)(2,1)S(1)} %get-tuple-element.17), channel_id=1, source_target_pairs={{0,4},{4,0},{8,12},{12,8},{16,20},{20,16},{24,28},{28,24},{1,5},{5... | collective-permute-start | bytes 786440 | tf_op jit(solution)/shard_map/ppermute | solution.py:95
  243.6 9.2 %collective-permute-start.20 = (bf16[2,256,512]{2,1,0:T(8,128)(2,1)S(1)}, bf16[2,256,512]{2,1,0:T(8,128)(2,1)S(1)}, u32[]{:S(2)}, u32[]{:S(2)}) collective-permute-start(bf16[2,256,512]{2,1,0:T(8,128)(2,1)S(1)} %get-tuple-element.39), channel_id=1, source_target_pairs={{0,24},{4,28},{8,0},{12,4},{16,8},{20,12},{24,16},{28,20},{1,25},{... | collective-permute-start | bytes 1572872 | tf_op jit(solution)/shard_map/ppermute | solution.py:95
  244.0 6.4 %collective-permute-start.14 = (bf16[256,512]{1,0:T(8,128)(2,1)S(1)}, bf16[256,512]{1,0:T(8,128)(2,1)S(1)}, u32[]{:S(2)}, u32[]{:S(2)}) collective-permute-start(bf16[256,512]{1,0:T(8,128)(2,1)S(1)} %get-tuple-element.25), channel_id=1, source_target_pairs={{0,4},{4,0},{8,12},{12,8},{16,20},{20,16},{24,28},{28,24},{1,5},{5... | collective-permute-start | bytes 786440 | tf_op jit(solution)/shard_map/ppermute | solution.py:95
  253.2 2.0 collective-permute-start.37
  253.4 2.5 collective-permute-start.38
  256.0 1.6 copy-start.1

commit v2 on v0

--- a/solution.py
+++ b/solution.py
@@ -1,10 +1,26 @@
 import jax
 import jax.numpy as jnp
 from jax import lax
+from jax.experimental import pallas as pl
+from jax.experimental.pallas import tpu as pltpu
 from jax.sharding import PartitionSpec as P
 
-
-def local(master, momentum, routes, counts, tokens, cotangent):
+CHUNKS = 4
+GATHER_GROUPS = ((0, 1, 2), (3,))
+SCATTER_GROUPS = ((3,), (0, 1, 2))
+ORDER = (
+    "wp", "ws", "cut", "bl", "yt", "z0.1", "ct", "cp", "cc", "tn", "co", "z1.1", "z0.2", "z1.2", "z2.1",
+    "x0.0", "z0.3", "z1.3", "x1.0", "z2.2", "z3.1", "cf", "x0.1", "tf", "tk", "w0", "p0", "yp0", "x1.1",
+    "x2.0", "z2.3", "w1", "p1", "yp1", "z3.2", "s0", "ys0", "x2.1", "s1", "ys1", "z3.3", "w2", "p2", "yp2",
+    "x3.0", "gn0", "go0", "gx0.0", "x3.1", "gx0.1", "gn1", "gx1.0", "gx1.1", "go1", "a0.3", "r0.3", "w3",
+    "p3", "yp3", "s2", "ys2", "a0.2", "r0.2", "a1.3", "r1.3", "s3", "ys3", "a0.1", "r0.1", "go2", "gn2",
+    "gx2.0", "a1.2", "r1.2", "gx2.1", "a2.3", "r2.3", "a0.0", "fs0", "gn3", "gx3.0", "go3", "gx3.1", "a1.1",
+    "r1.1", "a3.3", "r3.3", "a2.2", "r2.2", "a1.0", "fs1", "a3.2", "r3.2", "a2.1", "r2.1", "a3.1", "r3.1",
+    "a2.0", "fs2", "a3.0", "fs3", "fin",
+)
+
+
+def plain(master, momentum, routes, counts, tokens, cotangent):
     path_count = routes.shape[0]
     shards = lax.axis_size("shard")
     modules = master.shape[0]
@@ -21,9 +37,8 @@
     permuted = tokens.reshape(tok_rows, path_count, shards, rows_block)
     permuted = permuted.transpose(0, 2, 1, 3).reshape(tok_rows, model_width)
     columns = lax.all_to_all(permuted, "shard", split_axis=1, concat_axis=0, tiled=True)
-    columns_part = permuted
     pre_sum = jnp.dot(
-        columns_part,
+        permuted,
         lax.all_gather(local_weight, "shard", axis=0, tiled=True),
         preferred_element_type=jnp.float32,
     )
@@ -32,9 +47,8 @@
     signal = (
         cotangent.astype(jnp.float32) * gate_value * (1.0 + pre_act * (1.0 - gate_value))
     ).astype(jnp.bfloat16)
-    columns_part = columns
     product = lax.dot_general(
-        columns_part,
+        columns,
         lax.all_gather(signal, "shard", axis=0, tiled=True),
         (((0,), (0,)), ((), ())),
         preferred_element_type=jnp.float32,
@@ -48,6 +62,227 @@
     flat_recv = received.reshape(path_count, rows_block * feat_width).astype(jnp.float32)
     outer_grad = jnp.dot(mixing, flat_recv, precision=lax.Precision.HIGHEST).reshape(
         modules, rows_block, feat_width
+    )
+    momentum_new = 0.9 * momentum + outer_grad
+    master_new = master - 0.7 * (outer_grad + 0.9 * momentum_new)
+    return (master_new, momentum_new)
+
+
+def column_blocks(tokens, places, width):
+    rows, columns = tokens.shape
+    blocks = places.shape[0] // 2
+    tile = rows // 4
+
+    def body(places_ref, src, one, two):
+        for q in range(blocks):
+            for at, dst in ((q, one), (blocks + q, two)):
+                start = pl.multiple_of(places_ref[at] * width, width)
+                dst[:, q * width : (q + 1) * width] = src[:, pl.ds(start, width)]
+
+    shape = jax.ShapeDtypeStruct((rows, blocks * width), tokens.dtype)
+    return pl.pallas_call(
+        body,
+        out_shape=(shape, shape),
+        grid_spec=pltpu.PrefetchScalarGridSpec(
+            num_scalar_prefetch=1,
+            grid=(4,),
+            in_specs=[pl.BlockSpec((tile, columns), lambda i, o: (i, 0))],
+            out_specs=[pl.BlockSpec((tile, blocks * width), lambda i, o: (i, 0))] * 2,
+        ),
+    )(places, tokens)
+
+
+def ringed(master, momentum, routes, counts, tokens, cotangent):
+    bf16, f32 = jnp.bfloat16, jnp.float32
+    paths = routes.shape[0]
+    modules, rows, feats = master.shape
+    tok_rows, model_width = tokens.shape
+    inv_root = model_width ** (-0.5)
+    ring = paths // 2
+    half = feats // 2
+    width = half // CHUNKS
+    pair = 2 * rows
+    own_rows = ring * pair
+    p = lax.axis_index("path")
+    s = lax.axis_index("shard")
+    z, x = p // 2, p % 2
+    y, c = s // 2, s % 2
+    first = c == 0
+
+    def over(axis, pairs):
+        return lambda a: lax.ppermute(a, axis, pairs)
+
+    swap_core = over("shard", [(i, i ^ 1) for i in range(4)])
+    swap_y = over("shard", [(i, i ^ 2) for i in range(4)])
+    swap_x = over("path", [(i, i ^ 1) for i in range(paths)])
+    ahead = over("path", [(i, (i + 2) % paths) for i in range(paths)])
+    back = over("path", [(i, (i - 2) % paths) for i in range(paths)])
+
+    def mine_and_other(a):
+        low, high = a[..., :half], a[..., half:]
+        return jnp.where(first, low, high), jnp.where(first, high, low)
+
+    chosen = routes[:, 0]
+    m_own = lax.dynamic_index_in_dim(chosen, p, 0, keepdims=False)
+    m_near = lax.dynamic_index_in_dim(chosen, p ^ 1, 0, keepdims=False)
+    weight = counts.astype(f32)
+    mixing = (chosen[None, :] == jnp.arange(modules, dtype=jnp.int32)[:, None]).astype(f32) * weight[None, :]
+    mixing = mixing / jnp.sum(mixing, axis=1, keepdims=True)
+    mix_own = lax.dynamic_slice_in_dim(mixing, p, 1, 1).reshape(modules, 1, 1)
+    mix_near = lax.dynamic_slice_in_dim(mixing, p ^ 1, 1, 1).reshape(modules, 1, 1)
+
+    steps = jnp.arange(ring, dtype=jnp.int32)
+    owner = jnp.concatenate([((z - steps) % ring) * 2 + x, ((z - steps) % ring) * 2 + (1 - x)])
+    places = jnp.concatenate([owner * 2 + (1 - y), owner * 2 + y]).astype(jnp.int32)
+
+    val = {}
+    last = [None]
+
+    def after(*values):
+        if last[0] is None:
+            return values
+        return lax.optimization_barrier((*values, last[0]))[:-1]
+
+    def compute(name, fn, *values):
+        out = fn(*after(*values))
+        val[name] = out
+        last[0] = out[0] if isinstance(out, tuple) else out
+
+    def send(name, via, value):
+        (value,) = after(value)
+        val[name] = via(value)
+        last[0] = value
+
+    def stack(*parts):
+        return jnp.concatenate(parts, axis=0)
+
+    def start_weights(a):
+        keep, give = mine_and_other(a)
+        return keep.astype(bf16), give.astype(bf16)
+
+    def full_block(keep, got):
+        return jnp.concatenate([jnp.where(first, keep, got), jnp.where(first, got, keep)], axis=1)
+
+    def block_at(j, k):
+        return val["bl"][:, :, j * width : (j + 1) * width] if k == 0 else val[f"z{j}.{k}"]
+
+    def pick(m):
+        def fn(*blocks):
+            return stack(*[lax.dynamic_index_in_dim(b, m, 0, keepdims=False) for b in blocks])
+
+        return fn
+
+    def gathered(j):
+        near = [val[f"x{j}.{g}"] for g in range(len(GATHER_GROUPS))]
+        return stack(*[pick(m_own)(block_at(j, k)) for k in range(ring)], *near)
+
+    def far_sums(w):
+        return jnp.dot(val["tf"], w, preferred_element_type=f32).astype(bf16)
+
+    def signal(j):
+        def fn(far):
+            pre = jnp.dot(val["tn"], val[f"w{j}"], preferred_element_type=f32)
+            pre = (pre + far.astype(f32)) * inv_root
+            gate = jax.nn.sigmoid(pre)
+            cot = val["co"][:, j * width : (j + 1) * width].astype(f32)
+            return (cot * gate * (1.0 + pre * (1.0 - gate))).astype(bf16)
+
+        return fn
+
+    def grad(j, lo):
+        def fn(far):
+            sig = stack(val[f"s{j}"], far)
+            out = lax.dot_general(
+                val["tk"][:, lo : lo + own_rows], sig, (((0,), (0,)), ((), ())), preferred_element_type=f32
+            )
+            return (out * inv_root).astype(bf16)
+
+        return fn
+
+    def piece(j, k):
+        for g, group in enumerate(SCATTER_GROUPS):
+            if k in group:
+                at = group.index(k) * pair
+                return val[f"gx{j}.{g}"][at : at + pair]
+
+    def summed(j, k):
+        def fn(near, *total):
+            part = mix_own * val[f"go{j}"][k * pair : (k + 1) * pair].astype(f32) + mix_near * near.astype(f32)
+            if total:
+                part = part + total[0].astype(f32)
+            if k:
+                return part.astype(bf16)
+            low, high = part[:, :rows], part[:, rows:]
+            return jnp.where(first, high, low), jnp.where(first, low, high)
+
+        return fn
+
+    def task(name):
+        kind = name.rstrip("0123456789.")
+        number = name[len(kind) :].split(".")
+        j = int(number[0]) if number[0] else 0
+        k = int(number[1]) if len(number) > 1 else 0
+        if kind == "wp":
+            compute(name, start_weights, master)
+        elif kind == "ws":
+            send(name, swap_core, val["wp"][1])
+        elif kind == "bl":
+            compute(name, full_block, val["wp"][0], val["ws"])
+        elif kind == "cut":
+            compute(name, lambda t: column_blocks(t, places, pair), tokens)
+        elif kind == "yt":
+            send(name, swap_y, val["cut"][0])
+        elif kind == "ct":
+            send(name, swap_core, val["cut"][1])
+        elif kind == "cf":
+            send(name, swap_core, val["yt"])
+        elif kind == "tn":
+            compute(name, stack, val["cut"][1], val["ct"])
+        elif kind == "tf":
+            compute(name, stack, val["yt"], val["cf"])
+        elif kind == "tk":
+            compute(name, stack, val["tn"], val["tf"])
+        elif kind == "cp":
+            compute(name, mine_and_other, cotangent)
+        elif kind == "cc":
+            send(name, swap_core, val["cp"][1])
+        elif kind == "co":
+            compute(name, stack, val["cp"][0], val["cc"])
+        elif kind == "z":
+            send(name, ahead, block_at(j, k - 1))
+        elif kind == "x":
+            compute(name, pick(m_near), *[block_at(j, i) for i in GATHER_GROUPS[k]])
+            send(name, swap_x, val[name])
+        elif kind == "w":
+            val[name] = gathered(j)
+        elif kind == "p":
+            compute(name, far_sums, val[f"w{j}"])
+        elif kind == "yp":
+            send(name, swap_y, val[f"p{j}"])
+        elif kind == "s":
+            compute(name, signal(j), val[f"yp{j}"])
+        elif kind == "ys":
+            send(name, swap_y, val[f"s{j}"])
+        elif kind == "gn":
+            compute(name, grad(j, own_rows), val[f"ys{j}"])
+        elif kind == "go":
+            compute(name, grad(j, 0), val[f"ys{j}"])
+        elif kind == "gx":
+            group = SCATTER_GROUPS[k]
+            send(name, swap_x, val[f"gn{j}"][group[0] * pair : (group[-1] + 1) * pair])
+        elif kind == "a":
+            compute(name, summed(j, k), piece(j, k), *([val[f"r{j}.{k + 1}"]] if k < ring - 1 else []))
+        elif kind == "r":
+            send(name, back, val[f"a{j}.{k}"])
+        elif kind == "fs":
+            send(name, swap_core, val[f"a{j}.0"][0])
+
+    for name in ORDER:
+        task(name)
+    kept = jnp.concatenate([val[f"a{j}.0"][1] for j in range(CHUNKS)], axis=2)
+    came = jnp.concatenate([val[f"fs{j}"] for j in range(CHUNKS)], axis=2)
+    outer_grad = jnp.concatenate(
+        [jnp.where(first, kept, came), jnp.where(first, came, kept)], axis=2
     )
     momentum_new = 0.9 * momentum + outer_grad
     master_new = master - 0.7 * (outer_grad + 0.9 * momentum_new)
@@ -63,6 +298,11 @@
         P(("path", "shard"), None),
         P(("path", "shard"), None),
     )
+
+    def local(master, *rest):
+        few = mesh.shape["path"] == 8 and mesh.shape["shard"] == 4 and master.shape[0] <= 2
+        return (ringed if few else plain)(master, *rest)
+
     return jax.shard_map(
         local,
         mesh=mesh,

time: 445 us -> 206 us (0.46)
  blocking collectives: 170 us -> 0 us
  waiting for transfers between devices: 191 us -> 83.6 us
  starting transfers between devices: 5.72 us -> 76.4 us
  matrix products: 36.9 us -> 17.3 us
  local copies, waits for them, and re-layouts: 21.2 us -> 4.81 us
  between operations: 14.1 us -> 5.7 us
  other arithmetic: 5.83 us -> 12.6 us
  Pallas kernels: 0 us -> 5.09 us
    all_to_all x2 -> x0, blocking collectives: 170 us -> none  [the longest x1 100 us: local(): lax.all_to_all(outgoing, 'path', split_axis=0, concat_axis=0, tiled=True)]
    all_gather x2 -> x0, waiting for transfers between devices: 97.5 us -> none  [the longest x1 94.9 us: local(): lax.all_gather(local_weight, 'shard', axis=0, tiled=True)]
    all_to_all x1 -> x0, waiting for transfers between devices: 93.6 us -> none  [local(): lax.all_to_all(path_grad, 'path', split_axis=0, concat_axis=0, tiled=True)]
    ppermute x0 -> x57, waiting for transfers between devices: none -> 83.6 us  [over(): return lambda a: lax.ppermute(a, axis, pairs)]
    ppermute x0 -> x57, starting transfers between devices: none -> 76.4 us  [over(): return lambda a: lax.ppermute(a, axis, pairs)]
    dot_general x3 -> x16, matrix products: 36.9 us -> 17.3 us  [the longest x8 8.41 us: fn(): lax.dot_general(val['tk'][:, lo:lo + own_rows], sig, (((0,), (0,)), ((),...]
    unnamed x12 -> x43, local copies, waits for them, and re-layouts: 12.5 us -> 1.34 us
    all_to_all x1 -> x0, starting transfers between devices: 5.64 us -> none  [local(): lax.all_to_all(path_grad, 'path', split_axis=0, concat_axis=0, tiled=True)]
  transfers between devices with their start and end apart: 3 -> 57, of which waited for: 3 -> 24; matrix products, arithmetic and copies ran while one was open for 3% -> 12% of each run, Pallas kernels for 0% -> 2%
where the time goes in v2:
time: 206 us; the launch traced here: 205 us
  waiting for transfers between devices  83.6 us (41%)
  starting transfers between devices  76.4 us (37%)
  matrix products  17.3 us (8%)
  other arithmetic  12.6 us (6%)
  between operations  5.7 us (3%)
  Pallas kernels  5.09 us (2%)
  local copies, waits for them, and re-layouts  4.81 us (2%)
    ppermute x57, waiting for transfers between devices, over(): return lambda a: lax.ppermute(a, axis, pairs)  83.6 us
    ppermute x57, starting transfers between devices, over(): return lambda a: lax.ppermute(a, axis, pairs)  76.4 us
    dot_general x8, matrix products, fn(): lax.dot_general(val['tk'][:, lo:lo + own_rows], sig, (((0,), (0,)), ((),...  8.41 us
    pallas_call x1, Pallas kernels, column_blocks(): pl.pallas_call(body, out_shape=(shape, shape), grid_spec=pltpu.PrefetchSc...  5.09 us
    dot_general x4, matrix products, fn(): pre = jnp.dot(val['tn'], val[f'w{j}'], preferred_element_type=f32)  4.89 us
  transfers between devices with their start and end apart: 57, of which 24 were waited for; matrix products, arithmetic and copies ran while one was open for 12% of the time, Pallas kernels for 2%

profile of v2, /device:TPU:0, one launch (start us, length us, event | category | flops | bytes accessed | tf_op | source)
XLA Modules:
  0.0 205.5 jit_solution(12496303033473198658)
XLA Ops:
  0.6 1.7 select_convert_fusion
  3.5 5.1 %shard_map.77 = (bf16[384,2048]{1,0:T(8,128)(2,1)}, bf16[384,2048]{1,0:T(8,128)(2,1)}) custom-call(s32[16]{0:T(128)} %pad_add_fusion.places_ref, bf16[384,4096]{1,0:T(8,128)(2,1)} %src), custom_call_target="tpu_custom_call" | custom-call | tf_op jit(solution)/shard_map/pallas_call | solution.py:83
  10.8 3.0 %collective-permute-start.2 = (bf16[384,2048]{1,0:T(8,128)(2,1)}, bf16[384,2048]{1,0:T(8,128)(2,1)S(1)}, u32[]{:S(2)}, u32[]{:S(2)}) collective-permute-start(bf16[384,2048]{1,0:T(8,128)(2,1)} %get-tuple-element.111), channel_id=1, source_target_pairs={{0,2},{1,3},{2,0},{3,1},{4,6},{5,7},{6,4},{7,5},{8,10},{9,11},{10,... | collective-permute-start | bytes 4718600 | tf_op jit(solution)/shard_map/ppermute | solution.py:113
  20.2 1.6 collective-permute-start.5
  22.0 1.6 constant_dynamic-update-slice_fusion
  23.7 1.6 collective-permute-start.4
  25.4 5.8 %collective-permute-done.5 = bf16[2,256,256]{2,1,0:T(8,128)(2,1)S(1)} collective-permute-done((bf16[2,256,256]{2,1,0:T(8,128)(2,1)S(1)}, bf16[2,256,256]{2,1,0:T(8,128)(2,1)S(1)}, u32[]{:S(2)}, u32[]{:S(2)}) %collective-permute-start.5) | collective-permute-done | bytes 262176 | tf_op jit(solution)/shard_map/ppermute | solution.py:113
  31.2 5.5 %collective-permute-done.4 = bf16[2,256,256]{2,1,0:T(8,128)(2,1)S(1)} collective-permute-done((bf16[2,256,256]{2,1,0:T(8,128)(2,1)S(1)}, bf16[2,256,256]{2,1,0:T(8,128)(2,1)S(1)}, u32[]{:S(2)}, u32[]{:S(2)}) %collective-permute-start.4) | collective-permute-done | bytes 262176 | tf_op jit(solution)/shard_map/ppermute | solution.py:113
  38.1 4.3 %collective-permute-done.8 = bf16[2,256,256]{2,1,0:T(8,128)(2,1)S(1)} collective-permute-done((bf16[2,256,256]{2,1,0:T(8,128)(2,1)S(1)}, bf16[2,256,256]{2,1,0:T(8,128)(2,1)S(1)}, u32[]{:S(2)}, u32[]{:S(2)}) %collective-permute-start.8) | collective-permute-done | bytes 262176 | tf_op jit(solution)/shard_map/ppermute | solution.py:113
  42.5 5.5 %collective-permute-done.7 = bf16[2,256,256]{2,1,0:T(8,128)(2,1)S(1)} collective-permute-done((bf16[2,256,256]{2,1,0:T(8,128)(2,1)S(1)}, bf16[2,256,256]{2,1,0:T(8,128)(2,1)S(1)}, u32[]{:S(2)}, u32[]{:S(2)}) %collective-permute-start.7) | collective-permute-done | bytes 262176 | tf_op jit(solution)/shard_map/ppermute | solution.py:113
  48.1 5.2 %collective-permute-done.6 = bf16[2,256,256]{2,1,0:T(8,128)(2,1)S(1)} collective-permute-done((bf16[2,256,256]{2,1,0:T(8,128)(2,1)S(1)}, bf16[2,256,256]{2,1,0:T(8,128)(2,1)S(1)}, u32[]{:S(2)}, u32[]{:S(2)}) %collective-permute-start.6) | collective-permute-done | bytes 262176 | tf_op jit(solution)/shard_map/ppermute | solution.py:113
  53.4 1.6 collective-permute-start.11
  56.3 1.6 collective-permute-start.18
  57.9 6.4 %collective-permute-done.10 = bf16[2,256,256]{2,1,0:T(8,128)(2,1)S(1)} collective-permute-done((bf16[2,256,256]{2,1,0:T(8,128)(2,1)S(1)}, bf16[2,256,256]{2,1,0:T(8,128)(2,1)S(1)}, u32[]{:S(2)}, u32[]{:S(2)}) %collective-permute-start.10) | collective-permute-done | bytes 262176 | tf_op jit(solution)/shard_map/ppermute | solution.py:113
  64.3 1.6 collective-permute-start.12
  66.7 2.6 %collective-permute-done.12 = bf16[256,256]{1,0:T(8,128)(2,1)S(1)} collective-permute-done((bf16[256,256]{1,0:T(8,128)(2,1)S(1)}, bf16[256,256]{1,0:T(8,128)(2,1)S(1)}, u32[]{:S(2)}, u32[]{:S(2)}) %collective-permute-start.12) | collective-permute-done | bytes 131104 | tf_op jit(solution)/shard_map/ppermute | solution.py:113
  70.9 9.9 %collective-permute-done.14 = bf16[2,256,256]{2,1,0:T(8,128)(2,1)S(1)} collective-permute-done((bf16[2,256,256]{2,1,0:T(8,128)(2,1)S(1)}, bf16[2,256,256]{2,1,0:T(8,128)(2,1)S(1)}, u32[]{:S(2)}, u32[]{:S(2)}) %collective-permute-start.14) | collective-permute-done | bytes 262176 | tf_op jit(solution)/shard_map/ppermute | solution.py:113
  83.6 1.6 collective-permute-start.17
  85.8 4.2 %collective-permute-done.17 = bf16[256,256]{1,0:T(8,128)(2,1)S(1)} collective-permute-done((bf16[256,256]{1,0:T(8,128)(2,1)S(1)}, bf16[256,256]{1,0:T(8,128)(2,1)S(1)}, u32[]{:S(2)}, u32[]{:S(2)}) %collective-permute-start.17) | collective-permute-done | bytes 131104 | tf_op jit(solution)/shard_map/ppermute | solution.py:113
  91.1 1.6 collective-permute-start.24
  92.7 2.8 %collective-permute-done.21 = bf16[2,256,256]{2,1,0:T(8,128)(2,1)S(1)} collective-permute-done((bf16[2,256,256]{2,1,0:T(8,128)(2,1)S(1)}, bf16[2,256,256]{2,1,0:T(8,128)(2,1)S(1)}, u32[]{:S(2)}, u32[]{:S(2)}) %collective-permute-start.21) | collective-permute-done | bytes 262176 | tf_op jit(solution)/shard_map/ppermute | solution.py:113
  96.7 2.6 %collective-permute-start.19 = (bf16[768,256]{1,0:T(8,128)(2,1)S(1)}, bf16[768,256]{1,0:T(8,128)(2,1)S(1)}, u32[]{:S(2)}, u32[]{:S(2)}) collective-permute-start(bf16[768,256]{1,0:T(8,128)(2,1)S(1)} %multiply_convert_fusion.3), channel_id=1, source_target_pairs={{0,2},{1,3},{2,0},{3,1},{4,6},{5,7},{6,4},{7,5},{8,10},{9,11},{10,... | collective-permute-start | bytes 1179656 | tf_op jit(solution)/shard_map/ppermute | solution.py:113
  99.3 1.5 collective-permute-start.23
  100.9 2.6 %collective-permute-done.24 = bf16[768,256]{1,0:T(8,128)(2,1)S(1)} collective-permute-done((bf16[768,256]{1,0:T(8,128)(2,1)S(1)}, bf16[768,256]{1,0:T(8,128)(2,1)S(1)}, u32[]{:S(2)}, u32[]{:S(2)}) %collective-permute-start.24) | collective-permute-done | bytes 393248 | tf_op jit(solution)/shard_map/ppermute | solution.py:113
  108.0 1.5 collective-permute-start.31
  109.5 2.4 %collective-permute-done.19 = bf16[768,256]{1,0:T(8,128)(2,1)S(1)} collective-permute-done((bf16[768,256]{1,0:T(8,128)(2,1)S(1)}, bf16[768,256]{1,0:T(8,128)(2,1)S(1)}, u32[]{:S(2)}, u32[]{:S(2)}) %collective-permute-start.19) | collective-permute-done | bytes 393248 | tf_op jit(solution)/shard_map/ppermute | solution.py:113
  114.1 1.6 collective-permute-start.27
  116.4 4.0 %collective-permute-done.28 = bf16[768,256]{1,0:T(8,128)(2,1)S(1)} collective-permute-done((bf16[768,256]{1,0:T(8,128)(2,1)S(1)}, bf16[768,256]{1,0:T(8,128)(2,1)S(1)}, u32[]{:S(2)}, u32[]{:S(2)}) %collective-permute-start.28) | collective-permute-done | bytes 393248 | tf_op jit(solution)/shard_map/ppermute | solution.py:113
  124.8 1.6 collective-permute-start.39
  126.4 3.2 %collective-permute-start.29 = (bf16[2,256,256]{2,1,0:T(8,128)(2,1)S(1)}, bf16[2,256,256]{2,1,0:T(8,128)(2,1)S(1)}, u32[]{:S(2)}, u32[]{:S(2)}) collective-permute-start(bf16[2,256,256]{2,1,0:T(8,128)(2,1)S(1)} %add_convert_fusion.11), channel_id=1, source_target_pairs={{0,24},{4,28},{8,0},{12,4},{16,8},{20,12},{24,16},{28,20},{1,25},{... | collective-permute-start | bytes 786440 | tf_op jit(solution)/shard_map/ppermute | solution.py:113
  134.1 2.0 collective-permute-done.29
  136.2 4.3 %collective-permute-start.33 = (bf16[2,256,256]{2,1,0:T(8,128)(2,1)S(1)}, bf16[2,256,256]{2,1,0:T(8,128)(2,1)S(1)}, u32[]{:S(2)}, u32[]{:S(2)}) collective-permute-start(bf16[2,256,256]{2,1,0:T(8,128)(2,1)S(1)} %add_convert_fusion.10), channel_id=1, source_target_pairs={{0,24},{4,28},{8,0},{12,4},{16,8},{20,12},{24,16},{28,20},{1,25},{... | collective-permute-start | bytes 786440 | tf_op jit(solution)/shard_map/ppermute | solution.py:113
  140.9 1.9 collective-permute-done.34
  145.3 1.9 collective-permute-done.33
  147.5 4.6 %collective-permute-start.36 = (bf16[2,256,256]{2,1,0:T(8,128)(2,1)S(1)}, bf16[2,256,256]{2,1,0:T(8,128)(2,1)S(1)}, u32[]{:S(2)}, u32[]{:S(2)}) collective-permute-start(bf16[2,256,256]{2,1,0:T(8,128)(2,1)S(1)} %add_convert_fusion.8), channel_id=1, source_target_pairs={{0,24},{4,28},{8,0},{12,4},{16,8},{20,12},{24,16},{28,20},{1,25},{... | collective-permute-start | bytes 786440 | tf_op jit(solution)/shard_map/ppermute | solution.py:113
  154.2 1.6 collective-permute-start.38
  157.5 1.6 collective-permute-start.44
  159.0 1.5 collective-permute-done.38
  162.2 1.7 collective-permute-start.46
  165.6 3.4 %collective-permute-start.43 = (bf16[2,256,256]{2,1,0:T(8,128)(2,1)S(1)}, bf16[2,256,256]{2,1,0:T(8,128)(2,1)S(1)}, u32[]{:S(2)}, u32[]{:S(2)}) collective-permute-start(bf16[2,256,256]{2,1,0:T(8,128)(2,1)S(1)} %add_convert_fusion.5), channel_id=1, source_target_pairs={{0,24},{4,28},{8,0},{12,4},{16,8},{20,12},{24,16},{28,20},{1,25},{... | collective-permute-start | bytes 786440 | tf_op jit(solution)/shard_map/ppermute | solution.py:113
  171.0 3.6 %collective-permute-start.47 = (bf16[2,256,256]{2,1,0:T(8,128)(2,1)S(1)}, bf16[2,256,256]{2,1,0:T(8,128)(2,1)S(1)}, u32[]{:S(2)}, u32[]{:S(2)}) collective-permute-start(bf16[2,256,256]{2,1,0:T(8,128)(2,1)S(1)} %add_convert_fusion.3), channel_id=1, source_target_pairs={{0,24},{4,28},{8,0},{12,4},{16,8},{20,12},{24,16},{28,20},{1,25},{... | collective-permute-start | bytes 786440 | tf_op jit(solution)/shard_map/ppermute | solution.py:113
  176.0 5.3 %collective-permute-done.49 = bf16[2,256,256]{2,1,0:T(8,128)(2,1)S(1)} collective-permute-done((bf16[2,256,256]{2,1,0:T(8,128)(2,1)S(1)}, bf16[2,256,256]{2,1,0:T(8,128)(2,1)S(1)}, u32[]{:S(2)}, u32[]{:S(2)}) %collective-permute-start.49) | collective-permute-done | bytes 262176 | tf_op jit(solution)/shard_map/ppermute | solution.py:113
  181.5 4.3 %collective-permute-start.51 = (bf16[2,256,256]{2,1,0:T(8,128)(2,1)S(1)}, bf16[2,256,256]{2,1,0:T(8,128)(2,1)S(1)}, u32[]{:S(2)}, u32[]{:S(2)}) collective-permute-start(bf16[2,256,256]{2,1,0:T(8,128)(2,1)S(1)} %add_convert_fusion.2), channel_id=1, source_target_pairs={{0,24},{4,28},{8,0},{12,4},{16,8},{20,12},{24,16},{28,20},{1,25},{... | collective-permute-start | bytes 786440 | tf_op jit(solution)/shard_map/ppermute | solution.py:113
  186.5 4.3 %collective-permute-start.50 = (bf16[2,256,256]{2,1,0:T(8,128)(2,1)S(1)}, bf16[2,256,256]{2,1,0:T(8,128)(2,1)S(1)}, u32[]{:S(2)}, u32[]{:S(2)}) collective-permute-start(bf16[2,256,256]{2,1,0:T(8,128)(2,1)S(1)} %add_convert_fusion.1), channel_id=1, source_target_pairs={{0,24},{4,28},{8,0},{12,4},{16,8},{20,12},{24,16},{28,20},{1,25},{... | collective-permute-start | bytes 786440 | tf_op jit(solution)/shard_map/ppermute | solution.py:113
  191.5 2.8 %collective-permute-start.52 = (bf16[2,256,256]{2,1,0:T(8,128)(2,1)S(1)}, bf16[2,256,256]{2,1,0:T(8,128)(2,1)S(1)}, u32[]{:S(2)}, u32[]{:S(2)}) collective-permute-start(bf16[2,256,256]{2,1,0:T(8,128)(2,1)S(1)} %add_convert_fusion), channel_id=1, source_target_pairs={{0,24},{4,28},{8,0},{12,4},{16,8},{20,12},{24,16},{28,20},{1,25},{... | collective-permute-start | bytes 786440 | tf_op jit(solution)/shard_map/ppermute | solution.py:113
  194.3 3.1 %collective-permute-done.50 = bf16[2,256,256]{2,1,0:T(8,128)(2,1)S(1)} collective-permute-done((bf16[2,256,256]{2,1,0:T(8,128)(2,1)S(1)}, bf16[2,256,256]{2,1,0:T(8,128)(2,1)S(1)}, u32[]{:S(2)}, u32[]{:S(2)}) %collective-permute-start.50) | collective-permute-done | bytes 262176 | tf_op jit(solution)/shard_map/ppermute | solution.py:113
  197.7 2.6 %collective-permute-done.52 = bf16[2,256,256]{2,1,0:T(8,128)(2,1)S(1)} collective-permute-done((bf16[2,256,256]{2,1,0:T(8,128)(2,1)S(1)}, bf16[2,256,256]{2,1,0:T(8,128)(2,1)S(1)}, u32[]{:S(2)}, u32[]{:S(2)}) %collective-permute-start.52) | collective-permute-done | bytes 262176 | tf_op jit(solution)/shard_map/ppermute | solution.py:113
  202.8 2.7 %multiply_subtract_fusion = (f32[2,128,2048]{2,1,0:T(8,128)}, f32[2,128,2048]{2,1,0:T(8,128)}) fusion(f32[2,128,2048]{2,1,0:T(8,128)S(1)} %copy-done, f32[2,128,1024]{2,1,0:T(8,128)S(1)} %get-tuple-element.211, f32[2,128,1024]{2,1,0:T(8,128)S(1)} %get-tuple-element.210, f32[2,128,2048]{2,1,0:T(8,128)S(1)} %copy-done.1), kind=kLoop, calls=%fused_computation.1 | loop fusion | flops 3670016 | bytes 10485760 | tf_op jit(solution)/shard_map/sub | solution.py:288
  (221 shorter events, 51.1 us)
Async XLA Ops:
  10.7 11.1 %collective-permute-start.1 = (bf16[384,2048]{1,0:T(8,128)(2,1)S(1)}, bf16[384,2048]{1,0:T(8,128)(2,1)}, u32[]{:S(2)}, u32[]{:S(2)}) collective-permute-start(bf16[384,2048]{1,0:T(8,128)(2,1)S(1)} %copy-done.2), channel_id=1, source_target_pairs={{0,1},{1,0},{2,3},{3,2},{4,5},{5,4},{6,7},{7,6},{8,9},{9,8},{10,11... | collective-permute-start | bytes 4718600 | tf_op jit(solution)/shard_map/ppermute | solution.py:113
  10.8 42.5 %collective-permute-start.2 = (bf16[384,2048]{1,0:T(8,128)(2,1)}, bf16[384,2048]{1,0:T(8,128)(2,1)S(1)}, u32[]{:S(2)}, u32[]{:S(2)}) collective-permute-start(bf16[384,2048]{1,0:T(8,128)(2,1)} %get-tuple-element.111), channel_id=1, source_target_pairs={{0,2},{1,3},{2,0},{3,1},{4,6},{5,7},{6,4},{7,5},{8,10},{9,11},{10,... | collective-permute-start | bytes 4718600 | tf_op jit(solution)/shard_map/ppermute | solution.py:113
  20.2 10.9 %collective-permute-start.5 = (bf16[2,256,256]{2,1,0:T(8,128)(2,1)S(1)}, bf16[2,256,256]{2,1,0:T(8,128)(2,1)S(1)}, u32[]{:S(2)}, u32[]{:S(2)}) collective-permute-start(bf16[2,256,256]{2,1,0:T(8,128)(2,1)S(1)} %copy-done.5), channel_id=1, source_target_pairs={{0,8},{4,12},{8,16},{12,20},{16,24},{20,28},{24,0},{28,4},{1,9},{5... | collective-permute-start | bytes 786440 | tf_op jit(solution)/shard_map/ppermute | solution.py:113
  23.7 13.0 %collective-permute-start.4 = (bf16[2,256,256]{2,1,0:T(8,128)(2,1)S(1)}, bf16[2,256,256]{2,1,0:T(8,128)(2,1)S(1)}, u32[]{:S(2)}, u32[]{:S(2)}) collective-permute-start(bf16[2,256,256]{2,1,0:T(8,128)(2,1)S(1)} %copy-done.4), channel_id=1, source_target_pairs={{0,8},{4,12},{8,16},{12,20},{16,24},{20,28},{24,0},{28,4},{1,9},{5... | collective-permute-start | bytes 786440 | tf_op jit(solution)/shard_map/ppermute | solution.py:113
  31.1 11.2 %collective-permute-start.8 = (bf16[2,256,256]{2,1,0:T(8,128)(2,1)S(1)}, bf16[2,256,256]{2,1,0:T(8,128)(2,1)S(1)}, u32[]{:S(2)}, u32[]{:S(2)}) collective-permute-start(bf16[2,256,256]{2,1,0:T(8,128)(2,1)S(1)} %collective-permute-done.5), channel_id=1, source_target_pairs={{0,8},{4,12},{8,16},{12,20},{16,24},{20,28},{24,0},{28,4},{1,9},{5... | collective-permute-start | bytes 786440 | tf_op jit(solution)/shard_map/ppermute | solution.py:113
  36.8 11.2 %collective-permute-start.7 = (bf16[2,256,256]{2,1,0:T(8,128)(2,1)S(1)}, bf16[2,256,256]{2,1,0:T(8,128)(2,1)S(1)}, u32[]{:S(2)}, u32[]{:S(2)}) collective-permute-start(bf16[2,256,256]{2,1,0:T(8,128)(2,1)S(1)} %collective-permute-done.4), channel_id=1, source_target_pairs={{0,8},{4,12},{8,16},{12,20},{16,24},{20,28},{24,0},{28,4},{1,9},{5... | collective-permute-start | bytes 786440 | tf_op jit(solution)/shard_map/ppermute | solution.py:113
  36.8 16.5 %collective-permute-start.6 = (bf16[2,256,256]{2,1,0:T(8,128)(2,1)S(1)}, bf16[2,256,256]{2,1,0:T(8,128)(2,1)S(1)}, u32[]{:S(2)}, u32[]{:S(2)}) collective-permute-start(bf16[2,256,256]{2,1,0:T(8,128)(2,1)S(1)} %copy-done.3), channel_id=1, source_target_pairs={{0,8},{4,12},{8,16},{12,20},{16,24},{20,28},{24,0},{28,4},{1,9},{5... | collective-permute-start | bytes 786440 | tf_op jit(solution)/shard_map/ppermute | solution.py:113
  53.3 27.5 %collective-permute-start.9 = (bf16[384,2048]{1,0:T(8,128)(2,1)S(1)}, bf16[384,2048]{1,0:T(8,128)(2,1)S(1)}, u32[]{:S(2)}, u32[]{:S(2)}) collective-permute-start(bf16[384,2048]{1,0:T(8,128)(2,1)S(1)} %collective-permute-done.2), channel_id=1, source_target_pairs={{0,1},{1,0},{2,3},{3,2},{4,5},{5,4},{6,7},{7,6},{8,9},{9,8},{10,11... | collective-permute-start | bytes 4718600 | tf_op jit(solution)/shard_map/ppermute | solution.py:113
  53.3 11.0 %collective-permute-start.10 = (bf16[2,256,256]{2,1,0:T(8,128)(2,1)S(1)}, bf16[2,256,256]{2,1,0:T(8,128)(2,1)S(1)}, u32[]{:S(2)}, u32[]{:S(2)}) collective-permute-start(bf16[2,256,256]{2,1,0:T(8,128)(2,1)S(1)} %collective-permute-done.8), channel_id=1, source_target_pairs={{0,8},{4,12},{8,16},{12,20},{16,24},{20,28},{24,0},{28,4},{1,9},{5... | collective-permute-start | bytes 786440 | tf_op jit(solution)/shard_map/ppermute | solution.py:113
  53.4 12.5 %collective-permute-start.11 = (bf16[768,256]{1,0:T(8,128)(2,1)S(1)}, bf16[768,256]{1,0:T(8,128)(2,1)S(1)}, u32[]{:S(2)}, u32[]{:S(2)}) collective-permute-start(bf16[768,256]{1,0:T(8,128)(2,1)S(1)} %pad_maximum_fusion.19), channel_id=1, source_target_pairs={{0,4},{4,0},{8,12},{12,8},{16,20},{20,16},{24,28},{28,24},{1,5},{5... | collective-permute-start | bytes 1179656 | tf_op jit(solution)/shard_map/ppermute | solution.py:113
  55.0 15.8 %collective-permute-start.15 = (bf16[2,256,256]{2,1,0:T(8,128)(2,1)S(1)}, bf16[2,256,256]{2,1,0:T(8,128)(2,1)S(1)}, u32[]{:S(2)}, u32[]{:S(2)}) collective-permute-start(bf16[2,256,256]{2,1,0:T(8,128)(2,1)S(1)} %collective-permute-done.7), channel_id=1, source_target_pairs={{0,8},{4,12},{8,16},{12,20},{16,24},{20,28},{24,0},{28,4},{1,9},{5... | collective-permute-start | bytes 786440 | tf_op jit(solution)/shard_map/ppermute | solution.py:113
  56.3 24.4 %collective-permute-start.18 = (bf16[2,256,256]{2,1,0:T(8,128)(2,1)S(1)}, bf16[2,256,256]{2,1,0:T(8,128)(2,1)S(1)}, u32[]{:S(2)}, u32[]{:S(2)}) collective-permute-start(bf16[2,256,256]{2,1,0:T(8,128)(2,1)S(1)} %collective-permute-done.6), channel_id=1, source_target_pairs={{0,8},{4,12},{8,16},{12,20},{16,24},{20,28},{24,0},{28,4},{1,9},{5... | collective-permute-start | bytes 786440 | tf_op jit(solution)/shard_map/ppermute | solution.py:113
  65.9 14.8 %collective-permute-start.14 = (bf16[2,256,256]{2,1,0:T(8,128)(2,1)S(1)}, bf16[2,256,256]{2,1,0:T(8,128)(2,1)S(1)}, u32[]{:S(2)}, u32[]{:S(2)}) collective-permute-start(bf16[2,256,256]{2,1,0:T(8,128)(2,1)S(1)} %get-tuple-element.155), channel_id=1, source_target_pairs={{0,8},{4,12},{8,16},{12,20},{16,24},{20,28},{24,0},{28,4},{1,9},{5... | collective-permute-start | bytes 786440 | tf_op jit(solution)/shard_map/ppermute | solution.py:113
  69.3 11.5 %collective-permute-start.16 = (bf16[768,256]{1,0:T(8,128)(2,1)S(1)}, bf16[768,256]{1,0:T(8,128)(2,1)S(1)}, u32[]{:S(2)}, u32[]{:S(2)}) collective-permute-start(bf16[768,256]{1,0:T(8,128)(2,1)S(1)} %pad_maximum_fusion.20), channel_id=1, source_target_pairs={{0,4},{4,0},{8,12},{12,8},{16,20},{20,16},{24,28},{28,24},{1,5},{5... | collective-permute-start | bytes 1179656 | tf_op jit(solution)/shard_map/ppermute | solution.py:113
  83.0 12.5 %collective-permute-start.13 = (bf16[768,256]{1,0:T(8,128)(2,1)S(1)}, bf16[768,256]{1,0:T(8,128)(2,1)S(1)}, u32[]{:S(2)}, u32[]{:S(2)}) collective-permute-start(bf16[768,256]{1,0:T(8,128)(2,1)S(1)} %convolution_convert_fusion.3), channel_id=1, source_target_pairs={{0,2},{1,3},{2,0},{3,1},{4,6},{5,7},{6,4},{7,5},{8,10},{9,11},{10,... | collective-permute-start | bytes 1179656 | tf_op jit(solution)/shard_map/ppermute | solution.py:113
  85.2 15.7 %collective-permute-start.22 = (bf16[768,256]{1,0:T(8,128)(2,1)S(1)}, bf16[768,256]{1,0:T(8,128)(2,1)S(1)}, u32[]{:S(2)}, u32[]{:S(2)}) collective-permute-start(bf16[768,256]{1,0:T(8,128)(2,1)S(1)} %pad_maximum_fusion.21), channel_id=1, source_target_pairs={{0,4},{4,0},{8,12},{12,8},{16,20},{20,16},{24,28},{28,24},{1,5},{5... | collective-permute-start | bytes 1179656 | tf_op jit(solution)/shard_map/ppermute | solution.py:113
  85.8 9.7 %collective-permute-start.21 = (bf16[2,256,256]{2,1,0:T(8,128)(2,1)S(1)}, bf16[2,256,256]{2,1,0:T(8,128)(2,1)S(1)}, u32[]{:S(2)}, u32[]{:S(2)}) collective-permute-start(bf16[2,256,256]{2,1,0:T(8,128)(2,1)S(1)} %collective-permute-done.18), channel_id=1, source_target_pairs={{0,8},{4,12},{8,16},{12,20},{16,24},{20,28},{24,0},{28,4},{1,9},{5... | collective-permute-start | bytes 786440 | tf_op jit(solution)/shard_map/ppermute | solution.py:113
  91.1 12.4 %collective-permute-start.24 = (bf16[768,256]{1,0:T(8,128)(2,1)S(1)}, bf16[768,256]{1,0:T(8,128)(2,1)S(1)}, u32[]{:S(2)}, u32[]{:S(2)}) collective-permute-start(bf16[768,256]{1,0:T(8,128)(2,1)S(1)} %convolution_convert_fusion.2), channel_id=1, source_target_pairs={{0,2},{1,3},{2,0},{3,1},{4,6},{5,7},{6,4},{7,5},{8,10},{9,11},{10,... | collective-permute-start | bytes 1179656 | tf_op jit(solution)/shard_map/ppermute | solution.py:113
  92.7 8.2 %collective-permute-start.20 = (bf16[2,256,256]{2,1,0:T(8,128)(2,1)S(1)}, bf16[2,256,256]{2,1,0:T(8,128)(2,1)S(1)}, u32[]{:S(2)}, u32[]{:S(2)}) collective-permute-start(bf16[2,256,256]{2,1,0:T(8,128)(2,1)S(1)} %collective-permute-done.14), channel_id=1, source_target_pairs={{0,8},{4,12},{8,16},{12,20},{16,24},{20,28},{24,0},{28,4},{1,9},{5... | collective-permute-start | bytes 786440 | tf_op jit(solution)/shard_map/ppermute | solution.py:113
  96.7 15.2 %collective-permute-start.19 = (bf16[768,256]{1,0:T(8,128)(2,1)S(1)}, bf16[768,256]{1,0:T(8,128)(2,1)S(1)}, u32[]{:S(2)}, u32[]{:S(2)}) collective-permute-start(bf16[768,256]{1,0:T(8,128)(2,1)S(1)} %multiply_convert_fusion.3), channel_id=1, source_target_pairs={{0,2},{1,3},{2,0},{3,1},{4,6},{5,7},{6,4},{7,5},{8,10},{9,11},{10,... | collective-permute-start | bytes 1179656 | tf_op jit(solution)/shard_map/ppermute | solution.py:113
  104.7 15.6 %collective-permute-start.28 = (bf16[768,256]{1,0:T(8,128)(2,1)S(1)}, bf16[768,256]{1,0:T(8,128)(2,1)S(1)}, u32[]{:S(2)}, u32[]{:S(2)}) collective-permute-start(bf16[768,256]{1,0:T(8,128)(2,1)S(1)} %multiply_convert_fusion.2), channel_id=1, source_target_pairs={{0,2},{1,3},{2,0},{3,1},{4,6},{5,7},{6,4},{7,5},{8,10},{9,11},{10,... | collective-permute-start | bytes 1179656 | tf_op jit(solution)/shard_map/ppermute | solution.py:113
  106.0 9.6 %collective-permute-start.25 = (bf16[2,256,256]{2,1,0:T(8,128)(2,1)S(1)}, bf16[2,256,256]{2,1,0:T(8,128)(2,1)S(1)}, u32[]{:S(2)}, u32[]{:S(2)}) collective-permute-start(bf16[2,256,256]{2,1,0:T(8,128)(2,1)S(1)} %collective-permute-done.20), channel_id=1, source_target_pairs={{0,8},{4,12},{8,16},{12,20},{16,24},{20,28},{24,0},{28,4},{1,9},{5... | collective-permute-start | bytes 786440 | tf_op jit(solution)/shard_map/ppermute | solution.py:113
  107.0 23.6 %collective-permute-start.30 = (bf16[768,256]{1,0:T(8,128)(2,1)S(1)}, bf16[768,256]{1,0:T(8,128)(2,1)S(1)}, u32[]{:S(2)}, u32[]{:S(2)}) collective-permute-start(bf16[768,256]{1,0:T(8,128)(2,1)S(1)} %convolution_convert_fusion.1), channel_id=1, source_target_pairs={{0,2},{1,3},{2,0},{3,1},{4,6},{5,7},{6,4},{7,5},{8,10},{9,11},{10,... | collective-permute-start | bytes 1179656 | tf_op jit(solution)/shard_map/ppermute | solution.py:113
  108.0 16.8 %collective-permute-start.31 = (bf16[768,256]{1,0:T(8,128)(2,1)S(1)}, bf16[768,256]{1,0:T(8,128)(2,1)S(1)}, u32[]{:S(2)}, u32[]{:S(2)}) collective-permute-start(bf16[768,256]{1,0:T(8,128)(2,1)S(1)} %pad_maximum_fusion.22), channel_id=1, source_target_pairs={{0,4},{4,0},{8,12},{12,8},{16,20},{20,16},{24,28},{28,24},{1,5},{5... | collective-permute-start | bytes 1179656 | tf_op jit(solution)/shard_map/ppermute | solution.py:113
  114.1 9.9 %collective-permute-start.27 = (bf16[256,256]{1,0:T(8,128)(2,1)S(1)}, bf16[256,256]{1,0:T(8,128)(2,1)S(1)}, u32[]{:S(2)}, u32[]{:S(2)}) collective-permute-start(bf16[256,256]{1,0:T(8,128)(2,1)S(1)} %slice.260), channel_id=1, source_target_pairs={{0,4},{4,0},{8,12},{12,8},{16,20},{20,16},{24,28},{28,24},{1,5},{5... | collective-permute-start | bytes 393224 | tf_op jit(solution)/shard_map/ppermute | solution.py:113
  115.7 10.7 %collective-permute-start.32 = (bf16[256,256]{1,0:T(8,128)(2,1)S(1)}, bf16[256,256]{1,0:T(8,128)(2,1)S(1)}, u32[]{:S(2)}, u32[]{:S(2)}) collective-permute-start(bf16[256,256]{1,0:T(8,128)(2,1)S(1)} %dynamic-slice_bitcast_fusion), channel_id=1, source_target_pairs={{0,4},{4,0},{8,12},{12,8},{16,20},{20,16},{24,28},{28,24},{1,5},{5... | collective-permute-start | bytes 393224 | tf_op jit(solution)/shard_map/ppermute | solution.py:113
  120.3 12.8 %collective-permute-start.26 = (bf16[768,256]{1,0:T(8,128)(2,1)S(1)}, bf16[768,256]{1,0:T(8,128)(2,1)S(1)}, u32[]{:S(2)}, u32[]{:S(2)}) collective-permute-start(bf16[768,256]{1,0:T(8,128)(2,1)S(1)} %slice.259), channel_id=1, source_target_pairs={{0,4},{4,0},{8,12},{12,8},{16,20},{20,16},{24,28},{28,24},{1,5},{5... | collective-permute-start | bytes 1179656 | tf_op jit(solution)/shard_map/ppermute | solution.py:113
  124.0 16.6 %collective-permute-start.35 = (bf16[256,256]{1,0:T(8,128)(2,1)S(1)}, bf16[256,256]{1,0:T(8,128)(2,1)S(1)}, u32[]{:S(2)}, u32[]{:S(2)}) collective-permute-start(bf16[256,256]{1,0:T(8,128)(2,1)S(1)} %slice.268), channel_id=1, source_target_pairs={{0,4},{4,0},{8,12},{12,8},{16,20},{20,16},{24,28},{28,24},{1,5},{5... | collective-permute-start | bytes 393224 | tf_op jit(solution)/shard_map/ppermute | solution.py:113
  124.8 20.5 %collective-permute-start.39 = (bf16[768,256]{1,0:T(8,128)(2,1)S(1)}, bf16[768,256]{1,0:T(8,128)(2,1)S(1)}, u32[]{:S(2)}, u32[]{:S(2)}) collective-permute-start(bf16[768,256]{1,0:T(8,128)(2,1)S(1)} %slice.267), channel_id=1, source_target_pairs={{0,4},{4,0},{8,12},{12,8},{16,20},{20,16},{24,28},{28,24},{1,5},{5... | collective-permute-start | bytes 1179656 | tf_op jit(solution)/shard_map/ppermute | solution.py:113
  126.4 9.7 %collective-permute-start.29 = (bf16[2,256,256]{2,1,0:T(8,128)(2,1)S(1)}, bf16[2,256,256]{2,1,0:T(8,128)(2,1)S(1)}, u32[]{:S(2)}, u32[]{:S(2)}) collective-permute-start(bf16[2,256,256]{2,1,0:T(8,128)(2,1)S(1)} %add_convert_fusion.11), channel_id=1, source_target_pairs={{0,24},{4,28},{8,0},{12,4},{16,8},{20,12},{24,16},{28,20},{1,25},{... | collective-permute-start | bytes 786440 | tf_op jit(solution)/shard_map/ppermute | solution.py:113
  130.7 12.1 %collective-permute-start.34 = (bf16[768,256]{1,0:T(8,128)(2,1)S(1)}, bf16[768,256]{1,0:T(8,128)(2,1)S(1)}, u32[]{:S(2)}, u32[]{:S(2)}) collective-permute-start(bf16[768,256]{1,0:T(8,128)(2,1)S(1)} %convolution_convert_fusion), channel_id=1, source_target_pairs={{0,2},{1,3},{2,0},{3,1},{4,6},{5,7},{6,4},{7,5},{8,10},{9,11},{10,... | collective-permute-start | bytes 1179656 | tf_op jit(solution)/shard_map/ppermute | solution.py:113
  133.2 18.8 %collective-permute-start.37 = (bf16[768,256]{1,0:T(8,128)(2,1)S(1)}, bf16[768,256]{1,0:T(8,128)(2,1)S(1)}, u32[]{:S(2)}, u32[]{:S(2)}) collective-permute-start(bf16[768,256]{1,0:T(8,128)(2,1)S(1)} %multiply_convert_fusion.1), channel_id=1, source_target_pairs={{0,2},{1,3},{2,0},{3,1},{4,6},{5,7},{6,4},{7,5},{8,10},{9,11},{10,... | collective-permute-start | bytes 1179656 | tf_op jit(solution)/shard_map/ppermute | solution.py:113
  136.2 11.0 %collective-permute-start.33 = (bf16[2,256,256]{2,1,0:T(8,128)(2,1)S(1)}, bf16[2,256,256]{2,1,0:T(8,128)(2,1)S(1)}, u32[]{:S(2)}, u32[]{:S(2)}) collective-permute-start(bf16[2,256,256]{2,1,0:T(8,128)(2,1)S(1)} %add_convert_fusion.10), channel_id=1, source_target_pairs={{0,24},{4,28},{8,0},{12,4},{16,8},{20,12},{24,16},{28,20},{1,25},{... | collective-permute-start | bytes 786440 | tf_op jit(solution)/shard_map/ppermute | solution.py:113
  140.7 15.2 %collective-permute-start.40 = (bf16[2,256,256]{2,1,0:T(8,128)(2,1)S(1)}, bf16[2,256,256]{2,1,0:T(8,128)(2,1)S(1)}, u32[]{:S(2)}, u32[]{:S(2)}) collective-permute-start(bf16[2,256,256]{2,1,0:T(8,128)(2,1)S(1)} %add_convert_fusion.9), channel_id=1, source_target_pairs={{0,24},{4,28},{8,0},{12,4},{16,8},{20,12},{24,16},{28,20},{1,25},{... | collective-permute-start | bytes 786440 | tf_op jit(solution)/shard_map/ppermute | solution.py:113
  144.0 17.1 %collective-permute-start.42 = (bf16[768,256]{1,0:T(8,128)(2,1)S(1)}, bf16[768,256]{1,0:T(8,128)(2,1)S(1)}, u32[]{:S(2)}, u32[]{:S(2)}) collective-permute-start(bf16[768,256]{1,0:T(8,128)(2,1)S(1)} %multiply_convert_fusion), channel_id=1, source_target_pairs={{0,2},{1,3},{2,0},{3,1},{4,6},{5,7},{6,4},{7,5},{8,10},{9,11},{10,... | collective-permute-start | bytes 1179656 | tf_op jit(solution)/shard_map/ppermute | solution.py:113
  147.5 13.4 %collective-permute-start.36 = (bf16[2,256,256]{2,1,0:T(8,128)(2,1)S(1)}, bf16[2,256,256]{2,1,0:T(8,128)(2,1)S(1)}, u32[]{:S(2)}, u32[]{:S(2)}) collective-permute-start(bf16[2,256,256]{2,1,0:T(8,128)(2,1)S(1)} %add_convert_fusion.8), channel_id=1, source_target_pairs={{0,24},{4,28},{8,0},{12,4},{16,8},{20,12},{24,16},{28,20},{1,25},{... | collective-permute-start | bytes 786440 | tf_op jit(solution)/shard_map/ppermute | solution.py:113
  156.2 9.2 %collective-permute-start.41 = (bf16[2,256,256]{2,1,0:T(8,128)(2,1)S(1)}, bf16[2,256,256]{2,1,0:T(8,128)(2,1)S(1)}, u32[]{:S(2)}, u32[]{:S(2)}) collective-permute-start(bf16[2,256,256]{2,1,0:T(8,128)(2,1)S(1)} %add_convert_fusion.7), channel_id=1, source_target_pairs={{0,24},{4,28},{8,0},{12,4},{16,8},{20,12},{24,16},{28,20},{1,25},{... | collective-permute-start | bytes 786440 | tf_op jit(solution)/shard_map/ppermute | solution.py:113
  157.5 12.2 %collective-permute-start.44 = (bf16[768,256]{1,0:T(8,128)(2,1)S(1)}, bf16[768,256]{1,0:T(8,128)(2,1)S(1)}, u32[]{:S(2)}, u32[]{:S(2)}) collective-permute-start(bf16[768,256]{1,0:T(8,128)(2,1)S(1)} %slice.274), channel_id=1, source_target_pairs={{0,4},{4,0},{8,12},{12,8},{16,20},{20,16},{24,28},{28,24},{1,5},{5... | collective-permute-start | bytes 1179656 | tf_op jit(solution)/shard_map/ppermute | solution.py:113
  160.7 10.1 %collective-permute-start.45 = (bf16[2,256,256]{2,1,0:T(8,128)(2,1)S(1)}, bf16[2,256,256]{2,1,0:T(8,128)(2,1)S(1)}, u32[]{:S(2)}, u32[]{:S(2)}) collective-permute-start(bf16[2,256,256]{2,1,0:T(8,128)(2,1)S(1)} %add_convert_fusion.6), channel_id=1, source_target_pairs={{0,24},{4,28},{8,0},{12,4},{16,8},{20,12},{24,16},{28,20},{1,25},{... | collective-permute-start | bytes 786440 | tf_op jit(solution)/shard_map/ppermute | solution.py:113
  164.9 11.0 %collective-permute-start.48 = (bf16[768,256]{1,0:T(8,128)(2,1)S(1)}, bf16[768,256]{1,0:T(8,128)(2,1)S(1)}, u32[]{:S(2)}, u32[]{:S(2)}) collective-permute-start(bf16[768,256]{1,0:T(8,128)(2,1)S(1)} %slice.283), channel_id=1, source_target_pairs={{0,4},{4,0},{8,12},{12,8},{16,20},{20,16},{24,28},{28,24},{1,5},{5... | collective-permute-start | bytes 1179656 | tf_op jit(solution)/shard_map/ppermute | solution.py:113
  165.6 10.1 %collective-permute-start.43 = (bf16[2,256,256]{2,1,0:T(8,128)(2,1)S(1)}, bf16[2,256,256]{2,1,0:T(8,128)(2,1)S(1)}, u32[]{:S(2)}, u32[]{:S(2)}) collective-permute-start(bf16[2,256,256]{2,1,0:T(8,128)(2,1)S(1)} %add_convert_fusion.5), channel_id=1, source_target_pairs={{0,24},{4,28},{8,0},{12,4},{16,8},{20,12},{24,16},{28,20},{1,25},{... | collective-permute-start | bytes 786440 | tf_op jit(solution)/shard_map/ppermute | solution.py:113
  169.2 12.1 %collective-permute-start.49 = (bf16[2,256,256]{2,1,0:T(8,128)(2,1)S(1)}, bf16[2,256,256]{2,1,0:T(8,128)(2,1)S(1)}, u32[]{:S(2)}, u32[]{:S(2)}) collective-permute-start(bf16[2,256,256]{2,1,0:T(8,128)(2,1)S(1)} %add_convert_fusion.4), channel_id=1, source_target_pairs={{0,24},{4,28},{8,0},{12,4},{16,8},{20,12},{24,16},{28,20},{1,25},{... | collective-permute-start | bytes 786440 | tf_op jit(solution)/shard_map/ppermute | solution.py:113
  171.0 15.3 %collective-permute-start.47 = (bf16[2,256,256]{2,1,0:T(8,128)(2,1)S(1)}, bf16[2,256,256]{2,1,0:T(8,128)(2,1)S(1)}, u32[]{:S(2)}, u32[]{:S(2)}) collective-permute-start(bf16[2,256,256]{2,1,0:T(8,128)(2,1)S(1)} %add_convert_fusion.3), channel_id=1, source_target_pairs={{0,24},{4,28},{8,0},{12,4},{16,8},{20,12},{24,16},{28,20},{1,25},{... | collective-permute-start | bytes 786440 | tf_op jit(solution)/shard_map/ppermute | solution.py:113
  181.5 9.8 %collective-permute-start.51 = (bf16[2,256,256]{2,1,0:T(8,128)(2,1)S(1)}, bf16[2,256,256]{2,1,0:T(8,128)(2,1)S(1)}, u32[]{:S(2)}, u32[]{:S(2)}) collective-permute-start(bf16[2,256,256]{2,1,0:T(8,128)(2,1)S(1)} %add_convert_fusion.2), channel_id=1, source_target_pairs={{0,24},{4,28},{8,0},{12,4},{16,8},{20,12},{24,16},{28,20},{1,25},{... | collective-permute-start | bytes 786440 | tf_op jit(solution)/shard_map/ppermute | solution.py:113
  186.5 10.9 %collective-permute-start.50 = (bf16[2,256,256]{2,1,0:T(8,128)(2,1)S(1)}, bf16[2,256,256]{2,1,0:T(8,128)(2,1)S(1)}, u32[]{:S(2)}, u32[]{:S(2)}) collective-permute-start(bf16[2,256,256]{2,1,0:T(8,128)(2,1)S(1)} %add_convert_fusion.1), channel_id=1, source_target_pairs={{0,24},{4,28},{8,0},{12,4},{16,8},{20,12},{24,16},{28,20},{1,25},{... | collective-permute-start | bytes 786440 | tf_op jit(solution)/shard_map/ppermute | solution.py:113
  190.8 9.8 %collective-permute-start.53 = (f32[2,128,256]{2,1,0:T(8,128)S(1)}, f32[2,128,256]{2,1,0:T(8,128)S(1)}, u32[]{:S(2)}, u32[]{:S(2)}) collective-permute-start(f32[2,128,256]{2,1,0:T(8,128)S(1)} %get-tuple-element.223), channel_id=1, source_target_pairs={{0,1},{1,0},{2,3},{3,2},{4,5},{5,4},{6,7},{7,6},{8,9},{9,8},{10,11... | collective-permute-start | bytes 786440 | tf_op jit(solution)/shard_map/ppermute | solution.py:113
  190.8 9.9 %collective-permute-start.54 = (f32[2,128,256]{2,1,0:T(8,128)S(1)}, f32[2,128,256]{2,1,0:T(8,128)S(1)}, u32[]{:S(2)}, u32[]{:S(2)}) collective-permute-start(f32[2,128,256]{2,1,0:T(8,128)S(1)} %get-tuple-element.225), channel_id=1, source_target_pairs={{0,1},{1,0},{2,3},{3,2},{4,5},{5,4},{6,7},{7,6},{8,9},{9,8},{10,11... | collective-permute-start | bytes 786440 | tf_op jit(solution)/shard_map/ppermute | solution.py:113
  191.5 8.8 %collective-permute-start.52 = (bf16[2,256,256]{2,1,0:T(8,128)(2,1)S(1)}, bf16[2,256,256]{2,1,0:T(8,128)(2,1)S(1)}, u32[]{:S(2)}, u32[]{:S(2)}) collective-permute-start(bf16[2,256,256]{2,1,0:T(8,128)(2,1)S(1)} %add_convert_fusion), channel_id=1, source_target_pairs={{0,24},{4,28},{8,0},{12,4},{16,8},{20,12},{24,16},{28,20},{1,25},{... | collective-permute-start | bytes 786440 | tf_op jit(solution)/shard_map/ppermute | solution.py:113
  (17 other events, 94.6 us)

commit v3 on v2

--- a/solution.py
+++ b/solution.py
@@ -5,20 +5,20 @@
 from jax.experimental.pallas import tpu as pltpu
 from jax.sharding import PartitionSpec as P
 
-CHUNKS = 4
+CHUNKS = (2, 2, 2, 2)
 GATHER_GROUPS = ((0, 1, 2), (3,))
 SCATTER_GROUPS = ((3,), (0, 1, 2))
+TOKEN_PARTS = 1
 ORDER = (
-    "wp", "ws", "cut", "bl", "yt", "z0.1", "ct", "cp", "cc", "tn", "co", "z1.1", "z0.2", "z1.2", "z2.1",
-    "x0.0", "z0.3", "z1.3", "x1.0", "z2.2", "z3.1", "cf", "x0.1", "tf", "tk", "w0", "p0", "yp0", "x1.1",
-    "x2.0", "z2.3", "w1", "p1", "yp1", "z3.2", "s0", "ys0", "x2.1", "s1", "ys1", "z3.3", "w2", "p2", "yp2",
-    "x3.0", "gn0", "go0", "gx0.0", "x3.1", "gx0.1", "gn1", "gx1.0", "gx1.1", "go1", "a0.3", "r0.3", "w3",
-    "p3", "yp3", "s2", "ys2", "a0.2", "r0.2", "a1.3", "r1.3", "s3", "ys3", "a0.1", "r0.1", "go2", "gn2",
-    "gx2.0", "a1.2", "r1.2", "gx2.1", "a2.3", "r2.3", "a0.0", "fs0", "gn3", "gx3.0", "go3", "gx3.1", "a1.1",
-    "r1.1", "a3.3", "r3.3", "a2.2", "r2.2", "a1.0", "fs1", "a3.2", "r3.2", "a2.1", "r2.1", "a3.1", "r3.1",
-    "a2.0", "fs2", "a3.0", "fs3", "fin",
+    "wp", "ws", "cut", "bl", "ya0", "z0.1", "ct", "z1.1", "cp", "rt", "z0.2", "cc", "z1.2", "tn", "co",
+    "z2.1", "x0.0", "z0.3", "z1.3", "x1.0", "z2.2", "z3.1", "cf0", "x0.1", "tf", "tk", "w0", "p0", "yp0",
+    "x1.1", "x2.0", "z2.3", "w1", "p1", "yp1", "z3.2", "s0", "ys0", "x2.1", "s1", "ys1", "z3.3", "w2", "p2",
+    "yp2", "x3.0", "gn0", "go0", "gx0.0", "x3.1", "gx0.1", "gn1", "gx1.0", "gx1.1", "go1", "a0.3", "r0.3",
+    "w3", "p3", "yp3", "s2", "ys2", "a0.2", "r0.2", "a1.3", "r1.3", "s3", "ys3", "a0.1", "r0.1", "go2",
+    "gn2", "gx2.0", "a1.2", "r1.2", "gx2.1", "a2.3", "r2.3", "a0.0", "fs0", "gn3", "gx3.0", "go3", "gx3.1",
+    "a1.1", "r1.1", "a3.3", "r3.3", "a2.2", "r2.2", "a1.0", "fs1", "a3.2", "r3.2", "a2.1", "r2.1", "a3.1",
+    "r3.1", "a2.0", "fs2", "a3.0", "fs3",
 )
-
 
 def plain(master, momentum, routes, counts, tokens, cotangent):
     path_count = routes.shape[0]
@@ -100,7 +100,8 @@
     inv_root = model_width ** (-0.5)
     ring = paths // 2
     half = feats // 2
-    width = half // CHUNKS
+    widths = [half * part // sum(CHUNKS) for part in CHUNKS]
+    starts = [sum(widths[:j]) for j in range(len(widths))]
     pair = 2 * rows
     own_rows = ring * pair
     p = lax.axis_index("path")
@@ -122,18 +123,10 @@
         low, high = a[..., :half], a[..., half:]
         return jnp.where(first, low, high), jnp.where(first, high, low)
 
-    chosen = routes[:, 0]
-    m_own = lax.dynamic_index_in_dim(chosen, p, 0, keepdims=False)
-    m_near = lax.dynamic_index_in_dim(chosen, p ^ 1, 0, keepdims=False)
-    weight = counts.astype(f32)
-    mixing = (chosen[None, :] == jnp.arange(modules, dtype=jnp.int32)[:, None]).astype(f32) * weight[None, :]
-    mixing = mixing / jnp.sum(mixing, axis=1, keepdims=True)
-    mix_own = lax.dynamic_slice_in_dim(mixing, p, 1, 1).reshape(modules, 1, 1)
-    mix_near = lax.dynamic_slice_in_dim(mixing, p ^ 1, 1, 1).reshape(modules, 1, 1)
-
     steps = jnp.arange(ring, dtype=jnp.int32)
     owner = jnp.concatenate([((z - steps) % ring) * 2 + x, ((z - steps) % ring) * 2 + (1 - x)])
     places = jnp.concatenate([owner * 2 + (1 - y), owner * 2 + y]).astype(jnp.int32)
+    part_rows = tok_rows // TOKEN_PARTS
 
     val = {}
     last = [None]
@@ -141,7 +134,7 @@
     def after(*values):
         if last[0] is None:
             return values
-        return lax.optimization_barrier((*values, last[0]))[:-1]
+        return lax.optimization_barrier((*values, last[0]))[: len(values)]
 
     def compute(name, fn, *values):
         out = fn(*after(*values))
@@ -156,6 +149,18 @@
     def stack(*parts):
         return jnp.concatenate(parts, axis=0)
 
+    def route_values(routes, counts):
+        chosen = routes[:, 0]
+        m_own = lax.dynamic_index_in_dim(chosen, p, 0, keepdims=False)
+        m_near = lax.dynamic_index_in_dim(chosen, p ^ 1, 0, keepdims=False)
+        weight = counts.astype(f32)
+        every = jnp.arange(modules, dtype=jnp.int32)
+        mixing = (chosen[None, :] == every[:, None]).astype(f32) * weight[None, :]
+        mixing = mixing / jnp.sum(mixing, axis=1, keepdims=True)
+        mix_own = lax.dynamic_slice_in_dim(mixing, p, 1, 1).reshape(modules, 1, 1)
+        mix_near = lax.dynamic_slice_in_dim(mixing, p ^ 1, 1, 1).reshape(modules, 1, 1)
+        return m_own, m_near, mix_own, mix_near
+
     def start_weights(a):
         keep, give = mine_and_other(a)
         return keep.astype(bf16), give.astype(bf16)
@@ -164,7 +169,7 @@
         return jnp.concatenate([jnp.where(first, keep, got), jnp.where(first, got, keep)], axis=1)
 
     def block_at(j, k):
-        return val["bl"][:, :, j * width : (j + 1) * width] if k == 0 else val[f"z{j}.{k}"]
+        return val["bl"][:, :, starts[j] : starts[j] + widths[j]] if k == 0 else val[f"z{j}.{k}"]
 
     def pick(m):
         def fn(*blocks):
@@ -174,7 +179,7 @@
 
     def gathered(j):
         near = [val[f"x{j}.{g}"] for g in range(len(GATHER_GROUPS))]
-        return stack(*[pick(m_own)(block_at(j, k)) for k in range(ring)], *near)
+        return stack(*[pick(val["rt"][0])(block_at(j, k)) for k in range(ring)], *near)
 
     def far_sums(w):
         return jnp.dot(val["tf"], w, preferred_element_type=f32).astype(bf16)
@@ -184,7 +189,7 @@
             pre = jnp.dot(val["tn"], val[f"w{j}"], preferred_element_type=f32)
             pre = (pre + far.astype(f32)) * inv_root
             gate = jax.nn.sigmoid(pre)
-            cot = val["co"][:, j * width : (j + 1) * width].astype(f32)
+            cot = val["co"][:, starts[j] : starts[j] + widths[j]].astype(f32)
             return (cot * gate * (1.0 + pre * (1.0 - gate))).astype(bf16)
 
         return fn
@@ -207,6 +212,7 @@
 
     def summed(j, k):
         def fn(near, *total):
+            _, _, mix_own, mix_near = val["rt"]
             part = mix_own * val[f"go{j}"][k * pair : (k + 1) * pair].astype(f32) + mix_near * near.astype(f32)
             if total:
                 part = part + total[0].astype(f32)
@@ -228,18 +234,20 @@
             send(name, swap_core, val["wp"][1])
         elif kind == "bl":
             compute(name, full_block, val["wp"][0], val["ws"])
+        elif kind == "rt":
+            compute(name, route_values, routes, counts)
         elif kind == "cut":
             compute(name, lambda t: column_blocks(t, places, pair), tokens)
-        elif kind == "yt":
-            send(name, swap_y, val["cut"][0])
         elif kind == "ct":
             send(name, swap_core, val["cut"][1])
+        elif kind == "ya":
+            send(name, swap_y, val["cut"][0][j * part_rows : (j + 1) * part_rows])
         elif kind == "cf":
-            send(name, swap_core, val["yt"])
+            send(name, swap_core, val[f"ya{j}"])
         elif kind == "tn":
             compute(name, stack, val["cut"][1], val["ct"])
         elif kind == "tf":
-            compute(name, stack, val["yt"], val["cf"])
+            compute(name, stack, *[val[f"{way}{i}"] for way in ("ya", "cf") for i in range(TOKEN_PARTS)])
         elif kind == "tk":
             compute(name, stack, val["tn"], val["tf"])
         elif kind == "cp":
@@ -251,7 +259,7 @@
         elif kind == "z":
             send(name, ahead, block_at(j, k - 1))
         elif kind == "x":
-            compute(name, pick(m_near), *[block_at(j, i) for i in GATHER_GROUPS[k]])
+            compute(name, pick(val["rt"][1]), *[block_at(j, i) for i in GATHER_GROUPS[k]])
             send(name, swap_x, val[name])
         elif kind == "w":
             val[name] = gathered(j)
@@ -279,8 +287,8 @@
 
     for name in ORDER:
         task(name)
-    kept = jnp.concatenate([val[f"a{j}.0"][1] for j in range(CHUNKS)], axis=2)
-    came = jnp.concatenate([val[f"fs{j}"] for j in range(CHUNKS)], axis=2)
+    kept = jnp.concatenate([val[f"a{j}.0"][1] for j in range(len(widths))], axis=2)
+    came = jnp.concatenate([val[f"fs{j}"] for j in range(len(widths))], axis=2)
     outer_grad = jnp.concatenate(
         [jnp.where(first, kept, came), jnp.where(first, came, kept)], axis=2
     )

time: 206 us -> 197 us (0.956)
  starting transfers between devices: 76.4 us -> 62.7 us
  local copies, waits for them, and re-layouts: 4.81 us -> 13.7 us
  waiting for transfers between devices: 83.6 us -> 80.9 us
    ppermute x57, starting transfers between devices: 76.4 us -> 62.7 us  [over(): return lambda a: lax.ppermute(a, axis, pairs)]
    unnamed x43, local copies, waits for them, and re-layouts: 1.34 us -> 7.28 us
    ppermute x57, waiting for transfers between devices: 83.6 us -> 80.9 us  [over(): return lambda a: lax.ppermute(a, axis, pairs)]
  transfers between devices with their start and end apart: 57 -> 57, of which waited for: 24 -> 27; matrix products, arithmetic and copies ran while one was open for 12% -> 18% of each run, Pallas kernels for 2% -> 3%
where the time goes in v3:
time: 197 us
  waiting for transfers between devices  80.9 us (41%)
  starting transfers between devices  62.7 us (32%)
  matrix products  17.3 us (9%)
  local copies, waits for them, and re-layouts  13.7 us (7%)
  other arithmetic  11.6 us (6%)
  between operations  5.48 us (3%)
  Pallas kernels  4.96 us (3%)
    ppermute x57, waiting for transfers between devices, over(): return lambda a: lax.ppermute(a, axis, pairs)  80.9 us
    ppermute x57, starting transfers between devices, over(): return lambda a: lax.ppermute(a, axis, pairs)  62.7 us
    dot_general x8, matrix products, fn(): lax.dot_general(val['tk'][:, lo:lo + own_rows], sig, (((0,), (0,)), ((),...  8.42 us
    unnamed x43, local copies, waits for them, and re-layouts  7.28 us
    pallas_call x1, Pallas kernels, column_blocks(): pl.pallas_call(body, out_shape=(shape, shape), grid_spec=pltpu.PrefetchSc...  4.96 us
    dot_general x4, matrix products, fn(): pre = jnp.dot(val['tn'], val[f'w{j}'], preferred_element_type=f32)  4.89 us
    dot_general x4, matrix products, far_sums(): return jnp.dot(val['tf'], w, preferred_element_type=f32).astype(bf16)  3.98 us
  transfers between devices with their start and end apart: 57, of which 27 were waited for; matrix products, arithmetic and copies ran while one was open for 18% of the time, Pallas kernels for 3%

profile of v3, /device:TPU:0, one launch (start us, length us, event | category | flops | bytes accessed | tf_op | source)
XLA Modules:
  0.0 196.6 jit_solution(18181533290036457970)
XLA Ops:
  0.6 1.7 select_convert_fusion.1
  3.6 5.0 %shard_map.77 = (bf16[384,2048]{1,0:T(8,128)(2,1)}, bf16[384,2048]{1,0:T(8,128)(2,1)}) custom-call(s32[16]{0:T(128)} %pad_add_fusion.places_ref, bf16[384,4096]{1,0:T(8,128)(2,1)} %src), custom_call_target="tpu_custom_call" | custom-call | tf_op jit(solution)/shard_map/pallas_call | solution.py:83
  8.8 3.0 %collective-permute-start.4 = (bf16[384,2048]{1,0:T(8,128)(2,1)}, bf16[384,2048]{1,0:T(8,128)(2,1)S(1)}, u32[]{:S(2)}, u32[]{:S(2)}) collective-permute-start(bf16[384,2048]{1,0:T(8,128)(2,1)} %get-tuple-element.113), channel_id=1, source_target_pairs={{0,2},{1,3},{2,0},{3,1},{4,6},{5,7},{6,4},{7,5},{8,10},{9,11},{10,... | collective-permute-start | bytes 4718600 | tf_op jit(solution)/shard_map/ppermute | solution.py:114
  11.8 1.6 collective-permute-start.3
  13.4 1.6 collective-permute-start.2
  15.0 2.3 %broadcast_select_fusion.1 = (bf16[384,1024]{1,0:T(8,128)(2,1)S(1)}, bf16[384,1024]{1,0:T(8,128)(2,1)}) fusion(pred[]{:T(512)S(6)} %eq.24, bf16[384,2048]{1,0:T(8,128)(2,1)} %param.11), kind=kLoop, calls=%fused_computation.80 | loop fusion | flops 786432 | bytes 3145729 | tf_op jit(solution)/shard_map/jit(_where)/select_n | solution.py:124
  29.0 1.6 constant_dynamic-update-slice_fusion
  33.4 2.7 %collective-permute-done.8 = bf16[2,256,256]{2,1,0:T(8,128)(2,1)S(1)} collective-permute-done((bf16[2,256,256]{2,1,0:T(8,128)(2,1)}, bf16[2,256,256]{2,1,0:T(8,128)(2,1)S(1)}, u32[]{:S(2)}, u32[]{:S(2)}) %collective-permute-start.8) | collective-permute-done | bytes 262176 | tf_op jit(solution)/shard_map/ppermute | solution.py:114
  37.1 4.6 %collective-permute-done.7 = bf16[2,256,256]{2,1,0:T(8,128)(2,1)S(1)} collective-permute-done((bf16[2,256,256]{2,1,0:T(8,128)(2,1)}, bf16[2,256,256]{2,1,0:T(8,128)(2,1)S(1)}, u32[]{:S(2)}, u32[]{:S(2)}) %collective-permute-start.7) | collective-permute-done | bytes 262176 | tf_op jit(solution)/shard_map/ppermute | solution.py:114
  42.7 4.2 %collective-permute-done.6 = bf16[2,256,256]{2,1,0:T(8,128)(2,1)S(1)} collective-permute-done((bf16[2,256,256]{2,1,0:T(8,128)(2,1)S(1)}, bf16[2,256,256]{2,1,0:T(8,128)(2,1)S(1)}, u32[]{:S(2)}, u32[]{:S(2)}) %collective-permute-start.6) | collective-permute-done | bytes 262176 | tf_op jit(solution)/shard_map/ppermute | solution.py:114
  47.9 1.6 collective-permute-start.10
  54.1 4.7 %collective-permute-done.10 = bf16[2,256,256]{2,1,0:T(8,128)(2,1)S(1)} collective-permute-done((bf16[2,256,256]{2,1,0:T(8,128)(2,1)S(1)}, bf16[2,256,256]{2,1,0:T(8,128)(2,1)S(1)}, u32[]{:S(2)}, u32[]{:S(2)}) %collective-permute-start.10) | collective-permute-done | bytes 262176 | tf_op jit(solution)/shard_map/ppermute | solution.py:114
  58.9 5.5 %collective-permute-done.15 = bf16[2,256,256]{2,1,0:T(8,128)(2,1)S(1)} collective-permute-done((bf16[2,256,256]{2,1,0:T(8,128)(2,1)S(1)}, bf16[2,256,256]{2,1,0:T(8,128)(2,1)S(1)}, u32[]{:S(2)}, u32[]{:S(2)}) %collective-permute-start.15) | collective-permute-done | bytes 262176 | tf_op jit(solution)/shard_map/ppermute | solution.py:114
  66.0 6.9 %collective-permute-done.12 = bf16[256,256]{1,0:T(8,128)(2,1)S(1)} collective-permute-done((bf16[256,256]{1,0:T(8,128)(2,1)S(1)}, bf16[256,256]{1,0:T(8,128)(2,1)S(1)}, u32[]{:S(2)}, u32[]{:S(2)}) %collective-permute-start.12) | collective-permute-done | bytes 131104 | tf_op jit(solution)/shard_map/ppermute | solution.py:114
  73.0 2.3 %collective-permute-done.18 = bf16[2,256,256]{2,1,0:T(8,128)(2,1)S(1)} collective-permute-done((bf16[2,256,256]{2,1,0:T(8,128)(2,1)S(1)}, bf16[2,256,256]{2,1,0:T(8,128)(2,1)S(1)}, u32[]{:S(2)}, u32[]{:S(2)}) %collective-permute-start.18) | collective-permute-done | bytes 262176 | tf_op jit(solution)/shard_map/ppermute | solution.py:114
  77.5 1.6 collective-permute-start.13
  81.3 4.1 %collective-permute-done.17 = bf16[256,256]{1,0:T(8,128)(2,1)S(1)} collective-permute-done((bf16[256,256]{1,0:T(8,128)(2,1)S(1)}, bf16[256,256]{1,0:T(8,128)(2,1)S(1)}, u32[]{:S(2)}, u32[]{:S(2)}) %collective-permute-start.17) | collective-permute-done | bytes 131104 | tf_op jit(solution)/shard_map/ppermute | solution.py:114
  87.0 4.7 %collective-permute-done.21 = bf16[2,256,256]{2,1,0:T(8,128)(2,1)S(1)} collective-permute-done((bf16[2,256,256]{2,1,0:T(8,128)(2,1)S(1)}, bf16[2,256,256]{2,1,0:T(8,128)(2,1)S(1)}, u32[]{:S(2)}, u32[]{:S(2)}) %collective-permute-start.21) | collective-permute-done | bytes 262176 | tf_op jit(solution)/shard_map/ppermute | solution.py:114
  93.1 1.7 collective-permute-start.23
  95.4 3.2 %collective-permute-done.24 = bf16[768,256]{1,0:T(8,128)(2,1)S(1)} collective-permute-done((bf16[768,256]{1,0:T(8,128)(2,1)S(1)}, bf16[768,256]{1,0:T(8,128)(2,1)S(1)}, u32[]{:S(2)}, u32[]{:S(2)}) %collective-permute-start.24) | collective-permute-done | bytes 393248 | tf_op jit(solution)/shard_map/ppermute | solution.py:114
  103.1 1.7 collective-permute-start.31
  104.8 2.2 %collective-permute-done.19 = bf16[768,256]{1,0:T(8,128)(2,1)S(1)} collective-permute-done((bf16[768,256]{1,0:T(8,128)(2,1)S(1)}, bf16[768,256]{1,0:T(8,128)(2,1)S(1)}, u32[]{:S(2)}, u32[]{:S(2)}) %collective-permute-start.19) | collective-permute-done | bytes 393248 | tf_op jit(solution)/shard_map/ppermute | solution.py:114
  109.2 1.7 collective-permute-start.27
  111.5 4.0 %collective-permute-done.28 = bf16[768,256]{1,0:T(8,128)(2,1)S(1)} collective-permute-done((bf16[768,256]{1,0:T(8,128)(2,1)S(1)}, bf16[768,256]{1,0:T(8,128)(2,1)S(1)}, u32[]{:S(2)}, u32[]{:S(2)}) %collective-permute-start.28) | collective-permute-done | bytes 393248 | tf_op jit(solution)/shard_map/ppermute | solution.py:114
  115.4 1.6 collective-permute-start.26
  119.9 1.7 collective-permute-start.39
  121.6 1.8 collective-permute-start.29
  126.6 1.6 collective-permute-done.26
  128.3 2.0 %collective-permute-done.29 = bf16[2,256,256]{2,1,0:T(8,128)(2,1)S(1)} collective-permute-done((bf16[2,256,256]{2,1,0:T(8,128)(2,1)S(1)}, bf16[2,256,256]{2,1,0:T(8,128)(2,1)S(1)}, u32[]{:S(2)}, u32[]{:S(2)}) %collective-permute-start.29) | collective-permute-done | bytes 262176 | tf_op jit(solution)/shard_map/ppermute | solution.py:114
  130.4 2.2 %collective-permute-start.33 = (bf16[2,256,256]{2,1,0:T(8,128)(2,1)S(1)}, bf16[2,256,256]{2,1,0:T(8,128)(2,1)S(1)}, u32[]{:S(2)}, u32[]{:S(2)}) collective-permute-start(bf16[2,256,256]{2,1,0:T(8,128)(2,1)S(1)} %add_convert_fusion.10), channel_id=1, source_target_pairs={{0,24},{4,28},{8,0},{12,4},{16,8},{20,12},{24,16},{28,20},{1,25},{... | collective-permute-start | bytes 786440 | tf_op jit(solution)/shard_map/ppermute | solution.py:114
  132.8 1.9 collective-permute-start.40
  134.7 1.9 collective-permute-done.34
  139.0 2.3 %collective-permute-start.36 = (bf16[2,256,256]{2,1,0:T(8,128)(2,1)S(1)}, bf16[2,256,256]{2,1,0:T(8,128)(2,1)S(1)}, u32[]{:S(2)}, u32[]{:S(2)}) collective-permute-start(bf16[2,256,256]{2,1,0:T(8,128)(2,1)S(1)} %add_convert_fusion.8), channel_id=1, source_target_pairs={{0,24},{4,28},{8,0},{12,4},{16,8},{20,12},{24,16},{28,20},{1,25},{... | collective-permute-start | bytes 786440 | tf_op jit(solution)/shard_map/ppermute | solution.py:114
  141.3 2.5 %collective-permute-done.37 = bf16[768,256]{1,0:T(8,128)(2,1)S(1)} collective-permute-done((bf16[768,256]{1,0:T(8,128)(2,1)S(1)}, bf16[768,256]{1,0:T(8,128)(2,1)S(1)}, u32[]{:S(2)}, u32[]{:S(2)}) %collective-permute-start.37) | collective-permute-done | bytes 393248 | tf_op jit(solution)/shard_map/ppermute | solution.py:114
  147.6 1.9 collective-permute-start.41
  150.2 2.1 %collective-permute-done.38 = bf16[256,256]{1,0:T(8,128)(2,1)S(1)} collective-permute-done((bf16[256,256]{1,0:T(8,128)(2,1)S(1)}, bf16[256,256]{1,0:T(8,128)(2,1)S(1)}, u32[]{:S(2)}, u32[]{:S(2)}) %collective-permute-start.38) | collective-permute-done | bytes 131104 | tf_op jit(solution)/shard_map/ppermute | solution.py:114
  155.1 1.9 collective-permute-start.46
  159.4 2.2 %collective-permute-done.46 = bf16[256,256]{1,0:T(8,128)(2,1)S(1)} collective-permute-done((bf16[256,256]{1,0:T(8,128)(2,1)S(1)}, bf16[256,256]{1,0:T(8,128)(2,1)S(1)}, u32[]{:S(2)}, u32[]{:S(2)}) %collective-permute-start.46) | collective-permute-done | bytes 131104 | tf_op jit(solution)/shard_map/ppermute | solution.py:114
  161.8 1.6 collective-permute-start.49
  165.1 2.7 %collective-permute-done.43 = bf16[2,256,256]{2,1,0:T(8,128)(2,1)S(1)} collective-permute-done((bf16[2,256,256]{2,1,0:T(8,128)(2,1)S(1)}, bf16[2,256,256]{2,1,0:T(8,128)(2,1)S(1)}, u32[]{:S(2)}, u32[]{:S(2)}) %collective-permute-start.43) | collective-permute-done | bytes 262176 | tf_op jit(solution)/shard_map/ppermute | solution.py:114
  168.1 5.3 %collective-permute-done.49 = bf16[2,256,256]{2,1,0:T(8,128)(2,1)S(1)} collective-permute-done((bf16[2,256,256]{2,1,0:T(8,128)(2,1)S(1)}, bf16[2,256,256]{2,1,0:T(8,128)(2,1)S(1)}, u32[]{:S(2)}, u32[]{:S(2)}) %collective-permute-start.49) | collective-permute-done | bytes 262176 | tf_op jit(solution)/shard_map/ppermute | solution.py:114
  173.6 2.7 %collective-permute-start.51 = (bf16[2,256,256]{2,1,0:T(8,128)(2,1)S(1)}, bf16[2,256,256]{2,1,0:T(8,128)(2,1)S(1)}, u32[]{:S(2)}, u32[]{:S(2)}) collective-permute-start(bf16[2,256,256]{2,1,0:T(8,128)(2,1)S(1)} %add_convert_fusion.2), channel_id=1, source_target_pairs={{0,24},{4,28},{8,0},{12,4},{16,8},{20,12},{24,16},{28,20},{1,25},{... | collective-permute-start | bytes 786440 | tf_op jit(solution)/shard_map/ppermute | solution.py:114
  176.3 2.7 %collective-permute-done.47 = bf16[2,256,256]{2,1,0:T(8,128)(2,1)S(1)} collective-permute-done((bf16[2,256,256]{2,1,0:T(8,128)(2,1)S(1)}, bf16[2,256,256]{2,1,0:T(8,128)(2,1)S(1)}, u32[]{:S(2)}, u32[]{:S(2)}) %collective-permute-start.47) | collective-permute-done | bytes 262176 | tf_op jit(solution)/shard_map/ppermute | solution.py:114
  179.3 2.7 %collective-permute-start.50 = (bf16[2,256,256]{2,1,0:T(8,128)(2,1)S(1)}, bf16[2,256,256]{2,1,0:T(8,128)(2,1)S(1)}, u32[]{:S(2)}, u32[]{:S(2)}) collective-permute-start(bf16[2,256,256]{2,1,0:T(8,128)(2,1)S(1)} %add_convert_fusion.1), channel_id=1, source_target_pairs={{0,24},{4,28},{8,0},{12,4},{16,8},{20,12},{24,16},{28,20},{1,25},{... | collective-permute-start | bytes 786440 | tf_op jit(solution)/shard_map/ppermute | solution.py:114
  182.6 3.6 %collective-permute-start.52 = (bf16[2,256,256]{2,1,0:T(8,128)(2,1)S(1)}, bf16[2,256,256]{2,1,0:T(8,128)(2,1)S(1)}, u32[]{:S(2)}, u32[]{:S(2)}) collective-permute-start(bf16[2,256,256]{2,1,0:T(8,128)(2,1)S(1)} %add_convert_fusion), channel_id=1, source_target_pairs={{0,24},{4,28},{8,0},{12,4},{16,8},{20,12},{24,16},{28,20},{1,25},{... | collective-permute-start | bytes 786440 | tf_op jit(solution)/shard_map/ppermute | solution.py:114
  186.2 2.3 %collective-permute-done.50 = bf16[2,256,256]{2,1,0:T(8,128)(2,1)S(1)} collective-permute-done((bf16[2,256,256]{2,1,0:T(8,128)(2,1)S(1)}, bf16[2,256,256]{2,1,0:T(8,128)(2,1)S(1)}, u32[]{:S(2)}, u32[]{:S(2)}) %collective-permute-start.50) | collective-permute-done | bytes 262176 | tf_op jit(solution)/shard_map/ppermute | solution.py:114
  188.9 2.6 %collective-permute-done.52 = bf16[2,256,256]{2,1,0:T(8,128)(2,1)S(1)} collective-permute-done((bf16[2,256,256]{2,1,0:T(8,128)(2,1)S(1)}, bf16[2,256,256]{2,1,0:T(8,128)(2,1)S(1)}, u32[]{:S(2)}, u32[]{:S(2)}) %collective-permute-start.52) | collective-permute-done | bytes 262176 | tf_op jit(solution)/shard_map/ppermute | solution.py:114
  193.9 2.7 %multiply_subtract_fusion = (f32[2,128,2048]{2,1,0:T(8,128)}, f32[2,128,2048]{2,1,0:T(8,128)}) fusion(f32[2,128,2048]{2,1,0:T(8,128)S(1)} %copy-done, f32[2,128,1024]{2,1,0:T(8,128)S(1)} %get-tuple-element.215, f32[2,128,1024]{2,1,0:T(8,128)S(1)} %get-tuple-element.214, f32[2,128,2048]{2,1,0:T(8,128)S(1)} %copy-done.1), kind=kLoop, calls=%fused_computation.1 | loop fusion | flops 3670016 | bytes 10485760 | tf_op jit(solution)/shard_map/sub | solution.py:296
  (221 shorter events, 60.4 us)
Async XLA Ops:
  8.7 18.7 %collective-permute-start.1 = (bf16[384,2048]{1,0:T(8,128)(2,1)}, bf16[384,2048]{1,0:T(8,128)(2,1)}, u32[]{:S(2)}, u32[]{:S(2)}) collective-permute-start(bf16[384,2048]{1,0:T(8,128)(2,1)} %get-tuple-element.123), channel_id=1, source_target_pairs={{0,1},{1,0},{2,3},{3,2},{4,5},{5,4},{6,7},{7,6},{8,9},{9,8},{10,11... | collective-permute-start | bytes 4718600 | tf_op jit(solution)/shard_map/ppermute | solution.py:114
  8.8 38.1 %collective-permute-start.4 = (bf16[384,2048]{1,0:T(8,128)(2,1)}, bf16[384,2048]{1,0:T(8,128)(2,1)S(1)}, u32[]{:S(2)}, u32[]{:S(2)}) collective-permute-start(bf16[384,2048]{1,0:T(8,128)(2,1)} %get-tuple-element.113), channel_id=1, source_target_pairs={{0,2},{1,3},{2,0},{3,1},{4,6},{5,7},{6,4},{7,5},{8,10},{9,11},{10,... | collective-permute-start | bytes 4718600 | tf_op jit(solution)/shard_map/ppermute | solution.py:114
  11.8 11.1 %collective-permute-start.3 = (bf16[2,256,256]{2,1,0:T(8,128)(2,1)S(1)}, bf16[2,256,256]{2,1,0:T(8,128)(2,1)}, u32[]{:S(2)}, u32[]{:S(2)}) collective-permute-start(bf16[2,256,256]{2,1,0:T(8,128)(2,1)S(1)} %get-tuple-element.128), channel_id=1, source_target_pairs={{0,8},{4,12},{8,16},{12,20},{16,24},{20,28},{24,0},{28,4},{1,9},{5... | collective-permute-start | bytes 786440 | tf_op jit(solution)/shard_map/ppermute | solution.py:114
  13.4 14.0 %collective-permute-start.2 = (bf16[2,256,256]{2,1,0:T(8,128)(2,1)S(1)}, bf16[2,256,256]{2,1,0:T(8,128)(2,1)}, u32[]{:S(2)}, u32[]{:S(2)}) collective-permute-start(bf16[2,256,256]{2,1,0:T(8,128)(2,1)S(1)} %get-tuple-element.133), channel_id=1, source_target_pairs={{0,8},{4,12},{8,16},{12,20},{16,24},{20,28},{24,0},{28,4},{1,9},{5... | collective-permute-start | bytes 786440 | tf_op jit(solution)/shard_map/ppermute | solution.py:114
  24.9 11.1 %collective-permute-start.8 = (bf16[2,256,256]{2,1,0:T(8,128)(2,1)}, bf16[2,256,256]{2,1,0:T(8,128)(2,1)S(1)}, u32[]{:S(2)}, u32[]{:S(2)}) collective-permute-start(bf16[2,256,256]{2,1,0:T(8,128)(2,1)} %collective-permute-done.3), channel_id=1, source_target_pairs={{0,8},{4,12},{8,16},{12,20},{16,24},{20,28},{24,0},{28,4},{1,9},{5... | collective-permute-start | bytes 786440 | tf_op jit(solution)/shard_map/ppermute | solution.py:114
  27.4 14.3 %collective-permute-start.7 = (bf16[2,256,256]{2,1,0:T(8,128)(2,1)}, bf16[2,256,256]{2,1,0:T(8,128)(2,1)S(1)}, u32[]{:S(2)}, u32[]{:S(2)}) collective-permute-start(bf16[2,256,256]{2,1,0:T(8,128)(2,1)} %collective-permute-done.2), channel_id=1, source_target_pairs={{0,8},{4,12},{8,16},{12,20},{16,24},{20,28},{24,0},{28,4},{1,9},{5... | collective-permute-start | bytes 786440 | tf_op jit(solution)/shard_map/ppermute | solution.py:114
  32.0 14.9 %collective-permute-start.6 = (bf16[2,256,256]{2,1,0:T(8,128)(2,1)S(1)}, bf16[2,256,256]{2,1,0:T(8,128)(2,1)S(1)}, u32[]{:S(2)}, u32[]{:S(2)}) collective-permute-start(bf16[2,256,256]{2,1,0:T(8,128)(2,1)S(1)} %get-tuple-element.146), channel_id=1, source_target_pairs={{0,8},{4,12},{8,16},{12,20},{16,24},{20,28},{24,0},{28,4},{1,9},{5... | collective-permute-start | bytes 786440 | tf_op jit(solution)/shard_map/ppermute | solution.py:114
  46.9 28.4 %collective-permute-start.9 = (bf16[384,2048]{1,0:T(8,128)(2,1)S(1)}, bf16[384,2048]{1,0:T(8,128)(2,1)S(1)}, u32[]{:S(2)}, u32[]{:S(2)}) collective-permute-start(bf16[384,2048]{1,0:T(8,128)(2,1)S(1)} %collective-permute-done.4), channel_id=1, source_target_pairs={{0,1},{1,0},{2,3},{3,2},{4,5},{5,4},{6,7},{7,6},{8,9},{9,8},{10,11... | collective-permute-start | bytes 4718600 | tf_op jit(solution)/shard_map/ppermute | solution.py:114
  47.9 10.9 %collective-permute-start.10 = (bf16[2,256,256]{2,1,0:T(8,128)(2,1)S(1)}, bf16[2,256,256]{2,1,0:T(8,128)(2,1)S(1)}, u32[]{:S(2)}, u32[]{:S(2)}) collective-permute-start(bf16[2,256,256]{2,1,0:T(8,128)(2,1)S(1)} %collective-permute-done.8), channel_id=1, source_target_pairs={{0,8},{4,12},{8,16},{12,20},{16,24},{20,28},{24,0},{28,4},{1,9},{5... | collective-permute-start | bytes 786440 | tf_op jit(solution)/shard_map/ppermute | solution.py:114
  50.4 15.5 %collective-permute-start.11 = (bf16[768,256]{1,0:T(8,128)(2,1)S(1)}, bf16[768,256]{1,0:T(8,128)(2,1)S(1)}, u32[]{:S(2)}, u32[]{:S(2)}) collective-permute-start(bf16[768,256]{1,0:T(8,128)(2,1)S(1)} %pad_maximum_fusion.19), channel_id=1, source_target_pairs={{0,4},{4,0},{8,12},{12,8},{16,20},{20,16},{24,28},{28,24},{1,5},{5... | collective-permute-start | bytes 1179656 | tf_op jit(solution)/shard_map/ppermute | solution.py:114
  52.0 12.4 %collective-permute-start.15 = (bf16[2,256,256]{2,1,0:T(8,128)(2,1)S(1)}, bf16[2,256,256]{2,1,0:T(8,128)(2,1)S(1)}, u32[]{:S(2)}, u32[]{:S(2)}) collective-permute-start(bf16[2,256,256]{2,1,0:T(8,128)(2,1)S(1)} %collective-permute-done.7), channel_id=1, source_target_pairs={{0,8},{4,12},{8,16},{12,20},{16,24},{20,28},{24,0},{28,4},{1,9},{5... | collective-permute-start | bytes 786440 | tf_op jit(solution)/shard_map/ppermute | solution.py:114
  53.6 19.4 %collective-permute-start.16 = (bf16[768,256]{1,0:T(8,128)(2,1)S(1)}, bf16[768,256]{1,0:T(8,128)(2,1)S(1)}, u32[]{:S(2)}, u32[]{:S(2)}) collective-permute-start(bf16[768,256]{1,0:T(8,128)(2,1)S(1)} %pad_maximum_fusion.20), channel_id=1, source_target_pairs={{0,4},{4,0},{8,12},{12,8},{16,20},{20,16},{24,28},{28,24},{1,5},{5... | collective-permute-start | bytes 1179656 | tf_op jit(solution)/shard_map/ppermute | solution.py:114
  58.8 16.5 %collective-permute-start.14 = (bf16[2,256,256]{2,1,0:T(8,128)(2,1)S(1)}, bf16[2,256,256]{2,1,0:T(8,128)(2,1)S(1)}, u32[]{:S(2)}, u32[]{:S(2)}) collective-permute-start(bf16[2,256,256]{2,1,0:T(8,128)(2,1)S(1)} %get-tuple-element.159), channel_id=1, source_target_pairs={{0,8},{4,12},{8,16},{12,20},{16,24},{20,28},{24,0},{28,4},{1,9},{5... | collective-permute-start | bytes 786440 | tf_op jit(solution)/shard_map/ppermute | solution.py:114
  64.4 8.5 %collective-permute-start.12 = (bf16[256,256]{1,0:T(8,128)(2,1)S(1)}, bf16[256,256]{1,0:T(8,128)(2,1)S(1)}, u32[]{:S(2)}, u32[]{:S(2)}) collective-permute-start(bf16[256,256]{1,0:T(8,128)(2,1)S(1)} %dynamic-slice_bitcast_fusion.9), channel_id=1, source_target_pairs={{0,4},{4,0},{8,12},{12,8},{16,20},{20,16},{24,28},{28,24},{1,5},{5... | collective-permute-start | bytes 393224 | tf_op jit(solution)/shard_map/ppermute | solution.py:114
  65.9 9.4 %collective-permute-start.18 = (bf16[2,256,256]{2,1,0:T(8,128)(2,1)S(1)}, bf16[2,256,256]{2,1,0:T(8,128)(2,1)S(1)}, u32[]{:S(2)}, u32[]{:S(2)}) collective-permute-start(bf16[2,256,256]{2,1,0:T(8,128)(2,1)S(1)} %collective-permute-done.6), channel_id=1, source_target_pairs={{0,8},{4,12},{8,16},{12,20},{16,24},{20,28},{24,0},{28,4},{1,9},{5... | collective-permute-start | bytes 786440 | tf_op jit(solution)/shard_map/ppermute | solution.py:114
  77.5 14.3 %collective-permute-start.13 = (bf16[768,256]{1,0:T(8,128)(2,1)S(1)}, bf16[768,256]{1,0:T(8,128)(2,1)S(1)}, u32[]{:S(2)}, u32[]{:S(2)}) collective-permute-start(bf16[768,256]{1,0:T(8,128)(2,1)S(1)} %convolution_convert_fusion.3), channel_id=1, source_target_pairs={{0,2},{1,3},{2,0},{3,1},{4,6},{5,7},{6,4},{7,5},{8,10},{9,11},{10,... | collective-permute-start | bytes 1179656 | tf_op jit(solution)/shard_map/ppermute | solution.py:114
  80.7 14.6 %collective-permute-start.22 = (bf16[768,256]{1,0:T(8,128)(2,1)S(1)}, bf16[768,256]{1,0:T(8,128)(2,1)S(1)}, u32[]{:S(2)}, u32[]{:S(2)}) collective-permute-start(bf16[768,256]{1,0:T(8,128)(2,1)S(1)} %pad_maximum_fusion.21), channel_id=1, source_target_pairs={{0,4},{4,0},{8,12},{12,8},{16,20},{20,16},{24,28},{28,24},{1,5},{5... | collective-permute-start | bytes 1179656 | tf_op jit(solution)/shard_map/ppermute | solution.py:114
  81.3 10.4 %collective-permute-start.21 = (bf16[2,256,256]{2,1,0:T(8,128)(2,1)S(1)}, bf16[2,256,256]{2,1,0:T(8,128)(2,1)S(1)}, u32[]{:S(2)}, u32[]{:S(2)}) collective-permute-start(bf16[2,256,256]{2,1,0:T(8,128)(2,1)S(1)} %collective-permute-done.18), channel_id=1, source_target_pairs={{0,8},{4,12},{8,16},{12,20},{16,24},{20,28},{24,0},{28,4},{1,9},{5... | collective-permute-start | bytes 786440 | tf_op jit(solution)/shard_map/ppermute | solution.py:114
  86.5 12.1 %collective-permute-start.24 = (bf16[768,256]{1,0:T(8,128)(2,1)S(1)}, bf16[768,256]{1,0:T(8,128)(2,1)S(1)}, u32[]{:S(2)}, u32[]{:S(2)}) collective-permute-start(bf16[768,256]{1,0:T(8,128)(2,1)S(1)} %convolution_convert_fusion.2), channel_id=1, source_target_pairs={{0,2},{1,3},{2,0},{3,1},{4,6},{5,7},{6,4},{7,5},{8,10},{9,11},{10,... | collective-permute-start | bytes 1179656 | tf_op jit(solution)/shard_map/ppermute | solution.py:114
  93.0 14.0 %collective-permute-start.19 = (bf16[768,256]{1,0:T(8,128)(2,1)S(1)}, bf16[768,256]{1,0:T(8,128)(2,1)S(1)}, u32[]{:S(2)}, u32[]{:S(2)}) collective-permute-start(bf16[768,256]{1,0:T(8,128)(2,1)S(1)} %multiply_convert_fusion.3), channel_id=1, source_target_pairs={{0,2},{1,3},{2,0},{3,1},{4,6},{5,7},{6,4},{7,5},{8,10},{9,11},{10,... | collective-permute-start | bytes 1179656 | tf_op jit(solution)/shard_map/ppermute | solution.py:114
  99.8 15.6 %collective-permute-start.28 = (bf16[768,256]{1,0:T(8,128)(2,1)S(1)}, bf16[768,256]{1,0:T(8,128)(2,1)S(1)}, u32[]{:S(2)}, u32[]{:S(2)}) collective-permute-start(bf16[768,256]{1,0:T(8,128)(2,1)S(1)} %multiply_convert_fusion.2), channel_id=1, source_target_pairs={{0,2},{1,3},{2,0},{3,1},{4,6},{5,7},{6,4},{7,5},{8,10},{9,11},{10,... | collective-permute-start | bytes 1179656 | tf_op jit(solution)/shard_map/ppermute | solution.py:114
  100.6 10.3 %collective-permute-start.25 = (bf16[2,256,256]{2,1,0:T(8,128)(2,1)S(1)}, bf16[2,256,256]{2,1,0:T(8,128)(2,1)S(1)}, u32[]{:S(2)}, u32[]{:S(2)}) collective-permute-start(bf16[2,256,256]{2,1,0:T(8,128)(2,1)S(1)} %collective-permute-done.20), channel_id=1, source_target_pairs={{0,8},{4,12},{8,16},{12,20},{16,24},{20,28},{24,0},{28,4},{1,9},{5... | collective-permute-start | bytes 786440 | tf_op jit(solution)/shard_map/ppermute | solution.py:114
  101.6 22.9 %collective-permute-start.30 = (bf16[768,256]{1,0:T(8,128)(2,1)S(1)}, bf16[768,256]{1,0:T(8,128)(2,1)S(1)}, u32[]{:S(2)}, u32[]{:S(2)}) collective-permute-start(bf16[768,256]{1,0:T(8,128)(2,1)S(1)} %convolution_convert_fusion.1), channel_id=1, source_target_pairs={{0,2},{1,3},{2,0},{3,1},{4,6},{5,7},{6,4},{7,5},{8,10},{9,11},{10,... | collective-permute-start | bytes 1179656 | tf_op jit(solution)/shard_map/ppermute | solution.py:114
  103.1 16.8 %collective-permute-start.31 = (bf16[768,256]{1,0:T(8,128)(2,1)S(1)}, bf16[768,256]{1,0:T(8,128)(2,1)S(1)}, u32[]{:S(2)}, u32[]{:S(2)}) collective-permute-start(bf16[768,256]{1,0:T(8,128)(2,1)S(1)} %pad_maximum_fusion.22), channel_id=1, source_target_pairs={{0,4},{4,0},{8,12},{12,8},{16,20},{20,16},{24,28},{28,24},{1,5},{5... | collective-permute-start | bytes 1179656 | tf_op jit(solution)/shard_map/ppermute | solution.py:114
  109.2 10.1 %collective-permute-start.27 = (bf16[256,256]{1,0:T(8,128)(2,1)S(1)}, bf16[256,256]{1,0:T(8,128)(2,1)S(1)}, u32[]{:S(2)}, u32[]{:S(2)}) collective-permute-start(bf16[256,256]{1,0:T(8,128)(2,1)S(1)} %slice.260), channel_id=1, source_target_pairs={{0,4},{4,0},{8,12},{12,8},{16,20},{20,16},{24,28},{28,24},{1,5},{5... | collective-permute-start | bytes 393224 | tf_op jit(solution)/shard_map/ppermute | solution.py:114
  110.9 10.7 %collective-permute-start.32 = (bf16[256,256]{1,0:T(8,128)(2,1)S(1)}, bf16[256,256]{1,0:T(8,128)(2,1)S(1)}, u32[]{:S(2)}, u32[]{:S(2)}) collective-permute-start(bf16[256,256]{1,0:T(8,128)(2,1)S(1)} %dynamic-slice_bitcast_fusion), channel_id=1, source_target_pairs={{0,4},{4,0},{8,12},{12,8},{16,20},{20,16},{24,28},{28,24},{1,5},{5... | collective-permute-start | bytes 393224 | tf_op jit(solution)/shard_map/ppermute | solution.py:114
  115.4 12.8 %collective-permute-start.26 = (bf16[768,256]{1,0:T(8,128)(2,1)S(1)}, bf16[768,256]{1,0:T(8,128)(2,1)S(1)}, u32[]{:S(2)}, u32[]{:S(2)}) collective-permute-start(bf16[768,256]{1,0:T(8,128)(2,1)S(1)} %slice.259), channel_id=1, source_target_pairs={{0,4},{4,0},{8,12},{12,8},{16,20},{20,16},{24,28},{28,24},{1,5},{5... | collective-permute-start | bytes 1179656 | tf_op jit(solution)/shard_map/ppermute | solution.py:114
  119.3 13.4 %collective-permute-start.35 = (bf16[256,256]{1,0:T(8,128)(2,1)S(1)}, bf16[256,256]{1,0:T(8,128)(2,1)S(1)}, u32[]{:S(2)}, u32[]{:S(2)}) collective-permute-start(bf16[256,256]{1,0:T(8,128)(2,1)S(1)} %slice.268), channel_id=1, source_target_pairs={{0,4},{4,0},{8,12},{12,8},{16,20},{20,16},{24,28},{28,24},{1,5},{5... | collective-permute-start | bytes 393224 | tf_op jit(solution)/shard_map/ppermute | solution.py:114
  119.9 18.9 %collective-permute-start.39 = (bf16[768,256]{1,0:T(8,128)(2,1)S(1)}, bf16[768,256]{1,0:T(8,128)(2,1)S(1)}, u32[]{:S(2)}, u32[]{:S(2)}) collective-permute-start(bf16[768,256]{1,0:T(8,128)(2,1)S(1)} %slice.267), channel_id=1, source_target_pairs={{0,4},{4,0},{8,12},{12,8},{16,20},{20,16},{24,28},{28,24},{1,5},{5... | collective-permute-start | bytes 1179656 | tf_op jit(solution)/shard_map/ppermute | solution.py:114
  121.6 8.6 %collective-permute-start.29 = (bf16[2,256,256]{2,1,0:T(8,128)(2,1)S(1)}, bf16[2,256,256]{2,1,0:T(8,128)(2,1)S(1)}, u32[]{:S(2)}, u32[]{:S(2)}) collective-permute-start(bf16[2,256,256]{2,1,0:T(8,128)(2,1)S(1)} %add_convert_fusion.11), channel_id=1, source_target_pairs={{0,24},{4,28},{8,0},{12,4},{16,8},{20,12},{24,16},{28,20},{1,25},{... | collective-permute-start | bytes 786440 | tf_op jit(solution)/shard_map/ppermute | solution.py:114
  124.5 12.1 %collective-permute-start.34 = (bf16[768,256]{1,0:T(8,128)(2,1)S(1)}, bf16[768,256]{1,0:T(8,128)(2,1)S(1)}, u32[]{:S(2)}, u32[]{:S(2)}) collective-permute-start(bf16[768,256]{1,0:T(8,128)(2,1)S(1)} %convolution_convert_fusion), channel_id=1, source_target_pairs={{0,2},{1,3},{2,0},{3,1},{4,6},{5,7},{6,4},{7,5},{8,10},{9,11},{10,... | collective-permute-start | bytes 1179656 | tf_op jit(solution)/shard_map/ppermute | solution.py:114
  128.2 15.5 %collective-permute-start.37 = (bf16[768,256]{1,0:T(8,128)(2,1)S(1)}, bf16[768,256]{1,0:T(8,128)(2,1)S(1)}, u32[]{:S(2)}, u32[]{:S(2)}) collective-permute-start(bf16[768,256]{1,0:T(8,128)(2,1)S(1)} %multiply_convert_fusion.1), channel_id=1, source_target_pairs={{0,2},{1,3},{2,0},{3,1},{4,6},{5,7},{6,4},{7,5},{8,10},{9,11},{10,... | collective-permute-start | bytes 1179656 | tf_op jit(solution)/shard_map/ppermute | solution.py:114
  130.4 8.4 %collective-permute-start.33 = (bf16[2,256,256]{2,1,0:T(8,128)(2,1)S(1)}, bf16[2,256,256]{2,1,0:T(8,128)(2,1)S(1)}, u32[]{:S(2)}, u32[]{:S(2)}) collective-permute-start(bf16[2,256,256]{2,1,0:T(8,128)(2,1)S(1)} %add_convert_fusion.10), channel_id=1, source_target_pairs={{0,24},{4,28},{8,0},{12,4},{16,8},{20,12},{24,16},{28,20},{1,25},{... | collective-permute-start | bytes 786440 | tf_op jit(solution)/shard_map/ppermute | solution.py:114
  132.8 14.5 %collective-permute-start.40 = (bf16[2,256,256]{2,1,0:T(8,128)(2,1)S(1)}, bf16[2,256,256]{2,1,0:T(8,128)(2,1)S(1)}, u32[]{:S(2)}, u32[]{:S(2)}) collective-permute-start(bf16[2,256,256]{2,1,0:T(8,128)(2,1)S(1)} %add_convert_fusion.9), channel_id=1, source_target_pairs={{0,24},{4,28},{8,0},{12,4},{16,8},{20,12},{24,16},{28,20},{1,25},{... | collective-permute-start | bytes 786440 | tf_op jit(solution)/shard_map/ppermute | solution.py:114
  137.9 16.1 %collective-permute-start.42 = (bf16[768,256]{1,0:T(8,128)(2,1)S(1)}, bf16[768,256]{1,0:T(8,128)(2,1)S(1)}, u32[]{:S(2)}, u32[]{:S(2)}) collective-permute-start(bf16[768,256]{1,0:T(8,128)(2,1)S(1)} %multiply_convert_fusion), channel_id=1, source_target_pairs={{0,2},{1,3},{2,0},{3,1},{4,6},{5,7},{6,4},{7,5},{8,10},{9,11},{10,... | collective-permute-start | bytes 1179656 | tf_op jit(solution)/shard_map/ppermute | solution.py:114
  139.0 14.8 %collective-permute-start.36 = (bf16[2,256,256]{2,1,0:T(8,128)(2,1)S(1)}, bf16[2,256,256]{2,1,0:T(8,128)(2,1)S(1)}, u32[]{:S(2)}, u32[]{:S(2)}) collective-permute-start(bf16[2,256,256]{2,1,0:T(8,128)(2,1)S(1)} %add_convert_fusion.8), channel_id=1, source_target_pairs={{0,24},{4,28},{8,0},{12,4},{16,8},{20,12},{24,16},{28,20},{1,25},{... | collective-permute-start | bytes 786440 | tf_op jit(solution)/shard_map/ppermute | solution.py:114
  147.6 10.7 %collective-permute-start.41 = (bf16[2,256,256]{2,1,0:T(8,128)(2,1)S(1)}, bf16[2,256,256]{2,1,0:T(8,128)(2,1)S(1)}, u32[]{:S(2)}, u32[]{:S(2)}) collective-permute-start(bf16[2,256,256]{2,1,0:T(8,128)(2,1)S(1)} %add_convert_fusion.7), channel_id=1, source_target_pairs={{0,24},{4,28},{8,0},{12,4},{16,8},{20,12},{24,16},{28,20},{1,25},{... | collective-permute-start | bytes 786440 | tf_op jit(solution)/shard_map/ppermute | solution.py:114
  149.5 14.0 %collective-permute-start.44 = (bf16[768,256]{1,0:T(8,128)(2,1)S(1)}, bf16[768,256]{1,0:T(8,128)(2,1)S(1)}, u32[]{:S(2)}, u32[]{:S(2)}) collective-permute-start(bf16[768,256]{1,0:T(8,128)(2,1)S(1)} %slice.274), channel_id=1, source_target_pairs={{0,4},{4,0},{8,12},{12,8},{16,20},{20,16},{24,28},{28,24},{1,5},{5... | collective-permute-start | bytes 1179656 | tf_op jit(solution)/shard_map/ppermute | solution.py:114
  152.5 11.0 %collective-permute-start.45 = (bf16[2,256,256]{2,1,0:T(8,128)(2,1)S(1)}, bf16[2,256,256]{2,1,0:T(8,128)(2,1)S(1)}, u32[]{:S(2)}, u32[]{:S(2)}) collective-permute-start(bf16[2,256,256]{2,1,0:T(8,128)(2,1)S(1)} %add_convert_fusion.6), channel_id=1, source_target_pairs={{0,24},{4,28},{8,0},{12,4},{16,8},{20,12},{24,16},{28,20},{1,25},{... | collective-permute-start | bytes 786440 | tf_op jit(solution)/shard_map/ppermute | solution.py:114
  158.1 9.9 %collective-permute-start.48 = (bf16[768,256]{1,0:T(8,128)(2,1)S(1)}, bf16[768,256]{1,0:T(8,128)(2,1)S(1)}, u32[]{:S(2)}, u32[]{:S(2)}) collective-permute-start(bf16[768,256]{1,0:T(8,128)(2,1)S(1)} %slice.283), channel_id=1, source_target_pairs={{0,4},{4,0},{8,12},{12,8},{16,20},{20,16},{24,28},{28,24},{1,5},{5... | collective-permute-start | bytes 1179656 | tf_op jit(solution)/shard_map/ppermute | solution.py:114
  158.5 9.3 %collective-permute-start.43 = (bf16[2,256,256]{2,1,0:T(8,128)(2,1)S(1)}, bf16[2,256,256]{2,1,0:T(8,128)(2,1)S(1)}, u32[]{:S(2)}, u32[]{:S(2)}) collective-permute-start(bf16[2,256,256]{2,1,0:T(8,128)(2,1)S(1)} %add_convert_fusion.5), channel_id=1, source_target_pairs={{0,24},{4,28},{8,0},{12,4},{16,8},{20,12},{24,16},{28,20},{1,25},{... | collective-permute-start | bytes 786440 | tf_op jit(solution)/shard_map/ppermute | solution.py:114
  161.8 11.6 %collective-permute-start.49 = (bf16[2,256,256]{2,1,0:T(8,128)(2,1)S(1)}, bf16[2,256,256]{2,1,0:T(8,128)(2,1)S(1)}, u32[]{:S(2)}, u32[]{:S(2)}) collective-permute-start(bf16[2,256,256]{2,1,0:T(8,128)(2,1)S(1)} %add_convert_fusion.4), channel_id=1, source_target_pairs={{0,24},{4,28},{8,0},{12,4},{16,8},{20,12},{24,16},{28,20},{1,25},{... | collective-permute-start | bytes 786440 | tf_op jit(solution)/shard_map/ppermute | solution.py:114
  163.7 15.4 %collective-permute-start.47 = (bf16[2,256,256]{2,1,0:T(8,128)(2,1)S(1)}, bf16[2,256,256]{2,1,0:T(8,128)(2,1)S(1)}, u32[]{:S(2)}, u32[]{:S(2)}) collective-permute-start(bf16[2,256,256]{2,1,0:T(8,128)(2,1)S(1)} %add_convert_fusion.3), channel_id=1, source_target_pairs={{0,24},{4,28},{8,0},{12,4},{16,8},{20,12},{24,16},{28,20},{1,25},{... | collective-permute-start | bytes 786440 | tf_op jit(solution)/shard_map/ppermute | solution.py:114
  173.6 8.8 %collective-permute-start.51 = (bf16[2,256,256]{2,1,0:T(8,128)(2,1)S(1)}, bf16[2,256,256]{2,1,0:T(8,128)(2,1)S(1)}, u32[]{:S(2)}, u32[]{:S(2)}) collective-permute-start(bf16[2,256,256]{2,1,0:T(8,128)(2,1)S(1)} %add_convert_fusion.2), channel_id=1, source_target_pairs={{0,24},{4,28},{8,0},{12,4},{16,8},{20,12},{24,16},{28,20},{1,25},{... | collective-permute-start | bytes 786440 | tf_op jit(solution)/shard_map/ppermute | solution.py:114
  179.3 9.3 %collective-permute-start.50 = (bf16[2,256,256]{2,1,0:T(8,128)(2,1)S(1)}, bf16[2,256,256]{2,1,0:T(8,128)(2,1)S(1)}, u32[]{:S(2)}, u32[]{:S(2)}) collective-permute-start(bf16[2,256,256]{2,1,0:T(8,128)(2,1)S(1)} %add_convert_fusion.1), channel_id=1, source_target_pairs={{0,24},{4,28},{8,0},{12,4},{16,8},{20,12},{24,16},{28,20},{1,25},{... | collective-permute-start | bytes 786440 | tf_op jit(solution)/shard_map/ppermute | solution.py:114
  181.9 9.9 %collective-permute-start.53 = (f32[2,128,256]{2,1,0:T(8,128)S(1)}, f32[2,128,256]{2,1,0:T(8,128)S(1)}, u32[]{:S(2)}, u32[]{:S(2)}) collective-permute-start(f32[2,128,256]{2,1,0:T(8,128)S(1)} %get-tuple-element.227), channel_id=1, source_target_pairs={{0,1},{1,0},{2,3},{3,2},{4,5},{5,4},{6,7},{7,6},{8,9},{9,8},{10,11... | collective-permute-start | bytes 786440 | tf_op jit(solution)/shard_map/ppermute | solution.py:114
  181.9 9.9 %collective-permute-start.54 = (f32[2,128,256]{2,1,0:T(8,128)S(1)}, f32[2,128,256]{2,1,0:T(8,128)S(1)}, u32[]{:S(2)}, u32[]{:S(2)}) collective-permute-start(f32[2,128,256]{2,1,0:T(8,128)S(1)} %get-tuple-element.229), channel_id=1, source_target_pairs={{0,1},{1,0},{2,3},{3,2},{4,5},{5,4},{6,7},{7,6},{8,9},{9,8},{10,11... | collective-permute-start | bytes 786440 | tf_op jit(solution)/shard_map/ppermute | solution.py:114
  182.6 8.8 %collective-permute-start.52 = (bf16[2,256,256]{2,1,0:T(8,128)(2,1)S(1)}, bf16[2,256,256]{2,1,0:T(8,128)(2,1)S(1)}, u32[]{:S(2)}, u32[]{:S(2)}) collective-permute-start(bf16[2,256,256]{2,1,0:T(8,128)(2,1)S(1)} %add_convert_fusion), channel_id=1, source_target_pairs={{0,24},{4,28},{8,0},{12,4},{16,8},{20,12},{24,16},{28,20},{1,25},{... | collective-permute-start | bytes 786440 | tf_op jit(solution)/shard_map/ppermute | solution.py:114
  (17 other events, 180.8 us)

commit v4 on v3

--- a/solution.py
+++ b/solution.py
@@ -10,14 +10,14 @@
 SCATTER_GROUPS = ((3,), (0, 1, 2))
 TOKEN_PARTS = 1
 ORDER = (
-    "wp", "ws", "cut", "bl", "ya0", "z0.1", "ct", "z1.1", "cp", "rt", "z0.2", "cc", "z1.2", "tn", "co",
+    "wp", "ws", "cut", "ct", "bl", "ya0", "z0.1", "z1.1", "cp", "rt", "z0.2", "cc", "z1.2", "tn", "co",
     "z2.1", "x0.0", "z0.3", "z1.3", "x1.0", "z2.2", "z3.1", "cf0", "x0.1", "tf", "tk", "w0", "p0", "yp0",
-    "x1.1", "x2.0", "z2.3", "w1", "p1", "yp1", "z3.2", "s0", "ys0", "x2.1", "s1", "ys1", "z3.3", "w2", "p2",
-    "yp2", "x3.0", "gn0", "go0", "gx0.0", "x3.1", "gx0.1", "gn1", "gx1.0", "gx1.1", "go1", "a0.3", "r0.3",
-    "w3", "p3", "yp3", "s2", "ys2", "a0.2", "r0.2", "a1.3", "r1.3", "s3", "ys3", "a0.1", "r0.1", "go2",
-    "gn2", "gx2.0", "a1.2", "r1.2", "gx2.1", "a2.3", "r2.3", "a0.0", "fs0", "gn3", "gx3.0", "go3", "gx3.1",
-    "a1.1", "r1.1", "a3.3", "r3.3", "a2.2", "r2.2", "a1.0", "fs1", "a3.2", "r3.2", "a2.1", "r2.1", "a3.1",
-    "r3.1", "a2.0", "fs2", "a3.0", "fs3",
+    "x1.1", "x2.0", "z2.3", "w1", "p1", "yp1", "z3.2", "s0", "ys0", "x3.0", "x2.1", "s1", "ys1", "z3.3",
+    "w2", "p2", "yp2", "gn0", "go0", "gx0.0", "x3.1", "gx0.1", "gn1", "gx1.0", "gx1.1", "go1", "a0.3",
+    "r0.3", "w3", "p3", "yp3", "s2", "ys2", "a0.2", "r0.2", "a1.3", "r1.3", "s3", "ys3", "a0.1", "r0.1",
+    "go2", "gn2", "gx2.0", "a1.2", "r1.2", "gx2.1", "a2.3", "r2.3", "a0.0", "fs0", "gn3", "gx3.0", "go3",
+    "gx3.1", "a1.1", "r1.1", "a3.3", "r3.3", "a2.2", "r2.2", "a1.0", "fs1", "a3.2", "r3.2", "a2.1", "r2.1",
+    "a3.1", "r3.1", "a2.0", "fs2", "a3.0", "fs3", "d:r3.3",
 )
 
 def plain(master, momentum, routes, counts, tokens, cotangent):
@@ -130,11 +130,14 @@
 
     val = {}
     last = [None]
+    arrived = []
 
     def after(*values):
         if last[0] is None:
             return values
-        return lax.optimization_barrier((*values, last[0]))[: len(values)]
+        held = lax.optimization_barrier((*values, last[0], *arrived))[: len(values)]
+        arrived.clear()
+        return held
 
     def compute(name, fn, *values):
         out = fn(*after(*values))
@@ -286,7 +289,10 @@
             send(name, swap_core, val[f"a{j}.0"][0])
 
     for name in ORDER:
-        task(name)
+        if name.startswith("d:"):
+            arrived.append(val[name[2:]])
+        else:
+            task(name)
     kept = jnp.concatenate([val[f"a{j}.0"][1] for j in range(len(widths))], axis=2)
     came = jnp.concatenate([val[f"fs{j}"] for j in range(len(widths))], axis=2)
     outer_grad = jnp.concatenate(

time: 197 us -> 196 us (level)
  starting transfers between devices: 62.7 us -> 52.9 us
  waiting for transfers between devices: 80.9 us -> 90.5 us
    ppermute x57, starting transfers between devices: 62.7 us -> 52.9 us  [over(): return lambda a: lax.ppermute(a, axis, pairs)]
    ppermute x57, waiting for transfers between devices: 80.9 us -> 90.5 us  [over(): return lambda a: lax.ppermute(a, axis, pairs)]
    unnamed x43 -> x45, local copies, waits for them, and re-layouts: 7.28 us -> 7.23 us
  transfers between devices with their start and end apart: 57 -> 57, of which waited for: 27 -> 28; matrix products, arithmetic and copies ran while one was open for 18% -> 17% of each run, Pallas kernels for 3% -> 3%
where the time goes in v4:
time: 196 us; the launch traced here: 195 us
  waiting for transfers between devices  90.5 us (46%)
  starting transfers between devices  52.9 us (27%)
  matrix products  17.2 us (9%)
  local copies, waits for them, and re-layouts  13.7 us (7%)
  other arithmetic  10.1 us (5%)
  between operations  5.82 us (3%)
  Pallas kernels  4.96 us (3%)
    ppermute x57, waiting for transfers between devices, over(): return lambda a: lax.ppermute(a, axis, pairs)  90.5 us
    ppermute x57, starting transfers between devices, over(): return lambda a: lax.ppermute(a, axis, pairs)  52.9 us
    dot_general x8, matrix products, fn(): lax.dot_general(val['tk'][:, lo:lo + own_rows], sig, (((0,), (0,)), ((),...  8.47 us
    unnamed x45, local copies, waits for them, and re-layouts  7.23 us
    pallas_call x1, Pallas kernels, column_blocks(): pl.pallas_call(body, out_shape=(shape, shape), grid_spec=pltpu.PrefetchSc...  4.96 us
    dot_general x4, matrix products, fn(): pre = jnp.dot(val['tn'], val[f'w{j}'], preferred_element_type=f32)  4.85 us
    dot_general x4, matrix products, far_sums(): return jnp.dot(val['tf'], w, preferred_element_type=f32).astype(bf16)  3.93 us
  transfers between devices with their start and end apart: 57, of which 28 were waited for; matrix products, arithmetic and copies ran while one was open for 17% of the time, Pallas kernels for 3%

profile of v4, /device:TPU:0, one launch (start us, length us, event | category | flops | bytes accessed | tf_op | source)
XLA Modules:
  0.0 195.3 jit_solution(13328340248569719925)
XLA Ops:
  0.6 1.7 select_convert_fusion.1
  3.5 5.0 %shard_map.77 = (bf16[384,2048]{1,0:T(8,128)(2,1)}, bf16[384,2048]{1,0:T(8,128)(2,1)}) custom-call(s32[16]{0:T(128)} %pad_add_fusion.places_ref, bf16[384,4096]{1,0:T(8,128)(2,1)} %src), custom_call_target="tpu_custom_call" | custom-call | tf_op jit(solution)/shard_map/pallas_call | solution.py:83
  8.5 3.0 %collective-permute-start.4 = (bf16[384,2048]{1,0:T(8,128)(2,1)}, bf16[384,2048]{1,0:T(8,128)(2,1)S(1)}, u32[]{:S(2)}, u32[]{:S(2)}) collective-permute-start(bf16[384,2048]{1,0:T(8,128)(2,1)} %get-tuple-element.114), channel_id=1, source_target_pairs={{0,2},{1,3},{2,0},{3,1},{4,6},{5,7},{6,4},{7,5},{8,10},{9,11},{10,... | collective-permute-start | bytes 4718600 | tf_op jit(solution)/shard_map/ppermute | solution.py:114
  11.6 1.6 collective-permute-start.3
  13.3 1.6 collective-permute-start.2
  21.2 1.6 collective-permute-done.3
  25.0 2.2 %collective-permute-done.2 = bf16[2,256,256]{2,1,0:T(8,128)(2,1)} collective-permute-done((bf16[2,256,256]{2,1,0:T(8,128)(2,1)S(1)}, bf16[2,256,256]{2,1,0:T(8,128)(2,1)}, u32[]{:S(2)}, u32[]{:S(2)}) %collective-permute-start.2) | collective-permute-done | bytes 262176 | tf_op jit(solution)/shard_map/ppermute | solution.py:114
  27.3 1.6 constant_dynamic-update-slice_fusion.1
  28.9 1.6 constant_dynamic-update-slice_fusion
  33.2 2.9 %collective-permute-done.8 = bf16[2,256,256]{2,1,0:T(8,128)(2,1)S(1)} collective-permute-done((bf16[2,256,256]{2,1,0:T(8,128)(2,1)}, bf16[2,256,256]{2,1,0:T(8,128)(2,1)S(1)}, u32[]{:S(2)}, u32[]{:S(2)}) %collective-permute-start.8) | collective-permute-done | bytes 262176 | tf_op jit(solution)/shard_map/ppermute | solution.py:114
  37.1 4.6 %collective-permute-done.7 = bf16[2,256,256]{2,1,0:T(8,128)(2,1)S(1)} collective-permute-done((bf16[2,256,256]{2,1,0:T(8,128)(2,1)}, bf16[2,256,256]{2,1,0:T(8,128)(2,1)S(1)}, u32[]{:S(2)}, u32[]{:S(2)}) %collective-permute-start.7) | collective-permute-done | bytes 262176 | tf_op jit(solution)/shard_map/ppermute | solution.py:114
  42.7 4.2 %collective-permute-done.6 = bf16[2,256,256]{2,1,0:T(8,128)(2,1)S(1)} collective-permute-done((bf16[2,256,256]{2,1,0:T(8,128)(2,1)S(1)}, bf16[2,256,256]{2,1,0:T(8,128)(2,1)S(1)}, u32[]{:S(2)}, u32[]{:S(2)}) %collective-permute-start.6) | collective-permute-done | bytes 262176 | tf_op jit(solution)/shard_map/ppermute | solution.py:114
  50.0 1.6 collective-permute-start.11
  51.6 1.6 collective-permute-start.15
  53.7 5.2 %collective-permute-done.10 = bf16[2,256,256]{2,1,0:T(8,128)(2,1)S(1)} collective-permute-done((bf16[2,256,256]{2,1,0:T(8,128)(2,1)S(1)}, bf16[2,256,256]{2,1,0:T(8,128)(2,1)S(1)}, u32[]{:S(2)}, u32[]{:S(2)}) %collective-permute-start.10) | collective-permute-done | bytes 262176 | tf_op jit(solution)/shard_map/ppermute | solution.py:114
  59.0 5.5 %collective-permute-done.15 = bf16[2,256,256]{2,1,0:T(8,128)(2,1)S(1)} collective-permute-done((bf16[2,256,256]{2,1,0:T(8,128)(2,1)S(1)}, bf16[2,256,256]{2,1,0:T(8,128)(2,1)S(1)}, u32[]{:S(2)}, u32[]{:S(2)}) %collective-permute-start.15) | collective-permute-done | bytes 262176 | tf_op jit(solution)/shard_map/ppermute | solution.py:114
  64.5 1.5 collective-permute-start.12
  66.1 6.5 %collective-permute-done.12 = bf16[256,256]{1,0:T(8,128)(2,1)S(1)} collective-permute-done((bf16[256,256]{1,0:T(8,128)(2,1)S(1)}, bf16[256,256]{1,0:T(8,128)(2,1)S(1)}, u32[]{:S(2)}, u32[]{:S(2)}) %collective-permute-start.12) | collective-permute-done | bytes 131104 | tf_op jit(solution)/shard_map/ppermute | solution.py:114
  72.6 2.7 %collective-permute-done.18 = bf16[2,256,256]{2,1,0:T(8,128)(2,1)S(1)} collective-permute-done((bf16[2,256,256]{2,1,0:T(8,128)(2,1)S(1)}, bf16[2,256,256]{2,1,0:T(8,128)(2,1)S(1)}, u32[]{:S(2)}, u32[]{:S(2)}) %collective-permute-start.18) | collective-permute-done | bytes 262176 | tf_op jit(solution)/shard_map/ppermute | solution.py:114
  78.7 1.6 collective-permute-start.17
  81.0 4.1 %collective-permute-done.17 = bf16[256,256]{1,0:T(8,128)(2,1)S(1)} collective-permute-done((bf16[256,256]{1,0:T(8,128)(2,1)S(1)}, bf16[256,256]{1,0:T(8,128)(2,1)S(1)}, u32[]{:S(2)}, u32[]{:S(2)}) %collective-permute-start.17) | collective-permute-done | bytes 131104 | tf_op jit(solution)/shard_map/ppermute | solution.py:114
  87.1 3.7 %collective-permute-done.20 = bf16[2,256,256]{2,1,0:T(8,128)(2,1)S(1)} collective-permute-done((bf16[2,256,256]{2,1,0:T(8,128)(2,1)S(1)}, bf16[2,256,256]{2,1,0:T(8,128)(2,1)S(1)}, u32[]{:S(2)}, u32[]{:S(2)}) %collective-permute-start.20) | collective-permute-done | bytes 262176 | tf_op jit(solution)/shard_map/ppermute | solution.py:114
  92.6 2.6 %collective-permute-done.22 = bf16[2,256,256]{2,1,0:T(8,128)(2,1)S(1)} collective-permute-done((bf16[2,256,256]{2,1,0:T(8,128)(2,1)S(1)}, bf16[2,256,256]{2,1,0:T(8,128)(2,1)S(1)}, u32[]{:S(2)}, u32[]{:S(2)}) %collective-permute-start.22) | collective-permute-done | bytes 262176 | tf_op jit(solution)/shard_map/ppermute | solution.py:114
  95.3 1.7 collective-permute-start.31
  100.4 5.5 %collective-permute-done.23 = bf16[256,256]{1,0:T(8,128)(2,1)S(1)} collective-permute-done((bf16[256,256]{1,0:T(8,128)(2,1)S(1)}, bf16[256,256]{1,0:T(8,128)(2,1)S(1)}, u32[]{:S(2)}, u32[]{:S(2)}) %collective-permute-start.23) | collective-permute-done | bytes 131104 | tf_op jit(solution)/shard_map/ppermute | solution.py:114
  110.0 1.8 collective-permute-start.27
  112.2 1.8 collective-permute-start.26
  116.2 1.7 collective-permute-start.35
  119.6 1.9 collective-permute-start.29
  124.7 3.1 %collective-permute-done.26 = bf16[768,256]{1,0:T(8,128)(2,1)S(1)} collective-permute-done((bf16[768,256]{1,0:T(8,128)(2,1)S(1)}, bf16[768,256]{1,0:T(8,128)(2,1)S(1)}, u32[]{:S(2)}, u32[]{:S(2)}) %collective-permute-start.26) | collective-permute-done | bytes 393248 | tf_op jit(solution)/shard_map/ppermute | solution.py:114
  131.2 3.5 %collective-permute-done.34 = bf16[768,256]{1,0:T(8,128)(2,1)S(1)} collective-permute-done((bf16[768,256]{1,0:T(8,128)(2,1)S(1)}, bf16[768,256]{1,0:T(8,128)(2,1)S(1)}, u32[]{:S(2)}, u32[]{:S(2)}) %collective-permute-start.34) | collective-permute-done | bytes 393248 | tf_op jit(solution)/shard_map/ppermute | solution.py:114
  139.1 3.0 %collective-permute-done.37 = bf16[768,256]{1,0:T(8,128)(2,1)S(1)} collective-permute-done((bf16[768,256]{1,0:T(8,128)(2,1)S(1)}, bf16[768,256]{1,0:T(8,128)(2,1)S(1)}, u32[]{:S(2)}, u32[]{:S(2)}) %collective-permute-start.37) | collective-permute-done | bytes 393248 | tf_op jit(solution)/shard_map/ppermute | solution.py:114
  144.3 2.6 %collective-permute-start.38 = (bf16[256,256]{1,0:T(8,128)(2,1)S(1)}, bf16[256,256]{1,0:T(8,128)(2,1)S(1)}, u32[]{:S(2)}, u32[]{:S(2)}) collective-permute-start(bf16[256,256]{1,0:T(8,128)(2,1)S(1)} %slice.273), channel_id=1, source_target_pairs={{0,4},{4,0},{8,12},{12,8},{16,20},{20,16},{24,28},{28,24},{1,5},{5... | collective-permute-start | bytes 393224 | tf_op jit(solution)/shard_map/ppermute | solution.py:114
  148.5 2.8 %collective-permute-done.38 = bf16[256,256]{1,0:T(8,128)(2,1)S(1)} collective-permute-done((bf16[256,256]{1,0:T(8,128)(2,1)S(1)}, bf16[256,256]{1,0:T(8,128)(2,1)S(1)}, u32[]{:S(2)}, u32[]{:S(2)}) %collective-permute-start.38) | collective-permute-done | bytes 131104 | tf_op jit(solution)/shard_map/ppermute | solution.py:114
  152.9 1.6 collective-permute-start.46
  156.8 5.3 %collective-permute-done.46 = bf16[256,256]{1,0:T(8,128)(2,1)S(1)} collective-permute-done((bf16[256,256]{1,0:T(8,128)(2,1)S(1)}, bf16[256,256]{1,0:T(8,128)(2,1)S(1)}, u32[]{:S(2)}, u32[]{:S(2)}) %collective-permute-start.46) | collective-permute-done | bytes 131104 | tf_op jit(solution)/shard_map/ppermute | solution.py:114
  163.0 1.3 collective-permute-start.47
  164.4 2.0 %collective-permute-done.43 = bf16[2,256,256]{2,1,0:T(8,128)(2,1)S(1)} collective-permute-done((bf16[2,256,256]{2,1,0:T(8,128)(2,1)S(1)}, bf16[2,256,256]{2,1,0:T(8,128)(2,1)S(1)}, u32[]{:S(2)}, u32[]{:S(2)}) %collective-permute-start.43) | collective-permute-done | bytes 262176 | tf_op jit(solution)/shard_map/ppermute | solution.py:114
  166.6 5.3 %collective-permute-done.49 = bf16[2,256,256]{2,1,0:T(8,128)(2,1)S(1)} collective-permute-done((bf16[2,256,256]{2,1,0:T(8,128)(2,1)S(1)}, bf16[2,256,256]{2,1,0:T(8,128)(2,1)S(1)}, u32[]{:S(2)}, u32[]{:S(2)}) %collective-permute-start.49) | collective-permute-done | bytes 262176 | tf_op jit(solution)/shard_map/ppermute | solution.py:114
  172.2 1.9 collective-permute-start.51
  174.1 3.5 %collective-permute-done.47 = bf16[2,256,256]{2,1,0:T(8,128)(2,1)S(1)} collective-permute-done((bf16[2,256,256]{2,1,0:T(8,128)(2,1)S(1)}, bf16[2,256,256]{2,1,0:T(8,128)(2,1)S(1)}, u32[]{:S(2)}, u32[]{:S(2)}) %collective-permute-start.47) | collective-permute-done | bytes 262176 | tf_op jit(solution)/shard_map/ppermute | solution.py:114
  177.8 1.9 collective-permute-start.50
  180.2 1.5 collective-permute-done.51
  181.9 2.6 %collective-permute-start.52 = (bf16[2,256,256]{2,1,0:T(8,128)(2,1)S(1)}, bf16[2,256,256]{2,1,0:T(8,128)(2,1)S(1)}, u32[]{:S(2)}, u32[]{:S(2)}) collective-permute-start(bf16[2,256,256]{2,1,0:T(8,128)(2,1)S(1)} %add_convert_fusion), channel_id=1, source_target_pairs={{0,24},{4,28},{8,0},{12,4},{16,8},{20,12},{24,16},{28,20},{1,25},{... | collective-permute-start | bytes 786440 | tf_op jit(solution)/shard_map/ppermute | solution.py:114
  184.5 1.8 collective-permute-done.50
  186.6 3.5 %collective-permute-done.52 = bf16[2,256,256]{2,1,0:T(8,128)(2,1)S(1)} collective-permute-done((bf16[2,256,256]{2,1,0:T(8,128)(2,1)S(1)}, bf16[2,256,256]{2,1,0:T(8,128)(2,1)S(1)}, u32[]{:S(2)}, u32[]{:S(2)}) %collective-permute-start.52) | collective-permute-done | bytes 262176 | tf_op jit(solution)/shard_map/ppermute | solution.py:114
  190.6 1.4 collective-permute-done.56
  192.6 2.7 %multiply_subtract_fusion = (f32[2,128,2048]{2,1,0:T(8,128)}, f32[2,128,2048]{2,1,0:T(8,128)}) fusion(f32[2,128,2048]{2,1,0:T(8,128)S(1)} %copy-done, f32[2,128,1024]{2,1,0:T(8,128)S(1)} %get-tuple-element.215, f32[2,128,1024]{2,1,0:T(8,128)S(1)} %get-tuple-element.214, f32[2,128,2048]{2,1,0:T(8,128)S(1)} %copy-done.1), kind=kLoop, calls=%fused_computation.1 | loop fusion | flops 3670016 | bytes 10485760 | tf_op jit(solution)/shard_map/sub | solution.py:302
  (223 shorter events, 55.8 us)
Async XLA Ops:
  2.3 9.2 %collective-permute-start = (bf16[2,128,1024]{2,1,0:T(8,128)(2,1)S(1)}, bf16[2,128,1024]{2,1,0:T(8,128)(2,1)S(1)}, u32[]{:S(2)}, u32[]{:S(2)}) collective-permute-start(bf16[2,128,1024]{2,1,0:T(8,128)(2,1)S(1)} %get-tuple-element.107), channel_id=1, source_target_pairs={{0,1},{1,0},{2,3},{3,2},{4,5},{5,4},{6,7},{7,6},{8,9},{9,8},{10,11... | collective-permute-start | bytes 1572872 | tf_op jit(solution)/shard_map/ppermute | solution.py:114
  8.4 18.8 %collective-permute-start.1 = (bf16[384,2048]{1,0:T(8,128)(2,1)}, bf16[384,2048]{1,0:T(8,128)(2,1)}, u32[]{:S(2)}, u32[]{:S(2)}) collective-permute-start(bf16[384,2048]{1,0:T(8,128)(2,1)} %get-tuple-element.123), channel_id=1, source_target_pairs={{0,1},{1,0},{2,3},{3,2},{4,5},{5,4},{6,7},{7,6},{8,9},{9,8},{10,11... | collective-permute-start | bytes 4718600 | tf_op jit(solution)/shard_map/ppermute | solution.py:114
  8.5 38.5 %collective-permute-start.4 = (bf16[384,2048]{1,0:T(8,128)(2,1)}, bf16[384,2048]{1,0:T(8,128)(2,1)S(1)}, u32[]{:S(2)}, u32[]{:S(2)}) collective-permute-start(bf16[384,2048]{1,0:T(8,128)(2,1)} %get-tuple-element.114), channel_id=1, source_target_pairs={{0,2},{1,3},{2,0},{3,1},{4,6},{5,7},{6,4},{7,5},{8,10},{9,11},{10,... | collective-permute-start | bytes 4718600 | tf_op jit(solution)/shard_map/ppermute | solution.py:114
  11.6 11.1 %collective-permute-start.3 = (bf16[2,256,256]{2,1,0:T(8,128)(2,1)S(1)}, bf16[2,256,256]{2,1,0:T(8,128)(2,1)}, u32[]{:S(2)}, u32[]{:S(2)}) collective-permute-start(bf16[2,256,256]{2,1,0:T(8,128)(2,1)S(1)} %get-tuple-element.128), channel_id=1, source_target_pairs={{0,8},{4,12},{8,16},{12,20},{16,24},{20,28},{24,0},{28,4},{1,9},{5... | collective-permute-start | bytes 786440 | tf_op jit(solution)/shard_map/ppermute | solution.py:114
  13.3 14.0 %collective-permute-start.2 = (bf16[2,256,256]{2,1,0:T(8,128)(2,1)S(1)}, bf16[2,256,256]{2,1,0:T(8,128)(2,1)}, u32[]{:S(2)}, u32[]{:S(2)}) collective-permute-start(bf16[2,256,256]{2,1,0:T(8,128)(2,1)S(1)} %get-tuple-element.133), channel_id=1, source_target_pairs={{0,8},{4,12},{8,16},{12,20},{16,24},{20,28},{24,0},{28,4},{1,9},{5... | collective-permute-start | bytes 786440 | tf_op jit(solution)/shard_map/ppermute | solution.py:114
  25.0 11.1 %collective-permute-start.8 = (bf16[2,256,256]{2,1,0:T(8,128)(2,1)}, bf16[2,256,256]{2,1,0:T(8,128)(2,1)S(1)}, u32[]{:S(2)}, u32[]{:S(2)}) collective-permute-start(bf16[2,256,256]{2,1,0:T(8,128)(2,1)} %collective-permute-done.3), channel_id=1, source_target_pairs={{0,8},{4,12},{8,16},{12,20},{16,24},{20,28},{24,0},{28,4},{1,9},{5... | collective-permute-start | bytes 786440 | tf_op jit(solution)/shard_map/ppermute | solution.py:114
  27.3 14.5 %collective-permute-start.7 = (bf16[2,256,256]{2,1,0:T(8,128)(2,1)}, bf16[2,256,256]{2,1,0:T(8,128)(2,1)S(1)}, u32[]{:S(2)}, u32[]{:S(2)}) collective-permute-start(bf16[2,256,256]{2,1,0:T(8,128)(2,1)} %collective-permute-done.2), channel_id=1, source_target_pairs={{0,8},{4,12},{8,16},{12,20},{16,24},{20,28},{24,0},{28,4},{1,9},{5... | collective-permute-start | bytes 786440 | tf_op jit(solution)/shard_map/ppermute | solution.py:114
  31.9 15.1 %collective-permute-start.6 = (bf16[2,256,256]{2,1,0:T(8,128)(2,1)S(1)}, bf16[2,256,256]{2,1,0:T(8,128)(2,1)S(1)}, u32[]{:S(2)}, u32[]{:S(2)}) collective-permute-start(bf16[2,256,256]{2,1,0:T(8,128)(2,1)S(1)} %get-tuple-element.146), channel_id=1, source_target_pairs={{0,8},{4,12},{8,16},{12,20},{16,24},{20,28},{24,0},{28,4},{1,9},{5... | collective-permute-start | bytes 786440 | tf_op jit(solution)/shard_map/ppermute | solution.py:114
  47.0 28.4 %collective-permute-start.9 = (bf16[384,2048]{1,0:T(8,128)(2,1)S(1)}, bf16[384,2048]{1,0:T(8,128)(2,1)S(1)}, u32[]{:S(2)}, u32[]{:S(2)}) collective-permute-start(bf16[384,2048]{1,0:T(8,128)(2,1)S(1)} %collective-permute-done.4), channel_id=1, source_target_pairs={{0,1},{1,0},{2,3},{3,2},{4,5},{5,4},{6,7},{7,6},{8,9},{9,8},{10,11... | collective-permute-start | bytes 4718600 | tf_op jit(solution)/shard_map/ppermute | solution.py:114
  47.9 10.9 %collective-permute-start.10 = (bf16[2,256,256]{2,1,0:T(8,128)(2,1)S(1)}, bf16[2,256,256]{2,1,0:T(8,128)(2,1)S(1)}, u32[]{:S(2)}, u32[]{:S(2)}) collective-permute-start(bf16[2,256,256]{2,1,0:T(8,128)(2,1)S(1)} %collective-permute-done.8), channel_id=1, source_target_pairs={{0,8},{4,12},{8,16},{12,20},{16,24},{20,28},{24,0},{28,4},{1,9},{5... | collective-permute-start | bytes 786440 | tf_op jit(solution)/shard_map/ppermute | solution.py:114
  50.0 16.0 %collective-permute-start.11 = (bf16[768,256]{1,0:T(8,128)(2,1)S(1)}, bf16[768,256]{1,0:T(8,128)(2,1)S(1)}, u32[]{:S(2)}, u32[]{:S(2)}) collective-permute-start(bf16[768,256]{1,0:T(8,128)(2,1)S(1)} %pad_maximum_fusion.19), channel_id=1, source_target_pairs={{0,4},{4,0},{8,12},{12,8},{16,20},{20,16},{24,28},{28,24},{1,5},{5... | collective-permute-start | bytes 1179656 | tf_op jit(solution)/shard_map/ppermute | solution.py:114
  51.6 12.9 %collective-permute-start.15 = (bf16[2,256,256]{2,1,0:T(8,128)(2,1)S(1)}, bf16[2,256,256]{2,1,0:T(8,128)(2,1)S(1)}, u32[]{:S(2)}, u32[]{:S(2)}) collective-permute-start(bf16[2,256,256]{2,1,0:T(8,128)(2,1)S(1)} %collective-permute-done.7), channel_id=1, source_target_pairs={{0,8},{4,12},{8,16},{12,20},{16,24},{20,28},{24,0},{28,4},{1,9},{5... | collective-permute-start | bytes 786440 | tf_op jit(solution)/shard_map/ppermute | solution.py:114
  53.2 19.4 %collective-permute-start.16 = (bf16[768,256]{1,0:T(8,128)(2,1)S(1)}, bf16[768,256]{1,0:T(8,128)(2,1)S(1)}, u32[]{:S(2)}, u32[]{:S(2)}) collective-permute-start(bf16[768,256]{1,0:T(8,128)(2,1)S(1)} %pad_maximum_fusion.20), channel_id=1, source_target_pairs={{0,4},{4,0},{8,12},{12,8},{16,20},{20,16},{24,28},{28,24},{1,5},{5... | collective-permute-start | bytes 1179656 | tf_op jit(solution)/shard_map/ppermute | solution.py:114
  58.9 16.5 %collective-permute-start.14 = (bf16[2,256,256]{2,1,0:T(8,128)(2,1)S(1)}, bf16[2,256,256]{2,1,0:T(8,128)(2,1)S(1)}, u32[]{:S(2)}, u32[]{:S(2)}) collective-permute-start(bf16[2,256,256]{2,1,0:T(8,128)(2,1)S(1)} %get-tuple-element.154), channel_id=1, source_target_pairs={{0,8},{4,12},{8,16},{12,20},{16,24},{20,28},{24,0},{28,4},{1,9},{5... | collective-permute-start | bytes 786440 | tf_op jit(solution)/shard_map/ppermute | solution.py:114
  66.0 9.3 %collective-permute-start.18 = (bf16[2,256,256]{2,1,0:T(8,128)(2,1)S(1)}, bf16[2,256,256]{2,1,0:T(8,128)(2,1)S(1)}, u32[]{:S(2)}, u32[]{:S(2)}) collective-permute-start(bf16[2,256,256]{2,1,0:T(8,128)(2,1)S(1)} %collective-permute-done.6), channel_id=1, source_target_pairs={{0,8},{4,12},{8,16},{12,20},{16,24},{20,28},{24,0},{28,4},{1,9},{5... | collective-permute-start | bytes 786440 | tf_op jit(solution)/shard_map/ppermute | solution.py:114
  77.5 13.3 %collective-permute-start.13 = (bf16[768,256]{1,0:T(8,128)(2,1)S(1)}, bf16[768,256]{1,0:T(8,128)(2,1)S(1)}, u32[]{:S(2)}, u32[]{:S(2)}) collective-permute-start(bf16[768,256]{1,0:T(8,128)(2,1)S(1)} %convolution_convert_fusion.3), channel_id=1, source_target_pairs={{0,2},{1,3},{2,0},{3,1},{4,6},{5,7},{6,4},{7,5},{8,10},{9,11},{10,... | collective-permute-start | bytes 1179656 | tf_op jit(solution)/shard_map/ppermute | solution.py:114
  80.4 17.2 %collective-permute-start.21 = (bf16[768,256]{1,0:T(8,128)(2,1)S(1)}, bf16[768,256]{1,0:T(8,128)(2,1)S(1)}, u32[]{:S(2)}, u32[]{:S(2)}) collective-permute-start(bf16[768,256]{1,0:T(8,128)(2,1)S(1)} %pad_maximum_fusion.21), channel_id=1, source_target_pairs={{0,4},{4,0},{8,12},{12,8},{16,20},{20,16},{24,28},{28,24},{1,5},{5... | collective-permute-start | bytes 1179656 | tf_op jit(solution)/shard_map/ppermute | solution.py:114
  81.0 9.8 %collective-permute-start.20 = (bf16[2,256,256]{2,1,0:T(8,128)(2,1)S(1)}, bf16[2,256,256]{2,1,0:T(8,128)(2,1)S(1)}, u32[]{:S(2)}, u32[]{:S(2)}) collective-permute-start(bf16[2,256,256]{2,1,0:T(8,128)(2,1)S(1)} %collective-permute-done.18), channel_id=1, source_target_pairs={{0,8},{4,12},{8,16},{12,20},{16,24},{20,28},{24,0},{28,4},{1,9},{5... | collective-permute-start | bytes 786440 | tf_op jit(solution)/shard_map/ppermute | solution.py:114
  86.1 12.1 %collective-permute-start.24 = (bf16[768,256]{1,0:T(8,128)(2,1)S(1)}, bf16[768,256]{1,0:T(8,128)(2,1)S(1)}, u32[]{:S(2)}, u32[]{:S(2)}) collective-permute-start(bf16[768,256]{1,0:T(8,128)(2,1)S(1)} %convolution_convert_fusion.2), channel_id=1, source_target_pairs={{0,2},{1,3},{2,0},{3,1},{4,6},{5,7},{6,4},{7,5},{8,10},{9,11},{10,... | collective-permute-start | bytes 1179656 | tf_op jit(solution)/shard_map/ppermute | solution.py:114
  92.0 15.8 %collective-permute-start.19 = (bf16[768,256]{1,0:T(8,128)(2,1)S(1)}, bf16[768,256]{1,0:T(8,128)(2,1)S(1)}, u32[]{:S(2)}, u32[]{:S(2)}) collective-permute-start(bf16[768,256]{1,0:T(8,128)(2,1)S(1)} %multiply_convert_fusion.3), channel_id=1, source_target_pairs={{0,2},{1,3},{2,0},{3,1},{4,6},{5,7},{6,4},{7,5},{8,10},{9,11},{10,... | collective-permute-start | bytes 1179656 | tf_op jit(solution)/shard_map/ppermute | solution.py:114
  95.3 16.9 %collective-permute-start.31 = (bf16[768,256]{1,0:T(8,128)(2,1)S(1)}, bf16[768,256]{1,0:T(8,128)(2,1)S(1)}, u32[]{:S(2)}, u32[]{:S(2)}) collective-permute-start(bf16[768,256]{1,0:T(8,128)(2,1)S(1)} %pad_maximum_fusion.22), channel_id=1, source_target_pairs={{0,4},{4,0},{8,12},{12,8},{16,20},{20,16},{24,28},{28,24},{1,5},{5... | collective-permute-start | bytes 1179656 | tf_op jit(solution)/shard_map/ppermute | solution.py:114
  97.0 8.9 %collective-permute-start.23 = (bf16[256,256]{1,0:T(8,128)(2,1)S(1)}, bf16[256,256]{1,0:T(8,128)(2,1)S(1)}, u32[]{:S(2)}, u32[]{:S(2)}) collective-permute-start(bf16[256,256]{1,0:T(8,128)(2,1)S(1)} %dynamic-slice_bitcast_fusion.1), channel_id=1, source_target_pairs={{0,4},{4,0},{8,12},{12,8},{16,20},{20,16},{24,28},{28,24},{1,5},{5... | collective-permute-start | bytes 393224 | tf_op jit(solution)/shard_map/ppermute | solution.py:114
  99.4 15.6 %collective-permute-start.28 = (bf16[768,256]{1,0:T(8,128)(2,1)S(1)}, bf16[768,256]{1,0:T(8,128)(2,1)S(1)}, u32[]{:S(2)}, u32[]{:S(2)}) collective-permute-start(bf16[768,256]{1,0:T(8,128)(2,1)S(1)} %multiply_convert_fusion.2), channel_id=1, source_target_pairs={{0,2},{1,3},{2,0},{3,1},{4,6},{5,7},{6,4},{7,5},{8,10},{9,11},{10,... | collective-permute-start | bytes 1179656 | tf_op jit(solution)/shard_map/ppermute | solution.py:114
  100.4 11.4 %collective-permute-start.25 = (bf16[2,256,256]{2,1,0:T(8,128)(2,1)S(1)}, bf16[2,256,256]{2,1,0:T(8,128)(2,1)S(1)}, u32[]{:S(2)}, u32[]{:S(2)}) collective-permute-start(bf16[2,256,256]{2,1,0:T(8,128)(2,1)S(1)} %collective-permute-done.22), channel_id=1, source_target_pairs={{0,8},{4,12},{8,16},{12,20},{16,24},{20,28},{24,0},{28,4},{1,9},{5... | collective-permute-start | bytes 786440 | tf_op jit(solution)/shard_map/ppermute | solution.py:114
  106.9 15.6 %collective-permute-start.30 = (bf16[768,256]{1,0:T(8,128)(2,1)S(1)}, bf16[768,256]{1,0:T(8,128)(2,1)S(1)}, u32[]{:S(2)}, u32[]{:S(2)}) collective-permute-start(bf16[768,256]{1,0:T(8,128)(2,1)S(1)} %convolution_convert_fusion.1), channel_id=1, source_target_pairs={{0,2},{1,3},{2,0},{3,1},{4,6},{5,7},{6,4},{7,5},{8,10},{9,11},{10,... | collective-permute-start | bytes 1179656 | tf_op jit(solution)/shard_map/ppermute | solution.py:114
  110.0 8.9 %collective-permute-start.27 = (bf16[256,256]{1,0:T(8,128)(2,1)S(1)}, bf16[256,256]{1,0:T(8,128)(2,1)S(1)}, u32[]{:S(2)}, u32[]{:S(2)}) collective-permute-start(bf16[256,256]{1,0:T(8,128)(2,1)S(1)} %slice.260), channel_id=1, source_target_pairs={{0,4},{4,0},{8,12},{12,8},{16,20},{20,16},{24,28},{28,24},{1,5},{5... | collective-permute-start | bytes 393224 | tf_op jit(solution)/shard_map/ppermute | solution.py:114
  112.2 15.5 %collective-permute-start.26 = (bf16[768,256]{1,0:T(8,128)(2,1)S(1)}, bf16[768,256]{1,0:T(8,128)(2,1)S(1)}, u32[]{:S(2)}, u32[]{:S(2)}) collective-permute-start(bf16[768,256]{1,0:T(8,128)(2,1)S(1)} %slice.259), channel_id=1, source_target_pairs={{0,4},{4,0},{8,12},{12,8},{16,20},{20,16},{24,28},{28,24},{1,5},{5... | collective-permute-start | bytes 1179656 | tf_op jit(solution)/shard_map/ppermute | solution.py:114
  116.2 14.3 %collective-permute-start.35 = (bf16[256,256]{1,0:T(8,128)(2,1)S(1)}, bf16[256,256]{1,0:T(8,128)(2,1)S(1)}, u32[]{:S(2)}, u32[]{:S(2)}) collective-permute-start(bf16[256,256]{1,0:T(8,128)(2,1)S(1)} %slice.268), channel_id=1, source_target_pairs={{0,4},{4,0},{8,12},{12,8},{16,20},{20,16},{24,28},{28,24},{1,5},{5... | collective-permute-start | bytes 393224 | tf_op jit(solution)/shard_map/ppermute | solution.py:114
  118.9 17.9 %collective-permute-start.39 = (bf16[768,256]{1,0:T(8,128)(2,1)S(1)}, bf16[768,256]{1,0:T(8,128)(2,1)S(1)}, u32[]{:S(2)}, u32[]{:S(2)}) collective-permute-start(bf16[768,256]{1,0:T(8,128)(2,1)S(1)} %slice.267), channel_id=1, source_target_pairs={{0,4},{4,0},{8,12},{12,8},{16,20},{20,16},{24,28},{28,24},{1,5},{5... | collective-permute-start | bytes 1179656 | tf_op jit(solution)/shard_map/ppermute | solution.py:114
  119.6 9.4 %collective-permute-start.29 = (bf16[2,256,256]{2,1,0:T(8,128)(2,1)S(1)}, bf16[2,256,256]{2,1,0:T(8,128)(2,1)S(1)}, u32[]{:S(2)}, u32[]{:S(2)}) collective-permute-start(bf16[2,256,256]{2,1,0:T(8,128)(2,1)S(1)} %add_convert_fusion.11), channel_id=1, source_target_pairs={{0,24},{4,28},{8,0},{12,4},{16,8},{20,12},{24,16},{28,20},{1,25},{... | collective-permute-start | bytes 786440 | tf_op jit(solution)/shard_map/ppermute | solution.py:114
  122.6 12.1 %collective-permute-start.34 = (bf16[768,256]{1,0:T(8,128)(2,1)S(1)}, bf16[768,256]{1,0:T(8,128)(2,1)S(1)}, u32[]{:S(2)}, u32[]{:S(2)}) collective-permute-start(bf16[768,256]{1,0:T(8,128)(2,1)S(1)} %convolution_convert_fusion), channel_id=1, source_target_pairs={{0,2},{1,3},{2,0},{3,1},{4,6},{5,7},{6,4},{7,5},{8,10},{9,11},{10,... | collective-permute-start | bytes 1179656 | tf_op jit(solution)/shard_map/ppermute | solution.py:114
  127.7 14.3 %collective-permute-start.37 = (bf16[768,256]{1,0:T(8,128)(2,1)S(1)}, bf16[768,256]{1,0:T(8,128)(2,1)S(1)}, u32[]{:S(2)}, u32[]{:S(2)}) collective-permute-start(bf16[768,256]{1,0:T(8,128)(2,1)S(1)} %multiply_convert_fusion.1), channel_id=1, source_target_pairs={{0,2},{1,3},{2,0},{3,1},{4,6},{5,7},{6,4},{7,5},{8,10},{9,11},{10,... | collective-permute-start | bytes 1179656 | tf_op jit(solution)/shard_map/ppermute | solution.py:114
  129.2 8.5 %collective-permute-start.33 = (bf16[2,256,256]{2,1,0:T(8,128)(2,1)S(1)}, bf16[2,256,256]{2,1,0:T(8,128)(2,1)S(1)}, u32[]{:S(2)}, u32[]{:S(2)}) collective-permute-start(bf16[2,256,256]{2,1,0:T(8,128)(2,1)S(1)} %add_convert_fusion.10), channel_id=1, source_target_pairs={{0,24},{4,28},{8,0},{12,4},{16,8},{20,12},{24,16},{28,20},{1,25},{... | collective-permute-start | bytes 786440 | tf_op jit(solution)/shard_map/ppermute | solution.py:114
  130.6 16.3 %collective-permute-start.40 = (bf16[2,256,256]{2,1,0:T(8,128)(2,1)S(1)}, bf16[2,256,256]{2,1,0:T(8,128)(2,1)S(1)}, u32[]{:S(2)}, u32[]{:S(2)}) collective-permute-start(bf16[2,256,256]{2,1,0:T(8,128)(2,1)S(1)} %add_convert_fusion.9), channel_id=1, source_target_pairs={{0,24},{4,28},{8,0},{12,4},{16,8},{20,12},{24,16},{28,20},{1,25},{... | collective-permute-start | bytes 786440 | tf_op jit(solution)/shard_map/ppermute | solution.py:114
  135.9 15.8 %collective-permute-start.42 = (bf16[768,256]{1,0:T(8,128)(2,1)S(1)}, bf16[768,256]{1,0:T(8,128)(2,1)S(1)}, u32[]{:S(2)}, u32[]{:S(2)}) collective-permute-start(bf16[768,256]{1,0:T(8,128)(2,1)S(1)} %multiply_convert_fusion), channel_id=1, source_target_pairs={{0,2},{1,3},{2,0},{3,1},{4,6},{5,7},{6,4},{7,5},{8,10},{9,11},{10,... | collective-permute-start | bytes 1179656 | tf_op jit(solution)/shard_map/ppermute | solution.py:114
  137.9 13.6 %collective-permute-start.36 = (bf16[2,256,256]{2,1,0:T(8,128)(2,1)S(1)}, bf16[2,256,256]{2,1,0:T(8,128)(2,1)S(1)}, u32[]{:S(2)}, u32[]{:S(2)}) collective-permute-start(bf16[2,256,256]{2,1,0:T(8,128)(2,1)S(1)} %add_convert_fusion.8), channel_id=1, source_target_pairs={{0,24},{4,28},{8,0},{12,4},{16,8},{20,12},{24,16},{28,20},{1,25},{... | collective-permute-start | bytes 786440 | tf_op jit(solution)/shard_map/ppermute | solution.py:114
  147.2 8.9 %collective-permute-start.41 = (bf16[2,256,256]{2,1,0:T(8,128)(2,1)S(1)}, bf16[2,256,256]{2,1,0:T(8,128)(2,1)S(1)}, u32[]{:S(2)}, u32[]{:S(2)}) collective-permute-start(bf16[2,256,256]{2,1,0:T(8,128)(2,1)S(1)} %add_convert_fusion.7), channel_id=1, source_target_pairs={{0,24},{4,28},{8,0},{12,4},{16,8},{20,12},{24,16},{28,20},{1,25},{... | collective-permute-start | bytes 786440 | tf_op jit(solution)/shard_map/ppermute | solution.py:114
  147.9 14.8 %collective-permute-start.44 = (bf16[768,256]{1,0:T(8,128)(2,1)S(1)}, bf16[768,256]{1,0:T(8,128)(2,1)S(1)}, u32[]{:S(2)}, u32[]{:S(2)}) collective-permute-start(bf16[768,256]{1,0:T(8,128)(2,1)S(1)} %slice.274), channel_id=1, source_target_pairs={{0,4},{4,0},{8,12},{12,8},{16,20},{20,16},{24,28},{28,24},{1,5},{5... | collective-permute-start | bytes 1179656 | tf_op jit(solution)/shard_map/ppermute | solution.py:114
  151.4 11.4 %collective-permute-start.45 = (bf16[2,256,256]{2,1,0:T(8,128)(2,1)S(1)}, bf16[2,256,256]{2,1,0:T(8,128)(2,1)S(1)}, u32[]{:S(2)}, u32[]{:S(2)}) collective-permute-start(bf16[2,256,256]{2,1,0:T(8,128)(2,1)S(1)} %add_convert_fusion.6), channel_id=1, source_target_pairs={{0,24},{4,28},{8,0},{12,4},{16,8},{20,12},{24,16},{28,20},{1,25},{... | collective-permute-start | bytes 786440 | tf_op jit(solution)/shard_map/ppermute | solution.py:114
  152.9 9.2 %collective-permute-start.46 = (bf16[256,256]{1,0:T(8,128)(2,1)S(1)}, bf16[256,256]{1,0:T(8,128)(2,1)S(1)}, u32[]{:S(2)}, u32[]{:S(2)}) collective-permute-start(bf16[256,256]{1,0:T(8,128)(2,1)S(1)} %slice.284), channel_id=1, source_target_pairs={{0,4},{4,0},{8,12},{12,8},{16,20},{20,16},{24,28},{28,24},{1,5},{5... | collective-permute-start | bytes 393224 | tf_op jit(solution)/shard_map/ppermute | solution.py:114
  155.6 11.0 %collective-permute-start.48 = (bf16[768,256]{1,0:T(8,128)(2,1)S(1)}, bf16[768,256]{1,0:T(8,128)(2,1)S(1)}, u32[]{:S(2)}, u32[]{:S(2)}) collective-permute-start(bf16[768,256]{1,0:T(8,128)(2,1)S(1)} %slice.283), channel_id=1, source_target_pairs={{0,4},{4,0},{8,12},{12,8},{16,20},{20,16},{24,28},{28,24},{1,5},{5... | collective-permute-start | bytes 1179656 | tf_op jit(solution)/shard_map/ppermute | solution.py:114
  156.3 10.0 %collective-permute-start.43 = (bf16[2,256,256]{2,1,0:T(8,128)(2,1)S(1)}, bf16[2,256,256]{2,1,0:T(8,128)(2,1)S(1)}, u32[]{:S(2)}, u32[]{:S(2)}) collective-permute-start(bf16[2,256,256]{2,1,0:T(8,128)(2,1)S(1)} %add_convert_fusion.5), channel_id=1, source_target_pairs={{0,24},{4,28},{8,0},{12,4},{16,8},{20,12},{24,16},{28,20},{1,25},{... | collective-permute-start | bytes 786440 | tf_op jit(solution)/shard_map/ppermute | solution.py:114
  162.2 9.7 %collective-permute-start.49 = (bf16[2,256,256]{2,1,0:T(8,128)(2,1)S(1)}, bf16[2,256,256]{2,1,0:T(8,128)(2,1)S(1)}, u32[]{:S(2)}, u32[]{:S(2)}) collective-permute-start(bf16[2,256,256]{2,1,0:T(8,128)(2,1)S(1)} %add_convert_fusion.4), channel_id=1, source_target_pairs={{0,24},{4,28},{8,0},{12,4},{16,8},{20,12},{24,16},{28,20},{1,25},{... | collective-permute-start | bytes 786440 | tf_op jit(solution)/shard_map/ppermute | solution.py:114
  163.0 14.6 %collective-permute-start.47 = (bf16[2,256,256]{2,1,0:T(8,128)(2,1)S(1)}, bf16[2,256,256]{2,1,0:T(8,128)(2,1)S(1)}, u32[]{:S(2)}, u32[]{:S(2)}) collective-permute-start(bf16[2,256,256]{2,1,0:T(8,128)(2,1)S(1)} %add_convert_fusion.3), channel_id=1, source_target_pairs={{0,24},{4,28},{8,0},{12,4},{16,8},{20,12},{24,16},{28,20},{1,25},{... | collective-permute-start | bytes 786440 | tf_op jit(solution)/shard_map/ppermute | solution.py:114
  172.2 9.5 %collective-permute-start.51 = (bf16[2,256,256]{2,1,0:T(8,128)(2,1)S(1)}, bf16[2,256,256]{2,1,0:T(8,128)(2,1)S(1)}, u32[]{:S(2)}, u32[]{:S(2)}) collective-permute-start(bf16[2,256,256]{2,1,0:T(8,128)(2,1)S(1)} %add_convert_fusion.2), channel_id=1, source_target_pairs={{0,24},{4,28},{8,0},{12,4},{16,8},{20,12},{24,16},{28,20},{1,25},{... | collective-permute-start | bytes 786440 | tf_op jit(solution)/shard_map/ppermute | solution.py:114
  177.8 8.5 %collective-permute-start.50 = (bf16[2,256,256]{2,1,0:T(8,128)(2,1)S(1)}, bf16[2,256,256]{2,1,0:T(8,128)(2,1)S(1)}, u32[]{:S(2)}, u32[]{:S(2)}) collective-permute-start(bf16[2,256,256]{2,1,0:T(8,128)(2,1)S(1)} %add_convert_fusion.1), channel_id=1, source_target_pairs={{0,24},{4,28},{8,0},{12,4},{16,8},{20,12},{24,16},{28,20},{1,25},{... | collective-permute-start | bytes 786440 | tf_op jit(solution)/shard_map/ppermute | solution.py:114
  179.7 10.8 %collective-permute-start.53 = (f32[2,128,256]{2,1,0:T(8,128)S(1)}, f32[2,128,256]{2,1,0:T(8,128)S(1)}, u32[]{:S(2)}, u32[]{:S(2)}) collective-permute-start(f32[2,128,256]{2,1,0:T(8,128)S(1)} %get-tuple-element.227), channel_id=1, source_target_pairs={{0,1},{1,0},{2,3},{3,2},{4,5},{5,4},{6,7},{7,6},{8,9},{9,8},{10,11... | collective-permute-start | bytes 786440 | tf_op jit(solution)/shard_map/ppermute | solution.py:114
  179.7 10.8 %collective-permute-start.54 = (f32[2,128,256]{2,1,0:T(8,128)S(1)}, f32[2,128,256]{2,1,0:T(8,128)S(1)}, u32[]{:S(2)}, u32[]{:S(2)}) collective-permute-start(f32[2,128,256]{2,1,0:T(8,128)S(1)} %get-tuple-element.229), channel_id=1, source_target_pairs={{0,1},{1,0},{2,3},{3,2},{4,5},{5,4},{6,7},{7,6},{8,9},{9,8},{10,11... | collective-permute-start | bytes 786440 | tf_op jit(solution)/shard_map/ppermute | solution.py:114
  (18 other events, 181.0 us)

commit v5 on v4

--- a/solution.py
+++ b/solution.py
@@ -11,13 +11,13 @@
 TOKEN_PARTS = 1
 ORDER = (
     "wp", "ws", "cut", "ct", "bl", "ya0", "z0.1", "z1.1", "cp", "rt", "z0.2", "cc", "z1.2", "tn", "co",
-    "z2.1", "x0.0", "z0.3", "z1.3", "x1.0", "z2.2", "z3.1", "cf0", "x0.1", "tf", "tk", "w0", "p0", "yp0",
+    "z2.1", "x0.0", "z0.3", "z1.3", "x1.0", "z2.2", "z3.1", "cf0", "x0.1", "tf", "w0", "p0", "yp0", "tk",
     "x1.1", "x2.0", "z2.3", "w1", "p1", "yp1", "z3.2", "s0", "ys0", "x3.0", "x2.1", "s1", "ys1", "z3.3",
     "w2", "p2", "yp2", "gn0", "go0", "gx0.0", "x3.1", "gx0.1", "gn1", "gx1.0", "gx1.1", "go1", "a0.3",
     "r0.3", "w3", "p3", "yp3", "s2", "ys2", "a0.2", "r0.2", "a1.3", "r1.3", "s3", "ys3", "a0.1", "r0.1",
     "go2", "gn2", "gx2.0", "a1.2", "r1.2", "gx2.1", "a2.3", "r2.3", "a0.0", "fs0", "gn3", "gx3.0", "go3",
     "gx3.1", "a1.1", "r1.1", "a3.3", "r3.3", "a2.2", "r2.2", "a1.0", "fs1", "a3.2", "r3.2", "a2.1", "r2.1",
-    "a3.1", "r3.1", "a2.0", "fs2", "a3.0", "fs3", "d:r3.3",
+    "a3.1", "r3.1", "a2.0", "fs2", "a3.0", "fs3",
 )
 
 def plain(master, momentum, routes, counts, tokens, cotangent):

time: 196 us -> 197 us (level)
  starting transfers between devices: 52.9 us -> 65.6 us
  waiting for transfers between devices: 90.5 us -> 79.2 us
    ppermute x57, starting transfers between devices: 52.9 us -> 65.6 us  [over(): return lambda a: lax.ppermute(a, axis, pairs)]
    ppermute x57, waiting for transfers between devices: 90.5 us -> 79.2 us  [over(): return lambda a: lax.ppermute(a, axis, pairs)]
  transfers between devices with their start and end apart: 57 -> 57, of which waited for: 28 -> 25; matrix products, arithmetic and copies ran while one was open for 17% -> 18% of each run, Pallas kernels for 3% -> 3%
where the time goes in v5:
time: 197 us
  waiting for transfers between devices  79.2 us (40%)
  starting transfers between devices  65.6 us (33%)
  matrix products  17.2 us (9%)
  local copies, waits for them, and re-layouts  13.7 us (7%)
  other arithmetic  10.1 us (5%)
  between operations  5.83 us (3%)
  Pallas kernels  4.96 us (3%)
    ppermute x57, waiting for transfers between devices, over(): return lambda a: lax.ppermute(a, axis, pairs)  79.2 us
    ppermute x57, starting transfers between devices, over(): return lambda a: lax.ppermute(a, axis, pairs)  65.6 us
    dot_general x8, matrix products, fn(): lax.dot_general(val['tk'][:, lo:lo + own_rows], sig, (((0,), (0,)), ((),...  8.47 us
    unnamed x45, local copies, waits for them, and re-layouts  7.23 us
    pallas_call x1, Pallas kernels, column_blocks(): pl.pallas_call(body, out_shape=(shape, shape), grid_spec=pltpu.PrefetchSc...  4.96 us
    dot_general x4, matrix products, fn(): pre = jnp.dot(val['tn'], val[f'w{j}'], preferred_element_type=f32)  4.84 us
  transfers between devices with their start and end apart: 57, of which 25 were waited for; matrix products, arithmetic and copies ran while one was open for 18% of the time, Pallas kernels for 3%

profile of v5, /device:TPU:0, one launch (start us, length us, event | category | flops | bytes accessed | tf_op | source)
XLA Modules:
  0.0 196.7 jit_solution(4129006911157441345)
XLA Ops:
  0.6 1.7 select_convert_fusion.1
  3.5 5.0 %shard_map.77 = (bf16[384,2048]{1,0:T(8,128)(2,1)}, bf16[384,2048]{1,0:T(8,128)(2,1)}) custom-call(s32[16]{0:T(128)} %pad_add_fusion.places_ref, bf16[384,4096]{1,0:T(8,128)(2,1)} %src), custom_call_target="tpu_custom_call" | custom-call | tf_op jit(solution)/shard_map/pallas_call | solution.py:83
  8.5 3.0 %collective-permute-start.4 = (bf16[384,2048]{1,0:T(8,128)(2,1)}, bf16[384,2048]{1,0:T(8,128)(2,1)S(1)}, u32[]{:S(2)}, u32[]{:S(2)}) collective-permute-start(bf16[384,2048]{1,0:T(8,128)(2,1)} %get-tuple-element.114), channel_id=1, source_target_pairs={{0,2},{1,3},{2,0},{3,1},{4,6},{5,7},{6,4},{7,5},{8,10},{9,11},{10,... | collective-permute-start | bytes 4718600 | tf_op jit(solution)/shard_map/ppermute | solution.py:114
  11.6 1.6 collective-permute-start.3
  13.3 1.6 collective-permute-start.2
  21.2 1.6 collective-permute-done.3
  25.0 2.2 %collective-permute-done.2 = bf16[2,256,256]{2,1,0:T(8,128)(2,1)} collective-permute-done((bf16[2,256,256]{2,1,0:T(8,128)(2,1)S(1)}, bf16[2,256,256]{2,1,0:T(8,128)(2,1)}, u32[]{:S(2)}, u32[]{:S(2)}) %collective-permute-start.2) | collective-permute-done | bytes 262176 | tf_op jit(solution)/shard_map/ppermute | solution.py:114
  27.3 1.6 constant_dynamic-update-slice_fusion.1
  28.9 1.6 constant_dynamic-update-slice_fusion
  33.2 2.9 %collective-permute-done.8 = bf16[2,256,256]{2,1,0:T(8,128)(2,1)S(1)} collective-permute-done((bf16[2,256,256]{2,1,0:T(8,128)(2,1)}, bf16[2,256,256]{2,1,0:T(8,128)(2,1)S(1)}, u32[]{:S(2)}, u32[]{:S(2)}) %collective-permute-start.8) | collective-permute-done | bytes 262176 | tf_op jit(solution)/shard_map/ppermute | solution.py:114
  37.1 4.6 %collective-permute-done.7 = bf16[2,256,256]{2,1,0:T(8,128)(2,1)S(1)} collective-permute-done((bf16[2,256,256]{2,1,0:T(8,128)(2,1)}, bf16[2,256,256]{2,1,0:T(8,128)(2,1)S(1)}, u32[]{:S(2)}, u32[]{:S(2)}) %collective-permute-start.7) | collective-permute-done | bytes 262176 | tf_op jit(solution)/shard_map/ppermute | solution.py:114
  42.7 4.2 %collective-permute-done.6 = bf16[2,256,256]{2,1,0:T(8,128)(2,1)S(1)} collective-permute-done((bf16[2,256,256]{2,1,0:T(8,128)(2,1)S(1)}, bf16[2,256,256]{2,1,0:T(8,128)(2,1)S(1)}, u32[]{:S(2)}, u32[]{:S(2)}) %collective-permute-start.6) | collective-permute-done | bytes 262176 | tf_op jit(solution)/shard_map/ppermute | solution.py:114
  50.0 1.6 collective-permute-start.11
  51.6 1.6 collective-permute-start.15
  53.7 5.2 %collective-permute-done.10 = bf16[2,256,256]{2,1,0:T(8,128)(2,1)S(1)} collective-permute-done((bf16[2,256,256]{2,1,0:T(8,128)(2,1)S(1)}, bf16[2,256,256]{2,1,0:T(8,128)(2,1)S(1)}, u32[]{:S(2)}, u32[]{:S(2)}) %collective-permute-start.10) | collective-permute-done | bytes 262176 | tf_op jit(solution)/shard_map/ppermute | solution.py:114
  59.0 5.5 %collective-permute-done.15 = bf16[2,256,256]{2,1,0:T(8,128)(2,1)S(1)} collective-permute-done((bf16[2,256,256]{2,1,0:T(8,128)(2,1)S(1)}, bf16[2,256,256]{2,1,0:T(8,128)(2,1)S(1)}, u32[]{:S(2)}, u32[]{:S(2)}) %collective-permute-start.15) | collective-permute-done | bytes 262176 | tf_op jit(solution)/shard_map/ppermute | solution.py:114
  66.1 6.5 %collective-permute-done.12 = bf16[256,256]{1,0:T(8,128)(2,1)S(1)} collective-permute-done((bf16[256,256]{1,0:T(8,128)(2,1)S(1)}, bf16[256,256]{1,0:T(8,128)(2,1)S(1)}, u32[]{:S(2)}, u32[]{:S(2)}) %collective-permute-start.12) | collective-permute-done | bytes 131104 | tf_op jit(solution)/shard_map/ppermute | solution.py:114
  72.6 2.7 %collective-permute-done.18 = bf16[2,256,256]{2,1,0:T(8,128)(2,1)S(1)} collective-permute-done((bf16[2,256,256]{2,1,0:T(8,128)(2,1)S(1)}, bf16[2,256,256]{2,1,0:T(8,128)(2,1)S(1)}, u32[]{:S(2)}, u32[]{:S(2)}) %collective-permute-start.18) | collective-permute-done | bytes 262176 | tf_op jit(solution)/shard_map/ppermute | solution.py:114
  78.7 1.6 collective-permute-start.17
  81.0 4.1 %collective-permute-done.17 = bf16[256,256]{1,0:T(8,128)(2,1)S(1)} collective-permute-done((bf16[256,256]{1,0:T(8,128)(2,1)S(1)}, bf16[256,256]{1,0:T(8,128)(2,1)S(1)}, u32[]{:S(2)}, u32[]{:S(2)}) %collective-permute-start.17) | collective-permute-done | bytes 131104 | tf_op jit(solution)/shard_map/ppermute | solution.py:114
  87.1 3.7 %collective-permute-done.20 = bf16[2,256,256]{2,1,0:T(8,128)(2,1)S(1)} collective-permute-done((bf16[2,256,256]{2,1,0:T(8,128)(2,1)S(1)}, bf16[2,256,256]{2,1,0:T(8,128)(2,1)S(1)}, u32[]{:S(2)}, u32[]{:S(2)}) %collective-permute-start.20) | collective-permute-done | bytes 262176 | tf_op jit(solution)/shard_map/ppermute | solution.py:114
  92.7 2.6 %collective-permute-done.22 = bf16[2,256,256]{2,1,0:T(8,128)(2,1)S(1)} collective-permute-done((bf16[2,256,256]{2,1,0:T(8,128)(2,1)S(1)}, bf16[2,256,256]{2,1,0:T(8,128)(2,1)S(1)}, u32[]{:S(2)}, u32[]{:S(2)}) %collective-permute-start.22) | collective-permute-done | bytes 262176 | tf_op jit(solution)/shard_map/ppermute | solution.py:114
  95.3 1.7 collective-permute-start.31
  100.4 5.5 %collective-permute-done.23 = bf16[256,256]{1,0:T(8,128)(2,1)S(1)} collective-permute-done((bf16[256,256]{1,0:T(8,128)(2,1)S(1)}, bf16[256,256]{1,0:T(8,128)(2,1)S(1)}, u32[]{:S(2)}, u32[]{:S(2)}) %collective-permute-start.23) | collective-permute-done | bytes 131104 | tf_op jit(solution)/shard_map/ppermute | solution.py:114
  110.0 1.8 collective-permute-start.27
  112.3 1.8 collective-permute-start.26
  116.2 1.7 collective-permute-start.35
  119.6 1.9 collective-permute-start.29
  124.4 3.4 %collective-permute-done.26 = bf16[768,256]{1,0:T(8,128)(2,1)S(1)} collective-permute-done((bf16[768,256]{1,0:T(8,128)(2,1)S(1)}, bf16[768,256]{1,0:T(8,128)(2,1)S(1)}, u32[]{:S(2)}, u32[]{:S(2)}) %collective-permute-start.26) | collective-permute-done | bytes 393248 | tf_op jit(solution)/shard_map/ppermute | solution.py:114
  129.2 2.3 %collective-permute-start.33 = (bf16[2,256,256]{2,1,0:T(8,128)(2,1)S(1)}, bf16[2,256,256]{2,1,0:T(8,128)(2,1)S(1)}, u32[]{:S(2)}, u32[]{:S(2)}) collective-permute-start(bf16[2,256,256]{2,1,0:T(8,128)(2,1)S(1)} %add_convert_fusion.10), channel_id=1, source_target_pairs={{0,24},{4,28},{8,0},{12,4},{16,8},{20,12},{24,16},{28,20},{1,25},{... | collective-permute-start | bytes 786440 | tf_op jit(solution)/shard_map/ppermute | solution.py:114
  131.7 3.0 %collective-permute-done.34 = bf16[768,256]{1,0:T(8,128)(2,1)S(1)} collective-permute-done((bf16[768,256]{1,0:T(8,128)(2,1)S(1)}, bf16[768,256]{1,0:T(8,128)(2,1)S(1)}, u32[]{:S(2)}, u32[]{:S(2)}) %collective-permute-start.34) | collective-permute-done | bytes 393248 | tf_op jit(solution)/shard_map/ppermute | solution.py:114
  138.1 4.6 %collective-permute-start.36 = (bf16[2,256,256]{2,1,0:T(8,128)(2,1)S(1)}, bf16[2,256,256]{2,1,0:T(8,128)(2,1)S(1)}, u32[]{:S(2)}, u32[]{:S(2)}) collective-permute-start(bf16[2,256,256]{2,1,0:T(8,128)(2,1)S(1)} %add_convert_fusion.8), channel_id=1, source_target_pairs={{0,24},{4,28},{8,0},{12,4},{16,8},{20,12},{24,16},{28,20},{1,25},{... | collective-permute-start | bytes 786440 | tf_op jit(solution)/shard_map/ppermute | solution.py:114
  144.8 1.6 collective-permute-start.38
  148.4 2.0 %collective-permute-done.38 = bf16[256,256]{1,0:T(8,128)(2,1)S(1)} collective-permute-done((bf16[256,256]{1,0:T(8,128)(2,1)S(1)}, bf16[256,256]{1,0:T(8,128)(2,1)S(1)}, u32[]{:S(2)}, u32[]{:S(2)}) %collective-permute-start.38) | collective-permute-done | bytes 131104 | tf_op jit(solution)/shard_map/ppermute | solution.py:114
  150.5 1.8 collective-permute-start.45
  153.7 1.5 collective-permute-start.46
  157.1 2.4 %collective-permute-start.43 = (bf16[2,256,256]{2,1,0:T(8,128)(2,1)S(1)}, bf16[2,256,256]{2,1,0:T(8,128)(2,1)S(1)}, u32[]{:S(2)}, u32[]{:S(2)}) collective-permute-start(bf16[2,256,256]{2,1,0:T(8,128)(2,1)S(1)} %add_convert_fusion.5), channel_id=1, source_target_pairs={{0,24},{4,28},{8,0},{12,4},{16,8},{20,12},{24,16},{28,20},{1,25},{... | collective-permute-start | bytes 786440 | tf_op jit(solution)/shard_map/ppermute | solution.py:114
  159.8 1.9 collective-permute-start.49
  162.0 3.2 %collective-permute-start.47 = (bf16[2,256,256]{2,1,0:T(8,128)(2,1)S(1)}, bf16[2,256,256]{2,1,0:T(8,128)(2,1)S(1)}, u32[]{:S(2)}, u32[]{:S(2)}) collective-permute-start(bf16[2,256,256]{2,1,0:T(8,128)(2,1)S(1)} %add_convert_fusion.3), channel_id=1, source_target_pairs={{0,24},{4,28},{8,0},{12,4},{16,8},{20,12},{24,16},{28,20},{1,25},{... | collective-permute-start | bytes 786440 | tf_op jit(solution)/shard_map/ppermute | solution.py:114
  165.2 1.9 collective-permute-done.43
  167.4 5.3 %collective-permute-done.49 = bf16[2,256,256]{2,1,0:T(8,128)(2,1)S(1)} collective-permute-done((bf16[2,256,256]{2,1,0:T(8,128)(2,1)S(1)}, bf16[2,256,256]{2,1,0:T(8,128)(2,1)S(1)}, u32[]{:S(2)}, u32[]{:S(2)}) %collective-permute-start.49) | collective-permute-done | bytes 262176 | tf_op jit(solution)/shard_map/ppermute | solution.py:114
  172.9 3.5 %collective-permute-start.51 = (bf16[2,256,256]{2,1,0:T(8,128)(2,1)S(1)}, bf16[2,256,256]{2,1,0:T(8,128)(2,1)S(1)}, u32[]{:S(2)}, u32[]{:S(2)}) collective-permute-start(bf16[2,256,256]{2,1,0:T(8,128)(2,1)S(1)} %add_convert_fusion.2), channel_id=1, source_target_pairs={{0,24},{4,28},{8,0},{12,4},{16,8},{20,12},{24,16},{28,20},{1,25},{... | collective-permute-start | bytes 786440 | tf_op jit(solution)/shard_map/ppermute | solution.py:114
  176.4 1.5 collective-permute-done.47
  178.1 3.9 %collective-permute-start.50 = (bf16[2,256,256]{2,1,0:T(8,128)(2,1)S(1)}, bf16[2,256,256]{2,1,0:T(8,128)(2,1)S(1)}, u32[]{:S(2)}, u32[]{:S(2)}) collective-permute-start(bf16[2,256,256]{2,1,0:T(8,128)(2,1)S(1)} %add_convert_fusion.1), channel_id=1, source_target_pairs={{0,24},{4,28},{8,0},{12,4},{16,8},{20,12},{24,16},{28,20},{1,25},{... | collective-permute-start | bytes 786440 | tf_op jit(solution)/shard_map/ppermute | solution.py:114
  182.7 2.1 %collective-permute-start.52 = (bf16[2,256,256]{2,1,0:T(8,128)(2,1)S(1)}, bf16[2,256,256]{2,1,0:T(8,128)(2,1)S(1)}, u32[]{:S(2)}, u32[]{:S(2)}) collective-permute-start(bf16[2,256,256]{2,1,0:T(8,128)(2,1)S(1)} %add_convert_fusion), channel_id=1, source_target_pairs={{0,24},{4,28},{8,0},{12,4},{16,8},{20,12},{24,16},{28,20},{1,25},{... | collective-permute-start | bytes 786440 | tf_op jit(solution)/shard_map/ppermute | solution.py:114
  184.9 3.8 %collective-permute-done.50 = bf16[2,256,256]{2,1,0:T(8,128)(2,1)S(1)} collective-permute-done((bf16[2,256,256]{2,1,0:T(8,128)(2,1)S(1)}, bf16[2,256,256]{2,1,0:T(8,128)(2,1)S(1)}, u32[]{:S(2)}, u32[]{:S(2)}) %collective-permute-start.50) | collective-permute-done | bytes 262176 | tf_op jit(solution)/shard_map/ppermute | solution.py:114
  188.9 2.6 %collective-permute-done.52 = bf16[2,256,256]{2,1,0:T(8,128)(2,1)S(1)} collective-permute-done((bf16[2,256,256]{2,1,0:T(8,128)(2,1)S(1)}, bf16[2,256,256]{2,1,0:T(8,128)(2,1)S(1)}, u32[]{:S(2)}, u32[]{:S(2)}) %collective-permute-start.52) | collective-permute-done | bytes 262176 | tf_op jit(solution)/shard_map/ppermute | solution.py:114
  194.0 2.7 %multiply_subtract_fusion = (f32[2,128,2048]{2,1,0:T(8,128)}, f32[2,128,2048]{2,1,0:T(8,128)}) fusion(f32[2,128,2048]{2,1,0:T(8,128)S(1)} %copy-done, f32[2,128,1024]{2,1,0:T(8,128)S(1)} %get-tuple-element.215, f32[2,128,1024]{2,1,0:T(8,128)S(1)} %get-tuple-element.214, f32[2,128,2048]{2,1,0:T(8,128)S(1)} %copy-done.1), kind=kLoop, calls=%fused_computation.1 | loop fusion | flops 3670016 | bytes 10485760 | tf_op jit(solution)/shard_map/sub | solution.py:302
  (223 shorter events, 55.0 us)
Async XLA Ops:
  2.3 9.2 %collective-permute-start = (bf16[2,128,1024]{2,1,0:T(8,128)(2,1)S(1)}, bf16[2,128,1024]{2,1,0:T(8,128)(2,1)S(1)}, u32[]{:S(2)}, u32[]{:S(2)}) collective-permute-start(bf16[2,128,1024]{2,1,0:T(8,128)(2,1)S(1)} %get-tuple-element.107), channel_id=1, source_target_pairs={{0,1},{1,0},{2,3},{3,2},{4,5},{5,4},{6,7},{7,6},{8,9},{9,8},{10,11... | collective-permute-start | bytes 1572872 | tf_op jit(solution)/shard_map/ppermute | solution.py:114
  8.4 18.8 %collective-permute-start.1 = (bf16[384,2048]{1,0:T(8,128)(2,1)}, bf16[384,2048]{1,0:T(8,128)(2,1)}, u32[]{:S(2)}, u32[]{:S(2)}) collective-permute-start(bf16[384,2048]{1,0:T(8,128)(2,1)} %get-tuple-element.123), channel_id=1, source_target_pairs={{0,1},{1,0},{2,3},{3,2},{4,5},{5,4},{6,7},{7,6},{8,9},{9,8},{10,11... | collective-permute-start | bytes 4718600 | tf_op jit(solution)/shard_map/ppermute | solution.py:114
  8.5 38.5 %collective-permute-start.4 = (bf16[384,2048]{1,0:T(8,128)(2,1)}, bf16[384,2048]{1,0:T(8,128)(2,1)S(1)}, u32[]{:S(2)}, u32[]{:S(2)}) collective-permute-start(bf16[384,2048]{1,0:T(8,128)(2,1)} %get-tuple-element.114), channel_id=1, source_target_pairs={{0,2},{1,3},{2,0},{3,1},{4,6},{5,7},{6,4},{7,5},{8,10},{9,11},{10,... | collective-permute-start | bytes 4718600 | tf_op jit(solution)/shard_map/ppermute | solution.py:114
  11.6 11.1 %collective-permute-start.3 = (bf16[2,256,256]{2,1,0:T(8,128)(2,1)S(1)}, bf16[2,256,256]{2,1,0:T(8,128)(2,1)}, u32[]{:S(2)}, u32[]{:S(2)}) collective-permute-start(bf16[2,256,256]{2,1,0:T(8,128)(2,1)S(1)} %get-tuple-element.128), channel_id=1, source_target_pairs={{0,8},{4,12},{8,16},{12,20},{16,24},{20,28},{24,0},{28,4},{1,9},{5... | collective-permute-start | bytes 786440 | tf_op jit(solution)/shard_map/ppermute | solution.py:114
  13.3 14.0 %collective-permute-start.2 = (bf16[2,256,256]{2,1,0:T(8,128)(2,1)S(1)}, bf16[2,256,256]{2,1,0:T(8,128)(2,1)}, u32[]{:S(2)}, u32[]{:S(2)}) collective-permute-start(bf16[2,256,256]{2,1,0:T(8,128)(2,1)S(1)} %get-tuple-element.133), channel_id=1, source_target_pairs={{0,8},{4,12},{8,16},{12,20},{16,24},{20,28},{24,0},{28,4},{1,9},{5... | collective-permute-start | bytes 786440 | tf_op jit(solution)/shard_map/ppermute | solution.py:114
  25.0 11.1 %collective-permute-start.8 = (bf16[2,256,256]{2,1,0:T(8,128)(2,1)}, bf16[2,256,256]{2,1,0:T(8,128)(2,1)S(1)}, u32[]{:S(2)}, u32[]{:S(2)}) collective-permute-start(bf16[2,256,256]{2,1,0:T(8,128)(2,1)} %collective-permute-done.3), channel_id=1, source_target_pairs={{0,8},{4,12},{8,16},{12,20},{16,24},{20,28},{24,0},{28,4},{1,9},{5... | collective-permute-start | bytes 786440 | tf_op jit(solution)/shard_map/ppermute | solution.py:114
  27.3 14.5 %collective-permute-start.7 = (bf16[2,256,256]{2,1,0:T(8,128)(2,1)}, bf16[2,256,256]{2,1,0:T(8,128)(2,1)S(1)}, u32[]{:S(2)}, u32[]{:S(2)}) collective-permute-start(bf16[2,256,256]{2,1,0:T(8,128)(2,1)} %collective-permute-done.2), channel_id=1, source_target_pairs={{0,8},{4,12},{8,16},{12,20},{16,24},{20,28},{24,0},{28,4},{1,9},{5... | collective-permute-start | bytes 786440 | tf_op jit(solution)/shard_map/ppermute | solution.py:114
  31.9 15.1 %collective-permute-start.6 = (bf16[2,256,256]{2,1,0:T(8,128)(2,1)S(1)}, bf16[2,256,256]{2,1,0:T(8,128)(2,1)S(1)}, u32[]{:S(2)}, u32[]{:S(2)}) collective-permute-start(bf16[2,256,256]{2,1,0:T(8,128)(2,1)S(1)} %get-tuple-element.146), channel_id=1, source_target_pairs={{0,8},{4,12},{8,16},{12,20},{16,24},{20,28},{24,0},{28,4},{1,9},{5... | collective-permute-start | bytes 786440 | tf_op jit(solution)/shard_map/ppermute | solution.py:114
  47.0 28.4 %collective-permute-start.9 = (bf16[384,2048]{1,0:T(8,128)(2,1)S(1)}, bf16[384,2048]{1,0:T(8,128)(2,1)S(1)}, u32[]{:S(2)}, u32[]{:S(2)}) collective-permute-start(bf16[384,2048]{1,0:T(8,128)(2,1)S(1)} %collective-permute-done.4), channel_id=1, source_target_pairs={{0,1},{1,0},{2,3},{3,2},{4,5},{5,4},{6,7},{7,6},{8,9},{9,8},{10,11... | collective-permute-start | bytes 4718600 | tf_op jit(solution)/shard_map/ppermute | solution.py:114
  47.9 10.9 %collective-permute-start.10 = (bf16[2,256,256]{2,1,0:T(8,128)(2,1)S(1)}, bf16[2,256,256]{2,1,0:T(8,128)(2,1)S(1)}, u32[]{:S(2)}, u32[]{:S(2)}) collective-permute-start(bf16[2,256,256]{2,1,0:T(8,128)(2,1)S(1)} %collective-permute-done.8), channel_id=1, source_target_pairs={{0,8},{4,12},{8,16},{12,20},{16,24},{20,28},{24,0},{28,4},{1,9},{5... | collective-permute-start | bytes 786440 | tf_op jit(solution)/shard_map/ppermute | solution.py:114
  50.0 16.0 %collective-permute-start.11 = (bf16[768,256]{1,0:T(8,128)(2,1)S(1)}, bf16[768,256]{1,0:T(8,128)(2,1)S(1)}, u32[]{:S(2)}, u32[]{:S(2)}) collective-permute-start(bf16[768,256]{1,0:T(8,128)(2,1)S(1)} %pad_maximum_fusion.19), channel_id=1, source_target_pairs={{0,4},{4,0},{8,12},{12,8},{16,20},{20,16},{24,28},{28,24},{1,5},{5... | collective-permute-start | bytes 1179656 | tf_op jit(solution)/shard_map/ppermute | solution.py:114
  51.6 12.9 %collective-permute-start.15 = (bf16[2,256,256]{2,1,0:T(8,128)(2,1)S(1)}, bf16[2,256,256]{2,1,0:T(8,128)(2,1)S(1)}, u32[]{:S(2)}, u32[]{:S(2)}) collective-permute-start(bf16[2,256,256]{2,1,0:T(8,128)(2,1)S(1)} %collective-permute-done.7), channel_id=1, source_target_pairs={{0,8},{4,12},{8,16},{12,20},{16,24},{20,28},{24,0},{28,4},{1,9},{5... | collective-permute-start | bytes 786440 | tf_op jit(solution)/shard_map/ppermute | solution.py:114
  53.2 19.4 %collective-permute-start.16 = (bf16[768,256]{1,0:T(8,128)(2,1)S(1)}, bf16[768,256]{1,0:T(8,128)(2,1)S(1)}, u32[]{:S(2)}, u32[]{:S(2)}) collective-permute-start(bf16[768,256]{1,0:T(8,128)(2,1)S(1)} %pad_maximum_fusion.20), channel_id=1, source_target_pairs={{0,4},{4,0},{8,12},{12,8},{16,20},{20,16},{24,28},{28,24},{1,5},{5... | collective-permute-start | bytes 1179656 | tf_op jit(solution)/shard_map/ppermute | solution.py:114
  58.9 16.5 %collective-permute-start.14 = (bf16[2,256,256]{2,1,0:T(8,128)(2,1)S(1)}, bf16[2,256,256]{2,1,0:T(8,128)(2,1)S(1)}, u32[]{:S(2)}, u32[]{:S(2)}) collective-permute-start(bf16[2,256,256]{2,1,0:T(8,128)(2,1)S(1)} %get-tuple-element.154), channel_id=1, source_target_pairs={{0,8},{4,12},{8,16},{12,20},{16,24},{20,28},{24,0},{28,4},{1,9},{5... | collective-permute-start | bytes 786440 | tf_op jit(solution)/shard_map/ppermute | solution.py:114
  66.0 9.3 %collective-permute-start.18 = (bf16[2,256,256]{2,1,0:T(8,128)(2,1)S(1)}, bf16[2,256,256]{2,1,0:T(8,128)(2,1)S(1)}, u32[]{:S(2)}, u32[]{:S(2)}) collective-permute-start(bf16[2,256,256]{2,1,0:T(8,128)(2,1)S(1)} %collective-permute-done.6), channel_id=1, source_target_pairs={{0,8},{4,12},{8,16},{12,20},{16,24},{20,28},{24,0},{28,4},{1,9},{5... | collective-permute-start | bytes 786440 | tf_op jit(solution)/shard_map/ppermute | solution.py:114
  76.7 14.1 %collective-permute-start.13 = (bf16[768,256]{1,0:T(8,128)(2,1)S(1)}, bf16[768,256]{1,0:T(8,128)(2,1)S(1)}, u32[]{:S(2)}, u32[]{:S(2)}) collective-permute-start(bf16[768,256]{1,0:T(8,128)(2,1)S(1)} %convolution_convert_fusion.3), channel_id=1, source_target_pairs={{0,2},{1,3},{2,0},{3,1},{4,6},{5,7},{6,4},{7,5},{8,10},{9,11},{10,... | collective-permute-start | bytes 1179656 | tf_op jit(solution)/shard_map/ppermute | solution.py:114
  80.4 17.2 %collective-permute-start.21 = (bf16[768,256]{1,0:T(8,128)(2,1)S(1)}, bf16[768,256]{1,0:T(8,128)(2,1)S(1)}, u32[]{:S(2)}, u32[]{:S(2)}) collective-permute-start(bf16[768,256]{1,0:T(8,128)(2,1)S(1)} %pad_maximum_fusion.21), channel_id=1, source_target_pairs={{0,4},{4,0},{8,12},{12,8},{16,20},{20,16},{24,28},{28,24},{1,5},{5... | collective-permute-start | bytes 1179656 | tf_op jit(solution)/shard_map/ppermute | solution.py:114
  81.0 9.8 %collective-permute-start.20 = (bf16[2,256,256]{2,1,0:T(8,128)(2,1)S(1)}, bf16[2,256,256]{2,1,0:T(8,128)(2,1)S(1)}, u32[]{:S(2)}, u32[]{:S(2)}) collective-permute-start(bf16[2,256,256]{2,1,0:T(8,128)(2,1)S(1)} %collective-permute-done.18), channel_id=1, source_target_pairs={{0,8},{4,12},{8,16},{12,20},{16,24},{20,28},{24,0},{28,4},{1,9},{5... | collective-permute-start | bytes 786440 | tf_op jit(solution)/shard_map/ppermute | solution.py:114
  86.1 12.1 %collective-permute-start.24 = (bf16[768,256]{1,0:T(8,128)(2,1)S(1)}, bf16[768,256]{1,0:T(8,128)(2,1)S(1)}, u32[]{:S(2)}, u32[]{:S(2)}) collective-permute-start(bf16[768,256]{1,0:T(8,128)(2,1)S(1)} %convolution_convert_fusion.2), channel_id=1, source_target_pairs={{0,2},{1,3},{2,0},{3,1},{4,6},{5,7},{6,4},{7,5},{8,10},{9,11},{10,... | collective-permute-start | bytes 1179656 | tf_op jit(solution)/shard_map/ppermute | solution.py:114
  92.1 15.8 %collective-permute-start.19 = (bf16[768,256]{1,0:T(8,128)(2,1)S(1)}, bf16[768,256]{1,0:T(8,128)(2,1)S(1)}, u32[]{:S(2)}, u32[]{:S(2)}) collective-permute-start(bf16[768,256]{1,0:T(8,128)(2,1)S(1)} %multiply_convert_fusion.3), channel_id=1, source_target_pairs={{0,2},{1,3},{2,0},{3,1},{4,6},{5,7},{6,4},{7,5},{8,10},{9,11},{10,... | collective-permute-start | bytes 1179656 | tf_op jit(solution)/shard_map/ppermute | solution.py:114
  95.3 16.9 %collective-permute-start.31 = (bf16[768,256]{1,0:T(8,128)(2,1)S(1)}, bf16[768,256]{1,0:T(8,128)(2,1)S(1)}, u32[]{:S(2)}, u32[]{:S(2)}) collective-permute-start(bf16[768,256]{1,0:T(8,128)(2,1)S(1)} %pad_maximum_fusion.22), channel_id=1, source_target_pairs={{0,4},{4,0},{8,12},{12,8},{16,20},{20,16},{24,28},{28,24},{1,5},{5... | collective-permute-start | bytes 1179656 | tf_op jit(solution)/shard_map/ppermute | solution.py:114
  97.0 8.9 %collective-permute-start.23 = (bf16[256,256]{1,0:T(8,128)(2,1)S(1)}, bf16[256,256]{1,0:T(8,128)(2,1)S(1)}, u32[]{:S(2)}, u32[]{:S(2)}) collective-permute-start(bf16[256,256]{1,0:T(8,128)(2,1)S(1)} %dynamic-slice_bitcast_fusion.1), channel_id=1, source_target_pairs={{0,4},{4,0},{8,12},{12,8},{16,20},{20,16},{24,28},{28,24},{1,5},{5... | collective-permute-start | bytes 393224 | tf_op jit(solution)/shard_map/ppermute | solution.py:114
  99.4 15.6 %collective-permute-start.28 = (bf16[768,256]{1,0:T(8,128)(2,1)S(1)}, bf16[768,256]{1,0:T(8,128)(2,1)S(1)}, u32[]{:S(2)}, u32[]{:S(2)}) collective-permute-start(bf16[768,256]{1,0:T(8,128)(2,1)S(1)} %multiply_convert_fusion.2), channel_id=1, source_target_pairs={{0,2},{1,3},{2,0},{3,1},{4,6},{5,7},{6,4},{7,5},{8,10},{9,11},{10,... | collective-permute-start | bytes 1179656 | tf_op jit(solution)/shard_map/ppermute | solution.py:114
  100.4 11.4 %collective-permute-start.25 = (bf16[2,256,256]{2,1,0:T(8,128)(2,1)S(1)}, bf16[2,256,256]{2,1,0:T(8,128)(2,1)S(1)}, u32[]{:S(2)}, u32[]{:S(2)}) collective-permute-start(bf16[2,256,256]{2,1,0:T(8,128)(2,1)S(1)} %collective-permute-done.22), channel_id=1, source_target_pairs={{0,8},{4,12},{8,16},{12,20},{16,24},{20,28},{24,0},{28,4},{1,9},{5... | collective-permute-start | bytes 786440 | tf_op jit(solution)/shard_map/ppermute | solution.py:114
  106.9 15.6 %collective-permute-start.30 = (bf16[768,256]{1,0:T(8,128)(2,1)S(1)}, bf16[768,256]{1,0:T(8,128)(2,1)S(1)}, u32[]{:S(2)}, u32[]{:S(2)}) collective-permute-start(bf16[768,256]{1,0:T(8,128)(2,1)S(1)} %convolution_convert_fusion.1), channel_id=1, source_target_pairs={{0,2},{1,3},{2,0},{3,1},{4,6},{5,7},{6,4},{7,5},{8,10},{9,11},{10,... | collective-permute-start | bytes 1179656 | tf_op jit(solution)/shard_map/ppermute | solution.py:114
  110.0 8.9 %collective-permute-start.27 = (bf16[256,256]{1,0:T(8,128)(2,1)S(1)}, bf16[256,256]{1,0:T(8,128)(2,1)S(1)}, u32[]{:S(2)}, u32[]{:S(2)}) collective-permute-start(bf16[256,256]{1,0:T(8,128)(2,1)S(1)} %slice.260), channel_id=1, source_target_pairs={{0,4},{4,0},{8,12},{12,8},{16,20},{20,16},{24,28},{28,24},{1,5},{5... | collective-permute-start | bytes 393224 | tf_op jit(solution)/shard_map/ppermute | solution.py:114
  112.3 15.5 %collective-permute-start.26 = (bf16[768,256]{1,0:T(8,128)(2,1)S(1)}, bf16[768,256]{1,0:T(8,128)(2,1)S(1)}, u32[]{:S(2)}, u32[]{:S(2)}) collective-permute-start(bf16[768,256]{1,0:T(8,128)(2,1)S(1)} %slice.259), channel_id=1, source_target_pairs={{0,4},{4,0},{8,12},{12,8},{16,20},{20,16},{24,28},{28,24},{1,5},{5... | collective-permute-start | bytes 1179656 | tf_op jit(solution)/shard_map/ppermute | solution.py:114
  116.2 15.3 %collective-permute-start.35 = (bf16[256,256]{1,0:T(8,128)(2,1)S(1)}, bf16[256,256]{1,0:T(8,128)(2,1)S(1)}, u32[]{:S(2)}, u32[]{:S(2)}) collective-permute-start(bf16[256,256]{1,0:T(8,128)(2,1)S(1)} %slice.268), channel_id=1, source_target_pairs={{0,4},{4,0},{8,12},{12,8},{16,20},{20,16},{24,28},{28,24},{1,5},{5... | collective-permute-start | bytes 393224 | tf_op jit(solution)/shard_map/ppermute | solution.py:114
  118.9 17.6 %collective-permute-start.39 = (bf16[768,256]{1,0:T(8,128)(2,1)S(1)}, bf16[768,256]{1,0:T(8,128)(2,1)S(1)}, u32[]{:S(2)}, u32[]{:S(2)}) collective-permute-start(bf16[768,256]{1,0:T(8,128)(2,1)S(1)} %slice.267), channel_id=1, source_target_pairs={{0,4},{4,0},{8,12},{12,8},{16,20},{20,16},{24,28},{28,24},{1,5},{5... | collective-permute-start | bytes 1179656 | tf_op jit(solution)/shard_map/ppermute | solution.py:114
  119.6 9.4 %collective-permute-start.29 = (bf16[2,256,256]{2,1,0:T(8,128)(2,1)S(1)}, bf16[2,256,256]{2,1,0:T(8,128)(2,1)S(1)}, u32[]{:S(2)}, u32[]{:S(2)}) collective-permute-start(bf16[2,256,256]{2,1,0:T(8,128)(2,1)S(1)} %add_convert_fusion.11), channel_id=1, source_target_pairs={{0,24},{4,28},{8,0},{12,4},{16,8},{20,12},{24,16},{28,20},{1,25},{... | collective-permute-start | bytes 786440 | tf_op jit(solution)/shard_map/ppermute | solution.py:114
  122.6 12.1 %collective-permute-start.34 = (bf16[768,256]{1,0:T(8,128)(2,1)S(1)}, bf16[768,256]{1,0:T(8,128)(2,1)S(1)}, u32[]{:S(2)}, u32[]{:S(2)}) collective-permute-start(bf16[768,256]{1,0:T(8,128)(2,1)S(1)} %convolution_convert_fusion), channel_id=1, source_target_pairs={{0,2},{1,3},{2,0},{3,1},{4,6},{5,7},{6,4},{7,5},{8,10},{9,11},{10,... | collective-permute-start | bytes 1179656 | tf_op jit(solution)/shard_map/ppermute | solution.py:114
  127.8 14.9 %collective-permute-start.37 = (bf16[768,256]{1,0:T(8,128)(2,1)S(1)}, bf16[768,256]{1,0:T(8,128)(2,1)S(1)}, u32[]{:S(2)}, u32[]{:S(2)}) collective-permute-start(bf16[768,256]{1,0:T(8,128)(2,1)S(1)} %multiply_convert_fusion.1), channel_id=1, source_target_pairs={{0,2},{1,3},{2,0},{3,1},{4,6},{5,7},{6,4},{7,5},{8,10},{9,11},{10,... | collective-permute-start | bytes 1179656 | tf_op jit(solution)/shard_map/ppermute | solution.py:114
  129.2 8.7 %collective-permute-start.33 = (bf16[2,256,256]{2,1,0:T(8,128)(2,1)S(1)}, bf16[2,256,256]{2,1,0:T(8,128)(2,1)S(1)}, u32[]{:S(2)}, u32[]{:S(2)}) collective-permute-start(bf16[2,256,256]{2,1,0:T(8,128)(2,1)S(1)} %add_convert_fusion.10), channel_id=1, source_target_pairs={{0,24},{4,28},{8,0},{12,4},{16,8},{20,12},{24,16},{28,20},{1,25},{... | collective-permute-start | bytes 786440 | tf_op jit(solution)/shard_map/ppermute | solution.py:114
  131.7 14.8 %collective-permute-start.40 = (bf16[2,256,256]{2,1,0:T(8,128)(2,1)S(1)}, bf16[2,256,256]{2,1,0:T(8,128)(2,1)S(1)}, u32[]{:S(2)}, u32[]{:S(2)}) collective-permute-start(bf16[2,256,256]{2,1,0:T(8,128)(2,1)S(1)} %add_convert_fusion.9), channel_id=1, source_target_pairs={{0,24},{4,28},{8,0},{12,4},{16,8},{20,12},{24,16},{28,20},{1,25},{... | collective-permute-start | bytes 786440 | tf_op jit(solution)/shard_map/ppermute | solution.py:114
  135.9 16.6 %collective-permute-start.42 = (bf16[768,256]{1,0:T(8,128)(2,1)S(1)}, bf16[768,256]{1,0:T(8,128)(2,1)S(1)}, u32[]{:S(2)}, u32[]{:S(2)}) collective-permute-start(bf16[768,256]{1,0:T(8,128)(2,1)S(1)} %multiply_convert_fusion), channel_id=1, source_target_pairs={{0,2},{1,3},{2,0},{3,1},{4,6},{5,7},{6,4},{7,5},{8,10},{9,11},{10,... | collective-permute-start | bytes 1179656 | tf_op jit(solution)/shard_map/ppermute | solution.py:114
  138.1 14.2 %collective-permute-start.36 = (bf16[2,256,256]{2,1,0:T(8,128)(2,1)S(1)}, bf16[2,256,256]{2,1,0:T(8,128)(2,1)S(1)}, u32[]{:S(2)}, u32[]{:S(2)}) collective-permute-start(bf16[2,256,256]{2,1,0:T(8,128)(2,1)S(1)} %add_convert_fusion.8), channel_id=1, source_target_pairs={{0,24},{4,28},{8,0},{12,4},{16,8},{20,12},{24,16},{28,20},{1,25},{... | collective-permute-start | bytes 786440 | tf_op jit(solution)/shard_map/ppermute | solution.py:114
  146.7 10.2 %collective-permute-start.41 = (bf16[2,256,256]{2,1,0:T(8,128)(2,1)S(1)}, bf16[2,256,256]{2,1,0:T(8,128)(2,1)S(1)}, u32[]{:S(2)}, u32[]{:S(2)}) collective-permute-start(bf16[2,256,256]{2,1,0:T(8,128)(2,1)S(1)} %add_convert_fusion.7), channel_id=1, source_target_pairs={{0,24},{4,28},{8,0},{12,4},{16,8},{20,12},{24,16},{28,20},{1,25},{... | collective-permute-start | bytes 786440 | tf_op jit(solution)/shard_map/ppermute | solution.py:114
  147.7 14.1 %collective-permute-start.44 = (bf16[768,256]{1,0:T(8,128)(2,1)S(1)}, bf16[768,256]{1,0:T(8,128)(2,1)S(1)}, u32[]{:S(2)}, u32[]{:S(2)}) collective-permute-start(bf16[768,256]{1,0:T(8,128)(2,1)S(1)} %slice.274), channel_id=1, source_target_pairs={{0,4},{4,0},{8,12},{12,8},{16,20},{20,16},{24,28},{28,24},{1,5},{5... | collective-permute-start | bytes 1179656 | tf_op jit(solution)/shard_map/ppermute | solution.py:114
  150.5 11.3 %collective-permute-start.45 = (bf16[2,256,256]{2,1,0:T(8,128)(2,1)S(1)}, bf16[2,256,256]{2,1,0:T(8,128)(2,1)S(1)}, u32[]{:S(2)}, u32[]{:S(2)}) collective-permute-start(bf16[2,256,256]{2,1,0:T(8,128)(2,1)S(1)} %add_convert_fusion.6), channel_id=1, source_target_pairs={{0,24},{4,28},{8,0},{12,4},{16,8},{20,12},{24,16},{28,20},{1,25},{... | collective-permute-start | bytes 786440 | tf_op jit(solution)/shard_map/ppermute | solution.py:114
  156.3 11.0 %collective-permute-start.48 = (bf16[768,256]{1,0:T(8,128)(2,1)S(1)}, bf16[768,256]{1,0:T(8,128)(2,1)S(1)}, u32[]{:S(2)}, u32[]{:S(2)}) collective-permute-start(bf16[768,256]{1,0:T(8,128)(2,1)S(1)} %slice.283), channel_id=1, source_target_pairs={{0,4},{4,0},{8,12},{12,8},{16,20},{20,16},{24,28},{28,24},{1,5},{5... | collective-permute-start | bytes 1179656 | tf_op jit(solution)/shard_map/ppermute | solution.py:114
  157.1 10.0 %collective-permute-start.43 = (bf16[2,256,256]{2,1,0:T(8,128)(2,1)S(1)}, bf16[2,256,256]{2,1,0:T(8,128)(2,1)S(1)}, u32[]{:S(2)}, u32[]{:S(2)}) collective-permute-start(bf16[2,256,256]{2,1,0:T(8,128)(2,1)S(1)} %add_convert_fusion.5), channel_id=1, source_target_pairs={{0,24},{4,28},{8,0},{12,4},{16,8},{20,12},{24,16},{28,20},{1,25},{... | collective-permute-start | bytes 786440 | tf_op jit(solution)/shard_map/ppermute | solution.py:114
  159.8 12.9 %collective-permute-start.49 = (bf16[2,256,256]{2,1,0:T(8,128)(2,1)S(1)}, bf16[2,256,256]{2,1,0:T(8,128)(2,1)S(1)}, u32[]{:S(2)}, u32[]{:S(2)}) collective-permute-start(bf16[2,256,256]{2,1,0:T(8,128)(2,1)S(1)} %add_convert_fusion.4), channel_id=1, source_target_pairs={{0,24},{4,28},{8,0},{12,4},{16,8},{20,12},{24,16},{28,20},{1,25},{... | collective-permute-start | bytes 786440 | tf_op jit(solution)/shard_map/ppermute | solution.py:114
  162.0 15.9 %collective-permute-start.47 = (bf16[2,256,256]{2,1,0:T(8,128)(2,1)S(1)}, bf16[2,256,256]{2,1,0:T(8,128)(2,1)S(1)}, u32[]{:S(2)}, u32[]{:S(2)}) collective-permute-start(bf16[2,256,256]{2,1,0:T(8,128)(2,1)S(1)} %add_convert_fusion.3), channel_id=1, source_target_pairs={{0,24},{4,28},{8,0},{12,4},{16,8},{20,12},{24,16},{28,20},{1,25},{... | collective-permute-start | bytes 786440 | tf_op jit(solution)/shard_map/ppermute | solution.py:114
  172.9 9.6 %collective-permute-start.51 = (bf16[2,256,256]{2,1,0:T(8,128)(2,1)S(1)}, bf16[2,256,256]{2,1,0:T(8,128)(2,1)S(1)}, u32[]{:S(2)}, u32[]{:S(2)}) collective-permute-start(bf16[2,256,256]{2,1,0:T(8,128)(2,1)S(1)} %add_convert_fusion.2), channel_id=1, source_target_pairs={{0,24},{4,28},{8,0},{12,4},{16,8},{20,12},{24,16},{28,20},{1,25},{... | collective-permute-start | bytes 786440 | tf_op jit(solution)/shard_map/ppermute | solution.py:114
  178.1 10.5 %collective-permute-start.50 = (bf16[2,256,256]{2,1,0:T(8,128)(2,1)S(1)}, bf16[2,256,256]{2,1,0:T(8,128)(2,1)S(1)}, u32[]{:S(2)}, u32[]{:S(2)}) collective-permute-start(bf16[2,256,256]{2,1,0:T(8,128)(2,1)S(1)} %add_convert_fusion.1), channel_id=1, source_target_pairs={{0,24},{4,28},{8,0},{12,4},{16,8},{20,12},{24,16},{28,20},{1,25},{... | collective-permute-start | bytes 786440 | tf_op jit(solution)/shard_map/ppermute | solution.py:114
  182.0 9.8 %collective-permute-start.53 = (f32[2,128,256]{2,1,0:T(8,128)S(1)}, f32[2,128,256]{2,1,0:T(8,128)S(1)}, u32[]{:S(2)}, u32[]{:S(2)}) collective-permute-start(f32[2,128,256]{2,1,0:T(8,128)S(1)} %get-tuple-element.227), channel_id=1, source_target_pairs={{0,1},{1,0},{2,3},{3,2},{4,5},{5,4},{6,7},{7,6},{8,9},{9,8},{10,11... | collective-permute-start | bytes 786440 | tf_op jit(solution)/shard_map/ppermute | solution.py:114
  182.0 9.9 %collective-permute-start.54 = (f32[2,128,256]{2,1,0:T(8,128)S(1)}, f32[2,128,256]{2,1,0:T(8,128)S(1)}, u32[]{:S(2)}, u32[]{:S(2)}) collective-permute-start(f32[2,128,256]{2,1,0:T(8,128)S(1)} %get-tuple-element.229), channel_id=1, source_target_pairs={{0,1},{1,0},{2,3},{3,2},{4,5},{5,4},{6,7},{7,6},{8,9},{9,8},{10,11... | collective-permute-start | bytes 786440 | tf_op jit(solution)/shard_map/ppermute | solution.py:114
  182.7 8.8 %collective-permute-start.52 = (bf16[2,256,256]{2,1,0:T(8,128)(2,1)S(1)}, bf16[2,256,256]{2,1,0:T(8,128)(2,1)S(1)}, u32[]{:S(2)}, u32[]{:S(2)}) collective-permute-start(bf16[2,256,256]{2,1,0:T(8,128)(2,1)S(1)} %add_convert_fusion), channel_id=1, source_target_pairs={{0,24},{4,28},{8,0},{12,4},{16,8},{20,12},{24,16},{28,20},{1,25},{... | collective-permute-start | bytes 786440 | tf_op jit(solution)/shard_map/ppermute | solution.py:114
  (18 other events, 176.3 us)
